TPU v7x, 32 devices: a whole 2x2x4 slice. The times are simulated.
32 devices in a mesh: dp: 4 (over y, x), seq: 2 (over core), head: 4 (over z).
Axes of the slice: x: 2, y: 2, z: 4, core: 2. Of those that a mesh axis runs over, the one named last changes fastest.
Arguments:
- hidden_in: bfloat16 [1, 4, 512, 1024], P(None, 'dp', 'seq', 'head'), may hold values from -6 to 6
- cotangent: bfloat16 [1, 4, 512, 1024], P(None, 'dp', 'seq', 'head'), may hold values from -6 to 6
- norm_gain: bfloat16 [1024], P(('dp', 'seq')), may hold values from 0.5 to 1.5
- w_zx: bfloat16 [1024, 2, 2048], P(('dp', 'seq'), None, 'head'), may hold values from -0.1875 to 0.1875
- w_bc: bfloat16 [1024, 256], P(('dp', 'seq')), may hold values from -0.1875 to 0.1875
- w_dt: bfloat16 [1024, 32], P(('dp', 'seq'), 'head'), may hold values from -0.1875 to 0.1875
- w_out: bfloat16 [2048, 1024], P('head', ('dp', 'seq')), may hold values from -0.125 to 0.125
- conv_x: float32 [5, 2048], P(None, 'head'), may hold values from -0.5 to 0.5
- conv_bc: float32 [5, 256], replicated, may hold values from -0.5 to 0.5
- head_params: float32 [3, 32], P(None, 'head'), may hold values from -11 to 2.5
- gate_gain: float32 [2048], P('head'), may hold values from 0.5 to 1.5
Outputs:
- output: bfloat16 [1, 4, 512, 1024], P(None, 'dp', 'seq', 'head')
- grad_input: bfloat16 [1, 4, 512, 1024], P(None, 'dp', 'seq', 'head')
- grad_norm_gain: float32 [1024], P(('dp', 'seq'))
- grad_w_zx: float32 [1024, 2, 2048], P(('dp', 'seq'), None, 'head')
- grad_w_bc: float32 [1024, 256], P(('dp', 'seq'))
- grad_w_dt: float32 [1024, 32], P(('dp', 'seq'), 'head')
- grad_w_out: float32 [2048, 1024], P('head', ('dp', 'seq'))
- grad_conv_x: float32 [5, 2048], P(None, 'head')
- grad_conv_bc: float32 [5, 256], replicated
- grad_head_params: float32 [3, 32], P(None, 'head')
- grad_gate_gain: float32 [2048], P('head')
All inputs are finite; a program needn't handle non-finite values.
Results may differ from a plain program's by a relative error of at most 0.0092.
Values may be sent and summed in bfloat16 or wider, within the bound.
No kernel may reach another device: no remote copies, remote signals or barrier semaphores. Data moves between devices by JAX's collectives and lax.ppermute only.
A program may use at most 64 MiB of HBM per device.

v0:
```python
import functools

import jax
import jax.numpy as jnp
from jax import lax
from jax.experimental import pallas as pl
from jax.experimental.pallas import tpu as pltpu
from jax.sharding import PartitionSpec as P


epsilon = 1e-05
f32 = jnp.float32
bf16 = jnp.bfloat16
exact = lax.Precision.HIGHEST
LANES = 128
HALO = 16
EDGE = 8


def xor_route(count, k):
    return [(i, i ^ k) for i in range(count)]


def sent(block, axis, k):
    return lax.ppermute(block, axis, xor_route(lax.axis_size(axis), k))


def exchanged(block, axis):
    count = lax.axis_size(axis)
    return [block] + [sent(block, axis, k) for k in range(1, count)]


def scattered(blocks, axis):
    count = lax.axis_size(axis)
    return [blocks[0]] + [sent(blocks[k], axis, k) for k in range(1, count)]


def tree_sum(parts):
    while len(parts) > 1:
        parts = [a + b for a, b in zip(parts[0::2], parts[1::2])]
    return parts[0]


def f32_sum(parts):
    return tree_sum([part.astype(f32) for part in parts])


def passed_along(block, axis, distance):
    devices = range(lax.axis_size(axis))
    route = [(i - distance, i) for i in devices if i - distance in devices]
    return lax.ppermute(block, axis, route)


def entering(decay, state, axis, reverse):
    count, place = lax.axis_size(axis), lax.axis_index(axis)
    if count == 2:
        return passed_along(state, axis, -1 if reverse else 1)
    decays, states = lax.all_gather(decay, axis), lax.all_gather(state, axis)

    def turn(k, before):
        at = count - 1 - k if reverse else k
        reached = at > place if reverse else at < place
        return jnp.where(reached, decays[at] * before + states[at], before)

    return lax.fori_loop(0, count, turn, jnp.zeros_like(state))


def dot(a, b, left, right):
    return lax.dot_general(
        a.astype(bf16), b.astype(bf16), (((left,), (right,)), ((), ())), preferred_element_type=f32
    )


def nn(a, b):
    return dot(a, b, 1, 0)


def nt(a, b):
    return dot(a, b, 1, 1)


def tn(a, b):
    return dot(a, b, 0, 0)


def sigmoid(v):
    return 1.0 / (1.0 + jnp.exp(-v))


def softplus(v):
    e = jnp.exp(-jnp.abs(v))
    small = e * (1.0 - e * (0.5 - e * (1.0 / 3.0 - e * 0.25)))
    return jnp.maximum(v, 0.0) + jnp.where(e < 0.03, small, jnp.log(1.0 + e))


def iota(shape, axis):
    return lax.broadcasted_iota(jnp.int32, shape, axis)


def row_of(column):
    return jnp.broadcast_to(column, (column.shape[0], LANES)).T[0:1]


def column_of(row):
    return jnp.broadcast_to(row, (LANES, row.shape[1])).T


def per_head(values, pair_at, width):
    first = values[:, 2 * pair_at : 2 * pair_at + 1]
    second = values[:, 2 * pair_at + 1 : 2 * pair_at + 2]
    lane = iota((values.shape[0], 2 * width), 1)
    return jnp.where(lane < width, first, second)


def spread(values, heads, width):
    return jnp.concatenate([per_head(values, q, width) for q in range(heads // 2)], axis=1)


def gathered_heads(values, heads, width):
    lane = iota((values.shape[0], LANES), 1)
    wide = iota((values.shape[0], 2 * width), 1)
    total = jnp.zeros((values.shape[0], LANES), f32)
    for q in range(heads // 2):
        both = values[:, 2 * width * q : 2 * width * (q + 1)]
        first = jnp.sum(jnp.where(wide < width, both, 0.0), axis=1, keepdims=True)
        second = jnp.sum(jnp.where(wide < width, 0.0, both), axis=1, keepdims=True)
        total = jnp.where(lane == 2 * q, first, total)
        total = jnp.where(lane == 2 * q + 1, second, total)
    return total


def unit(pair, p, where):
    if pair:
        t, k = divmod(p, 4)
        return k ^ where[0], pl.multiple_of((t ^ where[1]) * LANES, LANES)
    j, u = divmod(p, 2)
    return j ^ where[0], u * LANES


def assembled(scratch, pieces, axis):
    at = 0
    for piece in pieces:
        size = piece.shape[axis]
        if axis == 0:
            scratch[at : at + size, :] = piece[...]
        else:
            scratch[:, at : at + size] = piece[...]
        at += size


def norm_kernel(pair, gain_lane, n_blocks, n_pieces, where, *refs):
    blocks, pieces = refs[:n_blocks], refs[n_blocks : n_blocks + n_pieces]
    normed, x_perm, inv_ref, gain_ref, edge_ref, hold = refs[n_blocks + n_pieces :]
    rows, part = blocks[0].shape
    swap = n_blocks * part // LANES // 2 if pair else 0
    total = jnp.zeros((rows, 1), f32)
    for k, block in enumerate(blocks):
        value = block[...].astype(f32)
        hold[k] = value
        total += jnp.sum(value * value, axis=1, keepdims=True)
    inv = lax.rsqrt(total / (n_blocks * part) + epsilon)
    inv_ref[...] = jnp.broadcast_to(inv, inv_ref.shape)
    eye = iota((LANES, LANES), 0) == iota((LANES, LANES), 1)
    per_piece = pieces[0].shape[0] // LANES
    for p in range(n_blocks * part // LANES):
        piece = pieces[p // per_piece]
        at = p % per_piece * LANES
        tile = piece.shape[1] - LANES
        gain = piece[at : at + LANES, tile : tile + LANES][:, gain_lane : gain_lane + 1]
        gain = jnp.sum(jnp.where(eye, gain.astype(f32), 0.0), axis=0, keepdims=True)
        block, lane = unit(pair, p, where)
        value = hold[block, :, pl.ds(lane, LANES)]
        cut = slice(p * LANES, (p + 1) * LANES)
        value16 = (value * inv * gain).astype(bf16)
        normed[:, cut] = value16
        there = p ^ swap
        edge_ref[:, there * LANES : (there + 1) * LANES] = value16[rows - HALO :, :]
        x_perm[:, cut] = value.astype(bf16)
        gain_ref[:, cut] = gain


def forward_kernel(heads, n_pieces, *refs):
    normed, edge, conv_x, conv_bc, params = refs[:5]
    pieces = refs[5 : 5 + n_pieces]
    (z_ref, xe_ref, be_ref, ux_ref, ubc_ref, dt_ref, cum_ref, y_ref, state_ref, w_in) = refs[
        5 + n_pieces : 15 + n_pieces
    ]
    rows_in, xe, be = refs[15 + n_pieces :]
    rows, inner = ux_ref.shape
    width = inner // heads
    state_n = ubc_ref.shape[1] // 2
    taps = conv_x.shape[0] - 1
    assembled(w_in, pieces, 0)
    rows_in[0:HALO, :] = edge[...]
    rows_in[HALO : HALO + rows, :] = normed[...]
    z_ref[...] = nn(normed[...], w_in[:, 0:inner]).astype(bf16)
    x_raw = nn(rows_in[...], w_in[:, inner : 2 * inner]).astype(bf16)
    xe_ref[...] = x_raw
    xe[...] = x_raw.astype(f32)
    bcd = nn(rows_in[...], w_in[:, 2 * inner :])
    bc_raw = bcd[:, 0 : 2 * state_n].astype(bf16)
    be_ref[...] = bc_raw
    be[...] = bc_raw.astype(f32)
    dt = bcd[HALO:, 2 * state_n :]
    dt_ref[...] = dt

    def conv(extended, weights):
        total = weights[taps : taps + 1, :]
        for k in range(taps):
            total = total + weights[k : k + 1, :] * extended[
                HALO - taps + 1 + k : HALO - taps + 1 + k + rows, :
            ]
        return total

    u_x = conv(xe, conv_x)
    ux_ref[...] = u_x
    u_bc = conv(be, conv_bc)
    ubc_ref[...] = u_bc
    x_act = u_x * sigmoid(u_x)
    bc_act = u_bc * sigmoid(u_bc)
    b_mat = bc_act[:, 0:state_n].astype(bf16)
    c_mat = bc_act[:, state_n:].astype(bf16)
    lane = iota((rows, LANES), 1)
    step = jnp.where(lane < heads, softplus(dt + params[0:1, :]), 0.0)
    lower = iota((rows, rows), 0) >= iota((rows, rows), 1)
    cum = lax.dot_general(
        lower.astype(f32),
        -step * jnp.exp(params[1:2, :]),
        (((1,), (0,)), ((), ())),
        precision=exact,
        preferred_element_type=f32,
    )
    cum_ref[...] = cum
    cum_t = cum.T
    gram = nt(c_mat, b_mat)
    scaled = x_act * spread(step, heads, width)
    scaled16 = scaled.astype(bf16)
    pair_lane = iota((rows, 2 * width), 1)
    for q in range(heads // 2):
        cut = slice(2 * width * q, 2 * width * (q + 1))
        both = []
        for h in (2 * q, 2 * q + 1):
            decay = jnp.exp(jnp.where(lower, cum[:, h : h + 1] - cum_t[h : h + 1, :], -jnp.inf))
            both.append(nn(decay * gram, scaled16[:, cut]))
        y_ref[:, cut] = (
            jnp.where(pair_lane < width, both[0], both[1])
            + x_act[:, cut] * per_head(jnp.broadcast_to(params[2:3, :], (rows, LANES)), q, width)
        )
    to_end = jnp.exp(cum[rows - 1 : rows, :] - cum)
    state_ref[...] = tn(scaled * spread(to_end, heads, width), b_mat)


def gate_kernel(pair, heads, n_blocks, n_pieces, where, *refs):
    state, ubc, cum, y_loc, z, gain = refs[:6]
    blocks = refs[6 : 6 + n_blocks]
    pieces = refs[6 + n_blocks : 6 + n_blocks + n_pieces]
    y_ref, go_ref, raw_ref, stats_ref, cot_ref, w_ref, hold = refs[6 + n_blocks + n_pieces :]
    rows, inner = y_ref.shape
    width = inner // heads
    state_n = ubc.shape[1] // 2
    assembled(w_ref, pieces, 1)
    for k, block in enumerate(blocks):
        hold[k] = block[...].astype(f32)
    for p in range(cot_ref.shape[1] // LANES):
        block, lane = unit(pair, p, where)
        cot_ref[:, p * LANES : (p + 1) * LANES] = hold[block, :, pl.ds(lane, LANES)].astype(bf16)
    u_c = ubc[:, state_n:]
    c_mat = u_c * sigmoid(u_c)
    y = y_loc[...] + nt(c_mat, state[...]) * spread(jnp.exp(cum[...]), heads, width)
    y_ref[...] = y
    z_val = z[...].astype(f32)
    gated = y * z_val * sigmoid(z_val)
    raw_ref[...] = (gated * gain[...]).astype(bf16)
    grad_o = nt(cot_ref[...], w_ref[...])
    go_ref[...] = grad_o
    squares = jnp.sum(gated * gated, axis=1, keepdims=True)
    cross = jnp.sum(grad_o * gain[...] * gated, axis=1, keepdims=True)
    lane = iota((rows, LANES), 1)
    both = jnp.where(lane == 0, squares, jnp.where(lane == 1, cross, 0.0))
    stats_ref[...] = both.T[0:8, :]


def out_kernel(pair, where, raw, weights, *refs):
    hold = refs[-1]
    part = nn(raw[...], weights[...]).astype(bf16)
    for p in range(weights.shape[1] // LANES):
        block, lane = unit(pair, p, where)
        hold[block, :, pl.ds(lane, LANES)] = part[:, p * LANES : (p + 1) * LANES]
    for k, ref in enumerate(refs[:-1]):
        ref[...] = hold[k]


def gate_back_kernel(heads, full_inner, n_stats, *refs):
    stats = refs[:n_stats]
    go, y, z, gain, ubc, cum = refs[n_stats : n_stats + 6]
    dy_ref, dz_ref, state_ref, inv_ref, ggain_ref = refs[n_stats + 6 :]
    rows, inner = y.shape
    width = inner // heads
    state_n = ubc.shape[1] // 2
    total = tree_sum([s[...] for s in stats])
    total = jnp.concatenate([total, jnp.zeros((LANES - total.shape[0], rows), f32)], axis=0).T
    inv = lax.rsqrt(total[:, 0:1] / full_inner + epsilon)
    coef = inv * inv * inv * (total[:, 1:2] / full_inner)
    inv_ref[...] = jnp.broadcast_to(inv, inv_ref.shape)
    z_val = z[...].astype(f32)
    sig = sigmoid(z_val)
    silu = z_val * sig
    y_val = y[...]
    gated = y_val * silu
    grad_o = go[...]
    ggain_ref[...] = jnp.sum(grad_o * gated * inv, axis=0, keepdims=True)
    grad_gin = inv * grad_o * gain[...] - gated * coef
    dy = grad_gin * silu
    dy_ref[...] = dy
    dz_ref[...] = (grad_gin * y_val * sig * (1.0 + z_val * (1.0 - sig))).astype(bf16)
    u_c = ubc[:, state_n:]
    c_mat = u_c * sigmoid(u_c)
    state_ref[...] = tn(dy * spread(jnp.exp(cum[...]), heads, width), c_mat)


def inner_back_kernel(
    heads, dy_ref, dz, cum_ref, dt, params, ux, ubc, state, raw, cot, inv, normed,
    dxs_ref, dbc_ref, dcum_ref, own_ref, other_ref,
):
    rows, inner = dy_ref.shape
    width = inner // heads
    state_n = ubc.shape[1] // 2
    cum = cum_ref[...]
    cum_t = cum.T
    u_x, u_bc = ux[...], ubc[...]
    x_act = u_x * sigmoid(u_x)
    bc_act = u_bc * sigmoid(u_bc)
    b_mat = bc_act[:, 0:state_n].astype(bf16)
    c_mat = bc_act[:, state_n:].astype(bf16)
    lane = iota((rows, LANES), 1)
    step = jnp.where(lane < heads, softplus(dt[...] + params[0:1, :]), 0.0)
    scaled16 = (x_act * spread(step, heads, width)).astype(bf16)
    dy = dy_ref[...]
    dy16 = dy.astype(bf16)
    gram = nt(c_mat, b_mat)
    lower = iota((rows, rows), 0) >= iota((rows, rows), 1)
    pair_lane = iota((rows, 2 * width), 1)
    grad_gram = jnp.zeros((rows, rows), f32)
    dcum = jnp.zeros((rows, LANES), f32)
    sub = iota((LANES, rows), 0)
    dcum_t = jnp.zeros((LANES, rows), f32)
    for q in range(heads // 2):
        cut = slice(2 * width * q, 2 * width * (q + 1))
        both = []
        for h in (2 * q, 2 * q + 1):
            decay = jnp.exp(jnp.where(lower, cum[:, h : h + 1] - cum_t[h : h + 1, :], -jnp.inf))
            mix = decay * gram
            both.append(tn(mix, dy16[:, cut]))
            own = (pair_lane < width) == (h % 2 == 0)
            grad_mix = nt(jnp.where(own, dy[:, cut], 0.0), scaled16[:, cut])
            grad_gram = grad_gram + grad_mix * decay
            expo = grad_mix * mix
            dcum = jnp.where(lane == h, jnp.sum(expo, axis=1, keepdims=True), dcum)
            dcum_t = jnp.where(sub == h, jnp.sum(expo, axis=0, keepdims=True), dcum_t)
        dxs_ref[:, cut] = jnp.where(pair_lane < width, both[0], both[1])
    exp_cum = spread(jnp.exp(cum), heads, width)
    cross = nt(c_mat, state[...]) * exp_cum
    dcum_ref[...] = dcum - dcum_t.T + gathered_heads(dy * cross, heads, width)
    dbc_ref[:, 0:state_n] = tn(grad_gram, c_mat)
    dbc_ref[:, state_n:] = nn(dy * exp_cum, state[...]) + nn(grad_gram, b_mat)
    weighted = (cot[...].astype(f32) * inv[:, 0:1]).astype(bf16)
    half = own_ref.shape[0]
    for ref, cut in ((own_ref, slice(0, half)), (other_ref, slice(half, 2 * half))):
        ref[:, 0:inner] = tn(normed[:, cut], dz[...]).astype(bf16)
        ref[:, inner:] = tn(weighted[:, cut], raw[...]).astype(bf16)


def ssd_back_kernel(
    heads, next_ref, dxs, dbc, dcum_ref, dy_ref, cum_ref, dt, params, ux, ubc, state,
    gux_ref, gubc_ref, edge_ref, raw_ref, ghead_ref,
):
    rows, inner = dy_ref.shape
    width = inner // heads
    state_n = ubc.shape[1] // 2
    cum = cum_ref[...]
    u_x, u_bc = ux[...], ubc[...]
    sig_x, sig_bc = sigmoid(u_x), sigmoid(u_bc)
    x_act = u_x * sig_x
    bc_act = u_bc * sig_bc
    b_mat = bc_act[:, 0:state_n].astype(bf16)
    lane = iota((rows, LANES), 1)
    shifted = dt[...] + params[0:1, :]
    step = jnp.where(lane < heads, softplus(shifted), 0.0)
    rate = -jnp.exp(params[1:2, :])
    step_wide = spread(step, heads, width)
    scaled = x_act * step_wide
    dy = dy_ref[...]
    grad_next = next_ref[...]
    to_end = spread(jnp.exp(cum[rows - 1 : rows, :] - cum), heads, width)
    from_next = nt(b_mat, grad_next) * to_end
    grad_scaled = dxs[...] + from_next
    grad_b = dbc[:, 0:state_n] + nn(scaled * to_end, grad_next)
    end_term = gathered_heads(scaled * from_next, heads, width)
    held = jnp.sum(state[...] * grad_next, axis=1, keepdims=True)
    held = jnp.broadcast_to(held, (inner, LANES))
    head_of = iota((inner, LANES), 0) // width == iota((inner, LANES), 1)
    held = jnp.sum(jnp.where(head_of, held, 0.0), axis=0, keepdims=True)
    last = jnp.sum(end_term, axis=0, keepdims=True) + jnp.exp(cum[rows - 1 : rows, :]) * held
    upper = iota((rows, rows), 0) <= iota((rows, rows), 1)
    grad_log = last + lax.dot_general(
        upper.astype(f32),
        dcum_ref[...] - end_term,
        (((1,), (0,)), ((), ())),
        precision=exact,
        preferred_element_type=f32,
    )
    grad_step = gathered_heads(grad_scaled * x_act, heads, width) + grad_log * rate
    grad_raw = jnp.where(lane < heads, grad_step * sigmoid(shifted), 0.0)
    raw_ref[...] = grad_raw.astype(bf16)
    row = iota((8, LANES), 0)
    bias_grad = jnp.sum(grad_raw, axis=0, keepdims=True)
    rate_grad = jnp.sum(grad_log * step, axis=0, keepdims=True) * rate
    skip_grad = jnp.sum(gathered_heads(dy * x_act, heads, width), axis=0, keepdims=True)
    ghead_ref[...] = jnp.where(
        row == 0, bias_grad, jnp.where(row == 1, rate_grad, jnp.where(row == 2, skip_grad, 0.0))
    )
    skip = spread(jnp.broadcast_to(params[2:3, :], (rows, LANES)), heads, width)
    gux = (grad_scaled * step_wide + dy * skip) * (sig_x * (1.0 + u_x * (1.0 - sig_x)))
    gux_ref[...] = gux
    slope = sig_bc * (1.0 + u_bc * (1.0 - sig_bc))
    gubc_ref[:, 0:state_n] = grad_b * slope[:, 0:state_n]
    gubc_ref[:, state_n:] = dbc[:, state_n:] * slope[:, state_n:]
    edge_ref[:, 0:inner] = gux_ref[0:EDGE, :]
    edge_ref[:, inner:] = gubc_ref[0:EDGE, :]


def last_kernel(pair, gain_lane, n_blocks, where, *refs):
    edge, gux, gubc, xe, be, dz, raw, normed, x_perm, inv, gain, conv_x, conv_bc, w_in = refs[:14]
    ggain, ghead = refs[14:16]
    blocks = refs[16 : 16 + n_blocks]
    gx_own, gx_other, gb_own, gb_other = refs[16 + n_blocks : 20 + n_blocks]
    hold, gx_ext, gb_ext, x_ext, b_ext, small = refs[20 + n_blocks :]
    rows, inner = gux.shape
    wide_bc = gubc.shape[1]
    taps = conv_x.shape[0] - 1
    small[...] = jnp.zeros(small.shape, f32)

    def conv_back(grad, ext, raw_ref, raw_ext, weights, next_rows, firsts, width):
        value = grad[...]
        ext[0:rows, :] = value
        ext[rows : rows + EDGE, :] = next_rows
        raw_ext[...] = raw_ref[...].astype(f32)

        def kept(k, row):
            for j, first in enumerate(firsts):
                small[first + k : first + k + 1, 0:wide_bc] = row[:, j * wide_bc : (j + 1) * wide_bc]

        total = jnp.zeros((rows, width), f32)
        for k in range(taps):
            ahead = taps - 1 - k
            total = total + weights[k : k + 1, :] * ext[ahead : ahead + rows, :]
            back = HALO - taps + 1 + k
            kept(k, jnp.sum(raw_ext[back : back + rows, :] * value, axis=0, keepdims=True))
        kept(taps, jnp.sum(value, axis=0, keepdims=True))
        return total.astype(bf16)

    n = taps + 1
    dx = conv_back(gux, gx_ext, xe, x_ext, conv_x, edge[:, 0:inner], (0, n), inner)
    dbc = conv_back(gubc, gb_ext, be, b_ext, conv_bc, edge[:, inner:], (2 * n,), wide_bc)
    for j in range(2):
        small[3 * n + j : 3 * n + j + 1, 0:wide_bc] = ggain[:, j * wide_bc : (j + 1) * wide_bc]
    small[3 * n + 2 : 3 * n + 5, 0:LANES] = ghead[0:3, :]
    dbcd = jnp.concatenate([dbc, raw[...]], axis=1)
    part = (
        nt(dz[...], w_in[:, 0:inner])
        + nt(dx, w_in[:, inner : 2 * inner])
        + nt(dbcd, w_in[:, 2 * inner :])
    )
    for p in range(part.shape[1] // LANES):
        block, lane = unit(pair, p, where)
        hold[block, :, pl.ds(lane, LANES)] = part[:, p * LANES : (p + 1) * LANES].astype(bf16)
    along = part * (x_perm[...].astype(f32) * inv[:, 0:1])
    dots = row_of(jnp.sum(along * gain[...], axis=1, keepdims=True))
    high = dots.astype(bf16).astype(f32)
    extra = jnp.where(iota((16, rows), 0) == 0, high, dots - high)
    extra = jnp.where(iota((16, rows), 0) < 2, extra, 0.0).astype(bf16)
    for k, ref in enumerate(blocks):
        ref[0:rows, :] = hold[k]
        ref[rows : rows + 16, :] = extra
    half = gx_own.shape[0]
    at = iota((half, LANES), 1) == gain_lane
    high = small[...].astype(bf16)
    low = (small[...] - high.astype(f32)).astype(bf16)
    count = small.shape[0]
    for cut, gx_ref, gb_ref in (
        (slice(0, half), gx_own, gb_own),
        (slice(half, 2 * half), gx_other, gb_other),
    ):
        gx_ref[...] = tn(normed[:, cut], dx).astype(bf16)
        g_bcd = tn(normed[:, cut], dbcd)
        g_gain = tn(along[:, cut], jnp.ones((rows, LANES), bf16))
        gb_ref[0:half, 0:wide_bc] = g_bcd[:, 0:wide_bc].astype(bf16)
        gb_ref[0:half, wide_bc:] = jnp.where(at, g_gain, g_bcd[:, wide_bc:]).astype(bf16)
        gb_ref[half : half + count, :] = high
        gb_ref[half + count :, :] = low


def fold_kernel(n_blocks, own, other, *blocks):
    size = (own.shape[0] - blocks[0].shape[0]) // (n_blocks - 1)
    extra = blocks[0].shape[0] - size
    for k, ref in enumerate(blocks):
        cut = slice(k * size, (k + 1) * size)
        ref[0:size, :] = (own[cut, :].astype(f32) + other[cut, :].astype(f32)).astype(bf16)
    if extra > 0:
        first, half = n_blocks * size, extra // 2
        total = [ref[first:, :].astype(f32) for ref in (own, other)]
        total = (total[0][:half] + total[0][half:]) + (total[1][:half] + total[1][half:])
        high = total.astype(bf16)
        low = (total - high.astype(f32)).astype(bf16)
        for ref in blocks:
            ref[size : size + half, :] = high
            ref[size + half :, :] = low


def small_kernel(taps, heads, n_blocks, *refs):
    gdt_ref, cx_ref, ghead_ref, ggain_ref, shared_ref = refs[n_blocks:]
    total = tree_sum([b[...].astype(f32) for b in refs[:n_blocks]])
    wide_bc = cx_ref.shape[1] // 2
    n, size = taps + 1, gdt_ref.shape[0]
    half = (total.shape[0] - size) // 2
    small = total[size : size + half] + total[size + half :]
    gdt_ref[...] = total[0:size, wide_bc : wide_bc + heads]
    for j in range(2):
        cut = slice(j * wide_bc, (j + 1) * wide_bc)
        cx_ref[:, cut] = small[j * n : (j + 1) * n, 0:wide_bc]
        ggain_ref[:, cut] = small[3 * n + j : 3 * n + j + 1, 0:wide_bc]
    ghead_ref[...] = small[3 * n + 2 : 3 * n + 5, 0:heads]
    shared_ref[0:size, :] = total[0:size].astype(bf16)
    high = small[2 * n : 2 * n + 8].astype(bf16)
    shared_ref[size : size + 8, :] = high
    shared_ref[size + 8 :, :] = (small[2 * n : 2 * n + 8] - high.astype(f32)).astype(bf16)


def shared_kernel(gain_lane, n_blocks, *refs):
    gbc_ref, cbc_ref, ngain_ref = refs[n_blocks:]
    total = tree_sum([b[...].astype(f32) for b in refs[:n_blocks]])
    size, wide_bc = gbc_ref.shape
    gbc_ref[...] = total[0:size, 0:wide_bc]
    rows = total[size : size + 8, 0:wide_bc] + total[size + 8 :, 0:wide_bc]
    cbc_ref[...] = rows[0 : cbc_ref.shape[0]]
    ngain_ref[...] = row_of(total[0:size, wide_bc:][:, gain_lane : gain_lane + 1])


def input_kernel(pair, full_d, n_blocks, where, *refs):
    blocks = refs[:n_blocks]
    x_local, cot, inv, gain, out_ref, out = refs[n_blocks:]
    rows, _ = x_local.shape
    total = tree_sum([b[...].astype(f32) for b in blocks])
    dots = column_of((total[rows : rows + 1, :] + total[rows + 1 : rows + 2, :]) / full_d)[:, 0:1]
    scale = inv[:, 0:1]
    for p in range(gain.shape[1] // LANES):
        block, lane = unit(pair, p, where)

        @pl.when(block == 0)
        def _():
            cut = pl.ds(lane, LANES)
            xhat = x_local[:, cut].astype(f32) * scale
            out[:, cut] = gain[:, p * LANES : (p + 1) * LANES] + 0.0 * xhat

    gains = out[...]
    xhat = x_local[...].astype(f32) * scale
    grad = cot[...].astype(f32) + scale * (total[0:rows, :] * gains - xhat * dots)
    out_ref[...] = grad.astype(bf16)


VMEM = pl.BlockSpec(memory_space=pltpu.VMEM)
SMEM = pl.BlockSpec(memory_space=pltpu.SMEM)


def call(kernel, outs, inputs, scratch=(), scalars=0):
    return pl.pallas_call(
        kernel,
        out_shape=[jax.ShapeDtypeStruct(shape, kind) for shape, kind in outs],
        in_specs=[SMEM] * scalars + [VMEM] * (len(inputs) - scalars),
        out_specs=[VMEM] * len(outs),
        scratch_shapes=[pltpu.VMEM(shape, kind) for shape, kind in scratch],
    )(*inputs)


def local(
    hidden_in, cotangent, norm_gain, w_zx, w_bc, w_dt, w_out, conv_x, conv_bc, head_params, gate_gain
):
    rows, part_d = hidden_in.shape[2:]
    heads = head_params.shape[1]
    inner = conv_x.shape[1]
    wide_bc = w_bc.shape[1]
    taps = conv_x.shape[0] - 1
    shard = w_zx.shape[0]
    dp_n, seq_n, head_n = lax.axis_size("dp"), lax.axis_size("seq"), lax.axis_size("head")
    full_d = part_d * head_n
    full_inner = inner * head_n
    dp_i, seq_i, head_i = lax.axis_index("dp"), lax.axis_index("seq"), lax.axis_index("head")
    pair = seq_n == 2 and dp_n == head_n == 4 and shard == LANES and part_d == 2 * LANES
    state_n = wide_bc // 2

    where = jnp.stack([head_i ^ dp_i, seq_i] if pair else [head_i, seq_i]).astype(jnp.int32)

    def gathered(part, axis):
        if not pair:
            return [lax.all_gather(part, ("dp", "seq"), axis=axis, tiled=True)]
        own = exchanged(part, "dp")
        return own + [sent(p, "seq", 1) for p in own]

    def reduced(own, other, extra=0):
        recv = sent(other, "seq", 1)
        blocks = call(
            functools.partial(fold_kernel, dp_n),
            [((shard + extra, own.shape[1]), bf16)] * dp_n,
            [own, recv],
        )
        return scattered(blocks, "dp")

    def reduced_apart(own, other):
        both = jnp.concatenate([own[: full_d // 2], other[: full_d // 2]], axis=0).astype(f32)
        return lax.psum_scatter(both, ("dp", "seq"), scatter_dimension=0, tiled=True)

    x_local = hidden_in[0, 0]
    cot_local = cotangent[0, 0]
    pad = jnp.zeros((shard, LANES - heads - 1), bf16)
    packed = [w_zx.reshape(shard, 2 * inner), w_bc, w_dt, norm_gain[:, None], pad]
    pieces = gathered(jnp.concatenate(packed, axis=1), 0)
    x_blocks = exchanged(x_local, "head")
    out_pieces = gathered(w_out, 1)
    cot_blocks = exchanged(cot_local, "head")
    params = jnp.pad(head_params, ((0, 5), (0, LANES - heads)))
    gain_row = gate_gain[None]
    n_in, n_out = len(pieces), len(out_pieces)
    wide_bcd = wide_bc + LANES

    normed, x_perm, inv_in, norm_row, edge = call(
        functools.partial(norm_kernel, pair, heads, head_n, n_in),
        [
            ((rows, full_d), bf16),
            ((rows, full_d), bf16),
            ((rows, LANES), f32),
            ((1, full_d), f32),
            ((HALO, full_d), bf16),
        ],
        [where, *x_blocks, *pieces],
        [((head_n, rows, part_d), f32)],
        1,
    )
    edge = passed_along(edge, "seq", 1)
    z, x_ext, bc_ext, u_x, u_bc, dt, cum, y_loc, own_state, w_in = call(
        functools.partial(forward_kernel, heads, n_in),
        [
            ((rows, inner), bf16),
            ((HALO + rows, inner), bf16),
            ((HALO + rows, wide_bc), bf16),
            ((rows, inner), f32),
            ((rows, wide_bc), f32),
            ((rows, LANES), f32),
            ((rows, LANES), f32),
            ((rows, inner), f32),
            ((inner, state_n), f32),
            ((full_d, 2 * inner + wide_bcd), bf16),
        ],
        [normed, edge, conv_x, conv_bc, params, *pieces],
        [
            ((HALO + rows, full_d), bf16),
            ((HALO + rows, inner), f32),
            ((HALO + rows, wide_bc), f32),
        ],
    )
    total_decay = jnp.repeat(jnp.exp(cum[rows - 1, :heads]), inner // heads)[:, None]
    state_in = entering(total_decay, own_state, "seq", False)
    y, grad_o, gated_raw, stats, cot_perm, w_out_full = call(
        functools.partial(gate_kernel, pair, heads, head_n, n_out),
        [
            ((rows, inner), f32),
            ((rows, inner), f32),
            ((rows, inner), bf16),
            ((8, rows), f32),
            ((rows, full_d), bf16),
            ((inner, full_d), bf16),
        ],
        [where, state_in, u_bc, cum, y_loc, z, gain_row, *cot_blocks, *out_pieces],
        [((head_n, rows, part_d), f32)],
        1,
    )
    stats = exchanged(stats, "head")
    out_blocks = call(
        functools.partial(out_kernel, pair),
        [((rows, part_d), bf16)] * head_n,
        [where, gated_raw, w_out_full],
        [((head_n, rows, part_d), bf16)],
        1,
    )
    out_sum = f32_sum(scattered(out_blocks, "head"))

    dy, dz, from_cross, inv_gate, g_ggain = call(
        functools.partial(gate_back_kernel, heads, full_inner, head_n),
        [
            ((rows, inner), f32),
            ((rows, inner), bf16),
            ((inner, state_n), f32),
            ((rows, LANES), f32),
            ((1, inner), f32),
        ],
        [*stats, grad_o, y, z, gain_row, u_bc, cum],
    )
    output = (x_local.astype(f32) + out_sum * inv_gate[:, :1]).astype(bf16)
    grad_next = entering(total_decay, from_cross, "seq", True)
    dxs, dbc, dcum, early_own, early_other = call(
        functools.partial(inner_back_kernel, heads),
        [
            ((rows, inner), f32),
            ((rows, wide_bc), f32),
            ((rows, LANES), f32),
            ((full_d // 2, 2 * inner), bf16),
            ((full_d // 2, 2 * inner), bf16),
        ],
        [dy, dz, cum, dt, params, u_x, u_bc, state_in, gated_raw, cot_perm, inv_gate, normed],
    )
    gux, gubc, edge_out, raw16, g_head = call(
        functools.partial(ssd_back_kernel, heads),
        [
            ((rows, inner), f32),
            ((rows, wide_bc), f32),
            ((EDGE, inner + wide_bc), f32),
            ((rows, LANES), bf16),
            ((8, LANES), f32),
        ],
        [grad_next, dxs, dbc, dcum, dy, cum, dt, params, u_x, u_bc, state_in],
    )
    edge_next = passed_along(edge_out, "seq", -1)
    n = taps + 1
    count = 24
    results = call(
        functools.partial(last_kernel, pair, heads, head_n),
        [((rows + 16, part_d), bf16)] * head_n
        + [((full_d // 2, inner), bf16)] * 2
        + [((full_d // 2 + 2 * count, wide_bcd), bf16)] * 2,
        [
            where, edge_next, gux, gubc, x_ext, bc_ext, dz, raw16, normed, x_perm, inv_in, norm_row,
            conv_x, conv_bc, w_in, g_ggain, g_head,
        ],
        [
            ((head_n, rows, part_d), bf16),
            ((rows + EDGE, inner), f32),
            ((rows + EDGE, wide_bc), f32),
            ((HALO + rows, inner), f32),
            ((HALO + rows, wide_bc), f32),
            ((count, wide_bcd), f32),
        ],
        1,
    )
    blocks, (gx_own, gx_other, gb_own, gb_other) = results[:head_n], results[head_n:]
    if pair:
        early = f32_sum(reduced(early_own, early_other))
        g_bcd = reduced(gb_own, gb_other, 2 * count)
        g_x = f32_sum(reduced(gx_own, gx_other))
        g_dt, g_cx, g_head, g_ggain, shared = call(
            functools.partial(small_kernel, taps, heads, dp_n),
            [
                ((shard, heads), f32),
                ((n, inner), f32),
                ((3, heads), f32),
                ((1, inner), f32),
                ((shard + 16, wide_bcd), bf16),
            ],
            g_bcd,
        )
    else:
        early = reduced_apart(early_own, early_other)
        g_bcd = reduced_apart(gb_own, gb_other)
        g_x = reduced_apart(gx_own, gx_other)
        small = lax.psum(
            gb_own[full_d // 2 :][:count].astype(f32) + gb_own[full_d // 2 + count :].astype(f32),
            ("dp", "seq"),
        )
        g_dt = g_bcd[:, wide_bc : wide_bc + heads]
        g_cx = jnp.concatenate([small[:n, :wide_bc], small[n : 2 * n, :wide_bc]], axis=1)
        g_ggain = small[3 * n : 3 * n + 2, :wide_bc].reshape(1, inner)
        g_head = small[3 * n + 2 : 3 * n + 5, :heads]
        shared = jnp.concatenate([g_bcd, small[2 * n : 3 * n]], axis=0)
    parts = scattered(blocks, "head")
    (grad_input,) = call(
        functools.partial(input_kernel, pair, full_d, head_n),
        [((rows, part_d), bf16)],
        [where, *parts, x_local, cot_local, inv_in, norm_row],
        [((rows, part_d), f32)],
        1,
    )
    shared = exchanged(shared, "head")
    if pair:
        g_bc, g_cbc, g_ngain = call(
            functools.partial(shared_kernel, heads, head_n),
            [((shard, wide_bc), f32), ((n, wide_bc), f32), ((1, shard), f32)],
            shared,
        )
        g_ngain = g_ngain.reshape(shard)
    else:
        shared = tree_sum(shared)
        g_bc, g_cbc = shared[:shard, :wide_bc], shared[shard:, :wide_bc]
        g_ngain = shared[:shard, wide_bc + heads]
    g_zx = jnp.stack([early[:, :inner], g_x], axis=1)
    return (
        output[None, None],
        grad_input[None, None],
        g_ngain,
        g_zx,
        g_bc,
        g_dt,
        early[:, inner:].T,
        g_cx,
        g_cbc,
        g_head,
        g_ggain.reshape(inner),
    )


def solution(mesh):
    tokens = P(None, "dp", "seq", "head")
    zx = P(("dp", "seq"), None, "head")
    bc = P(("dp", "seq"), None)
    dt = P(("dp", "seq"), "head")
    out = P("head", ("dp", "seq"))
    gain, heads = P(("dp", "seq")), P(None, "head")

    return jax.shard_map(
        local,
        mesh=mesh,
        in_specs=(tokens, tokens, gain, zx, bc, dt, out, heads, P(), heads, P("head")),
        out_specs=(tokens, tokens, gain, zx, bc, dt, out, heads, P(), heads, P("head")),
        check_vma=False,
    )
```

profile of v0, /device:TPU:0, one launch (start us, length us, event | category | flops | bytes accessed | tf_op | source)
XLA Modules:
  0.0 158.5 jit_solution(17486559484894016380)
XLA Ops:
  4.3 4.0 %collective-permute-start.5 = (bf16[128,1408]{1,0:T(8,128)(2,1)S(1)}, bf16[128,1408]{1,0:T(8,128)(2,1)S(1)}, u32[]{:S(2)}, u32[]{:S(2)}) collective-permute-start(bf16[128,1408]{1,0:T(8,128)(2,1)S(1)} %concatenate.3.refs_4_.refs_5_), channel_id=1, source_target_pairs={{0,24},{8,16},{16,8},{24,0},{1,25},{9,17},{17,9},{25,1},{2,26},{10... | collective-permute-start | bytes 1081352 | tf_op jit(solution)/shard_map/ppermute | solution.py:25
  8.9 4.0 %collective-permute-start.2 = (bf16[256,256]{1,0:T(8,128)(2,1)}, bf16[256,256]{1,0:T(8,128)(2,1)S(1)}, u32[]{:S(2)}, u32[]{:S(2)}) collective-permute-start(bf16[256,256]{1,0:T(8,128)(2,1)} %bitcast.20), channel_id=1, source_target_pairs={{0,3},{1,2},{2,1},{3,0},{4,7},{5,6},{6,5},{7,4},{8,11},{9,10},{10,... | collective-permute-start | bytes 393224 | tf_op jit(solution)/shard_map/ppermute | solution.py:25
  12.9 3.2 %collective-permute-done.2.refs_3_ = bf16[256,256]{1,0:T(8,128)(2,1)S(1)} collective-permute-done((bf16[256,256]{1,0:T(8,128)(2,1)}, bf16[256,256]{1,0:T(8,128)(2,1)S(1)}, u32[]{:S(2)}, u32[]{:S(2)}) %collective-permute-start.2) | collective-permute-done | bytes 131104 | tf_op jit(solution)/shard_map/ppermute | solution.py:25
  16.1 3.8 %collective-permute-start.1 = (bf16[256,256]{1,0:T(8,128)(2,1)}, bf16[256,256]{1,0:T(8,128)(2,1)S(1)}, u32[]{:S(2)}, u32[]{:S(2)}) collective-permute-start(bf16[256,256]{1,0:T(8,128)(2,1)} %bitcast.21), channel_id=1, source_target_pairs={{0,2},{1,3},{2,0},{3,1},{4,6},{5,7},{6,4},{7,5},{8,10},{9,11},{10,... | collective-permute-start | bytes 393224 | tf_op jit(solution)/shard_map/ppermute | solution.py:25
  19.8 4.6 %collective-permute-done.4.refs_6_.refs_7_ = bf16[128,1408]{1,0:T(8,128)(2,1)S(1)} collective-permute-done((bf16[128,1408]{1,0:T(8,128)(2,1)S(1)}, bf16[128,1408]{1,0:T(8,128)(2,1)S(1)}, u32[]{:S(2)}, u32[]{:S(2)}) %collective-permute-start.4) | collective-permute-done | bytes 360480 | tf_op jit(solution)/shard_map/ppermute | solution.py:25
  26.7 4.1 %collective-permute-done.refs_1_ = bf16[256,256]{1,0:T(8,128)(2,1)S(1)} collective-permute-done((bf16[256,256]{1,0:T(8,128)(2,1)}, bf16[256,256]{1,0:T(8,128)(2,1)S(1)}, u32[]{:S(2)}, u32[]{:S(2)}) %collective-permute-start) | collective-permute-done | bytes 131104 | tf_op jit(solution)/shard_map/ppermute | solution.py:25
  30.8 3.6 %collective-permute-start.14 = (bf16[256,256]{1,0:T(8,128)(2,1)}, bf16[256,256]{1,0:T(8,128)(2,1)S(1)}, u32[]{:S(2)}, u32[]{:S(2)}) collective-permute-start(bf16[256,256]{1,0:T(8,128)(2,1)} %bitcast.26), channel_id=1, source_target_pairs={{0,3},{1,2},{2,1},{3,0},{4,7},{5,6},{6,5},{7,4},{8,11},{9,10},{10,... | collective-permute-start | bytes 393224 | tf_op jit(solution)/shard_map/ppermute | solution.py:25
  36.8 3.3 %shard_map.194 = (bf16[256,1024]{1,0:T(8,128)(2,1)}, bf16[256,1024]{1,0:T(8,128)(2,1)}, f32[256,128]{1,0:T(8,128)}, f32[1,1024]{1,0:T(1,128)}, bf16[16,1024]{1,0:T(8,128)(2,1)}) custom-call(s32[2]{0:T(128)} %pad_add_fusion.where, bf16[256,256]{1,0:T(8,128)(2,1)} %bitcast.23, bf16[256,256]{1,0:T(8,128)(2,1)} %copy-done.32, bf16[256,256]{1,0:T(8,128)(2,1)} %copy-done.30, ...), custom_call_target="tpu_custom_call" | custom-call | tf_op jit(solution)/shard_map/pallas_call | solution.py:576
  46.2 5.9 %shard_map.195 = (bf16[256,512]{1,0:T(8,128)(2,1)}, bf16[272,512]{1,0:T(8,128)(2,1)}, bf16[272,256]{1,0:T(8,128)(2,1)}, f32[256,512]{1,0:T(8,128)}, f32[256,256]...) custom-call(bf16[256,1024]{1,0:T(8,128)(2,1)} %get-tuple-element.79., ...), custom_call_target="tpu_custom_call" | custom-call | tf_op jit(solution)/shard_map/pallas_call | solution.py:576
  54.8 2.3 %collective-permute-done.15.refs_11_ = bf16[512,128]{1,0:T(8,128)(2,1)S(1)} collective-permute-done((bf16[512,128]{1,0:T(8,128)(2,1)S(1)}, bf16[512,128]{1,0:T(8,128)(2,1)S(1)}, u32[]{:S(2)}, u32[]{:S(2)}) %collective-permute-start.15) | collective-permute-done | bytes 131104 | tf_op jit(solution)/shard_map/ppermute | solution.py:25
  59.2 4.2 %shard_map.196 = (f32[256,512]{1,0:T(8,128)}, f32[256,512]{1,0:T(8,128)}, bf16[256,512]{1,0:T(8,128)(2,1)}, f32[8,256]{1,0:T(8,128)}, bf16[256,1024]{1,0:T(8,128)(2,1)}, /*index=5*/bf16[512,1024]{1,0:T(8,128)(2,1)}) custom-call(s32[2]{0:T(128)} %pad_add_fusion.where, f32[512,128]{1,0:T(8,128)} %copy-done.1, ...), custom_call_target="tpu_custom_call" | custom-call | tf_op jit(solution)/shard_map/pallas_call | solution.py:576
  63.4 3.3 %collective-permute-start.27 = (f32[8,256]{1,0:T(8,128)}, f32[8,256]{1,0:T(8,128)S(1)}, u32[]{:S(2)}, u32[]{:S(2)}) collective-permute-start(f32[8,256]{1,0:T(8,128)} %get-tuple-element.92.refs_0_), channel_id=1, source_target_pairs={{0,3},{1,2},{2,1},{3,0},{4,7},{5,6},{6,5},{7,4},{8,11},{9,10},{10,... | collective-permute-start | bytes 24584 | tf_op jit(solution)/shard_map/ppermute | solution.py:25
  69.2 2.3 %collective-permute-done.26.refs_2_ = f32[8,256]{1,0:T(8,128)S(1)} collective-permute-done((f32[8,256]{1,0:T(8,128)}, f32[8,256]{1,0:T(8,128)S(1)}, u32[]{:S(2)}, u32[]{:S(2)}) %collective-permute-start.26) | collective-permute-done | bytes 8224 | tf_op jit(solution)/shard_map/ppermute | solution.py:25
  72.1 3.1 %shard_map.198 = (f32[256,512]{1,0:T(8,128)}, bf16[256,512]{1,0:T(8,128)(2,1)}, f32[512,128]{1,0:T(8,128)}, f32[256,128]{1,0:T(8,128)}, f32[1,512]{1,0:T(1,128)}) custom-call(f32[8,256]{1,0:T(8,128)} %get-tuple-element.92.refs_0_, f32[8,256]{1,0:T(8,128)} %copy-done.48, f32[8,256]{1,0:T(8,128)} %copy-done.47, f32[8,256]{1,0:T(8,128)} %copy-done.46, ...), custom_call_target="tpu_custom_call" | custom-call | tf_op jit(solution)/shard_map/pallas_call | solution.py:576
  75.2 6.9 %shard_map.199 = (f32[256,512]{1,0:T(8,128)}, f32[256,256]{1,0:T(8,128)}, f32[256,128]{1,0:T(8,128)}, bf16[512,1024]{1,0:T(8,128)(2,1)}, bf16[512,1024]{1,0:T(8,128)(2,1)}) custom-call(f32[256,512]{1,0:T(8,128)} %get-tuple-element.97.dy_ref, bf16[256,512]{1,0:T(8,128)(2,1)} %get-tuple-element.98.dz.refs_5_, ...), custom_call_target="tpu_custom_call" | custom-call | tf_op jit(solution)/shard_map/pallas_call | solution.py:576
  83.6 1.9 %collective-permute-done.28.next_ref = f32[512,128]{1,0:T(8,128)S(1)} collective-permute-done((f32[512,128]{1,0:T(8,128)S(1)}, f32[512,128]{1,0:T(8,128)S(1)}, u32[]{:S(2)}, u32[]{:S(2)}) %collective-permute-start.28) | collective-permute-done | bytes 262176 | tf_op jit(solution)/shard_map/ppermute | solution.py:51
  86.2 4.6 %shard_map.200 = (f32[256,512]{1,0:T(8,128)}, f32[256,256]{1,0:T(8,128)}, f32[8,768]{1,0:T(8,128)}, bf16[256,128]{1,0:T(8,128)(2,1)}, f32[8,128]{1,0:T(8,128)}) custom-call(f32[512,128]{1,0:T(8,128)} %copy-done.15, f32[256,512]{1,0:T(8,128)} %get-tuple-element.102.dxs, f32[256,256]{1,0:T(8,128)} %get-tuple-element.103.dbc, ...), custom_call_target="tpu_custom_call" | custom-call | tf_op jit(solution)/shard_map/pallas_call | solution.py:576
  92.1 2.0 %collective-permute-done.29.refs_0_ = f32[8,768]{1,0:T(8,128)S(1)} collective-permute-done((f32[8,768]{1,0:T(8,128)}, f32[8,768]{1,0:T(8,128)S(1)}, u32[]{:S(2)}, u32[]{:S(2)}) %collective-permute-start.29) | collective-permute-done | bytes 24608 | tf_op jit(solution)/shard_map/ppermute | solution.py:51
  94.7 6.7 %shard_map.201 = (bf16[272,256]{1,0:T(8,128)(2,1)}, bf16[272,256]{1,0:T(8,128)(2,1)}, bf16[272,256]{1,0:T(8,128)(2,1)}, bf16[272,256]{1,0:T(8,128)(2,1)}, bf16[5...) custom-call(s32[2]{0:T(128)} %pad_add_fusion.where, ...), custom_call_target="tpu_custom_call" | custom-call | tf_op jit(solution)/shard_map/pallas_call | solution.py:576
  102.0 2.6 %shard_map.197 = (bf16[256,256]{1,0:T(8,128)(2,1)}, bf16[256,256]{1,0:T(8,128)(2,1)}, bf16[256,256]{1,0:T(8,128)(2,1)}, bf16[256,256]{1,0:T(8,128)(2,1)}) custom-call(s32[2]{0:T(128)} %pad_add_fusion.where, bf16[256,512]{1,0:T(8,128)(2,1)} %get-tuple-element.86.raw, bf16[512,1024]{1,0:T(8,128)(2,1)} %get-tuple-element.87.weights), custom_call_target="tpu_custom_call" | custom-call | tf_op jit(solution)/shard_map/pallas_call | solution.py:576
  106.7 2.3 %collective-permute-start.24 = (bf16[256,256]{1,0:T(8,128)(2,1)}, bf16[256,256]{1,0:T(8,128)(2,1)S(1)}, u32[]{:S(2)}, u32[]{:S(2)}) collective-permute-start(bf16[256,256]{1,0:T(8,128)(2,1)} %get-tuple-element.91), channel_id=1, source_target_pairs={{0,3},{1,2},{2,1},{3,0},{4,7},{5,6},{6,5},{7,4},{8,11},{9,10},{10,... | collective-permute-start | bytes 393224 | tf_op jit(solution)/shard_map/ppermute | solution.py:25
  109.0 2.0 %shard_map.203 = (bf16[176,384]{1,0:T(8,128)(2,1)}, bf16[176,384]{1,0:T(8,128)(2,1)}, bf16[176,384]{1,0:T(8,128)(2,1)}, bf16[176,384]{1,0:T(8,128)(2,1)}) custom-call(bf16[560,384]{1,0:T(8,128)(2,1)} %get-tuple-element.121.own, bf16[560,384]{1,0:T(8,128)(2,1)} %copy-done.14), custom_call_target="tpu_custom_call" | custom-call | tf_op jit(solution)/shard_map/pallas_call | solution.py:576
  111.0 2.1 %collective-permute-done.22 = bf16[256,256]{1,0:T(8,128)(2,1)S(1)} collective-permute-done((bf16[256,256]{1,0:T(8,128)(2,1)}, bf16[256,256]{1,0:T(8,128)(2,1)S(1)}, u32[]{:S(2)}, u32[]{:S(2)}) %collective-permute-start.22) | collective-permute-done | bytes 131104 | tf_op jit(solution)/shard_map/ppermute | solution.py:25
  113.7 4.2 %collective-permute-done.23 = bf16[256,256]{1,0:T(8,128)(2,1)S(1)} collective-permute-done((bf16[256,256]{1,0:T(8,128)(2,1)}, bf16[256,256]{1,0:T(8,128)(2,1)S(1)}, u32[]{:S(2)}, u32[]{:S(2)}) %collective-permute-start.23) | collective-permute-done | bytes 131104 | tf_op jit(solution)/shard_map/ppermute | solution.py:25
  120.0 1.9 %collective-permute-start.30 = (bf16[272,256]{1,0:T(8,128)(2,1)}, bf16[272,256]{1,0:T(8,128)(2,1)S(1)}, u32[]{:S(2)}, u32[]{:S(2)}) collective-permute-start(bf16[272,256]{1,0:T(8,128)(2,1)} %get-tuple-element.118), channel_id=1, source_target_pairs={{0,1},{1,0},{2,3},{3,2},{4,5},{5,4},{6,7},{7,6},{8,9},{9,8},{10,11... | collective-permute-start | bytes 417800 | tf_op jit(solution)/shard_map/ppermute | solution.py:25
  123.6 4.7 %collective-permute-start.32 = (bf16[272,256]{1,0:T(8,128)(2,1)}, bf16[272,256]{1,0:T(8,128)(2,1)S(1)}, u32[]{:S(2)}, u32[]{:S(2)}) collective-permute-start(bf16[272,256]{1,0:T(8,128)(2,1)} %get-tuple-element.120), channel_id=1, source_target_pairs={{0,3},{1,2},{2,1},{3,0},{4,7},{5,6},{6,5},{7,4},{8,11},{9,10},{10,... | collective-permute-start | bytes 417800 | tf_op jit(solution)/shard_map/ppermute | solution.py:25
  128.3 2.0 %shard_map.207 = (bf16[128,512]{1,0:T(8,128)(2,1)}, bf16[128,512]{1,0:T(8,128)(2,1)}, bf16[128,512]{1,0:T(8,128)(2,1)}, bf16[128,512]{1,0:T(8,128)(2,1)}) custom-call(bf16[512,512]{1,0:T(8,128)(2,1)} %get-tuple-element.135.own, bf16[512,512]{1,0:T(8,128)(2,1)} %copy-done.12), custom_call_target="tpu_custom_call" | custom-call | tf_op jit(solution)/shard_map/pallas_call | solution.py:576
  134.4 2.6 %shard_map.206 = (bf16[128,1024]{1,0:T(8,128)(2,1)}, bf16[128,1024]{1,0:T(8,128)(2,1)}, bf16[128,1024]{1,0:T(8,128)(2,1)}, bf16[128,1024]{1,0:T(8,128)(2,1)}) custom-call(bf16[512,1024]{1,0:T(8,128)(2,1)} %get-tuple-element.129.own, bf16[512,1024]{1,0:T(8,128)(2,1)} %copy-done.10), custom_call_target="tpu_custom_call" | custom-call | tf_op jit(solution)/shard_map/pallas_call | solution.py:576
  142.9 2.5 %shard_map.202 = bf16[256,256]{1,0:T(8,128)(2,1)} custom-call(s32[2]{0:T(128)} %pad_add_fusion.where, bf16[272,256]{1,0:T(8,128)(2,1)} %get-tuple-element.117.refs_0_, bf16[272,256]{1,0:T(8,128)(2,1)} %copy-done.17, bf16[272,256]{1,0:T(8,128)(2,1)} %copy-done.18, bf16[272,256]{1,0:T(8,128)(2,1)} %copy-done.19, bf16[256,256]{1,0:T(8,128)(2,1)} %bitcast.24, ...), custom_call_target="tpu_custom_call" | custom-call | tf_op jit(solution)/shard_map/pallas_call | solution.py:576
  146.1 2.1 %collective-permute-start.38 = (bf16[144,384]{1,0:T(8,128)(2,1)S(1)}, bf16[144,384]{1,0:T(8,128)(2,1)S(1)}, u32[]{:S(2)}, u32[]{:S(2)}) collective-permute-start(bf16[144,384]{1,0:T(8,128)(2,1)S(1)} %copy-done.39), channel_id=1, source_target_pairs={{0,2},{1,3},{2,0},{3,1},{4,6},{5,7},{6,4},{7,5},{8,10},{9,11},{10,... | collective-permute-start | bytes 331784 | tf_op jit(solution)/shard_map/ppermute | solution.py:25
  148.1 2.3 %collective-permute-start.37 = (bf16[144,384]{1,0:T(8,128)(2,1)S(1)}, bf16[144,384]{1,0:T(8,128)(2,1)S(1)}, u32[]{:S(2)}, u32[]{:S(2)}) collective-permute-start(bf16[144,384]{1,0:T(8,128)(2,1)S(1)} %copy-done.39), channel_id=1, source_target_pairs={{0,1},{1,0},{2,3},{3,2},{4,5},{5,4},{6,7},{7,6},{8,9},{9,8},{10,11... | collective-permute-start | bytes 331784 | tf_op jit(solution)/shard_map/ppermute | solution.py:25
  150.5 2.5 %collective-permute-done.38.refs_2_ = bf16[144,384]{1,0:T(8,128)(2,1)S(1)} collective-permute-done((bf16[144,384]{1,0:T(8,128)(2,1)S(1)}, bf16[144,384]{1,0:T(8,128)(2,1)S(1)}, u32[]{:S(2)}, u32[]{:S(2)}) %collective-permute-start.38) | collective-permute-done | bytes 110624 | tf_op jit(solution)/shard_map/ppermute | solution.py:25
  (196 shorter events, 49.9 us)
Async XLA Ops:
  4.3 15.5 %collective-permute-start.5 = (bf16[128,1408]{1,0:T(8,128)(2,1)S(1)}, bf16[128,1408]{1,0:T(8,128)(2,1)S(1)}, u32[]{:S(2)}, u32[]{:S(2)}) collective-permute-start(bf16[128,1408]{1,0:T(8,128)(2,1)S(1)} %concatenate.3.refs_4_.refs_5_), channel_id=1, source_target_pairs={{0,24},{8,16},{16,8},{24,0},{1,25},{9,17},{17,9},{25,1},{2,26},{10... | collective-permute-start | bytes 1081352 | tf_op jit(solution)/shard_map/ppermute | solution.py:25
  8.3 16.1 %collective-permute-start.4 = (bf16[128,1408]{1,0:T(8,128)(2,1)S(1)}, bf16[128,1408]{1,0:T(8,128)(2,1)S(1)}, u32[]{:S(2)}, u32[]{:S(2)}) collective-permute-start(bf16[128,1408]{1,0:T(8,128)(2,1)S(1)} %concatenate.3.refs_4_.refs_5_), channel_id=1, source_target_pairs={{0,16},{8,24},{16,0},{24,8},{1,17},{9,25},{17,1},{25,9},{2,18},{10... | collective-permute-start | bytes 1081352 | tf_op jit(solution)/shard_map/ppermute | solution.py:25
  8.8 15.9 %collective-permute-start.3 = (bf16[128,1408]{1,0:T(8,128)(2,1)S(1)}, bf16[128,1408]{1,0:T(8,128)(2,1)S(1)}, u32[]{:S(2)}, u32[]{:S(2)}) collective-permute-start(bf16[128,1408]{1,0:T(8,128)(2,1)S(1)} %concatenate.3.refs_4_.refs_5_), channel_id=1, source_target_pairs={{0,8},{8,0},{16,24},{24,16},{1,9},{9,1},{17,25},{25,17},{2,10},{10... | collective-permute-start | bytes 1081352 | tf_op jit(solution)/shard_map/ppermute | solution.py:25
  8.9 7.2 %collective-permute-start.2 = (bf16[256,256]{1,0:T(8,128)(2,1)}, bf16[256,256]{1,0:T(8,128)(2,1)S(1)}, u32[]{:S(2)}, u32[]{:S(2)}) collective-permute-start(bf16[256,256]{1,0:T(8,128)(2,1)} %bitcast.20), channel_id=1, source_target_pairs={{0,3},{1,2},{2,1},{3,0},{4,7},{5,6},{6,5},{7,4},{8,11},{9,10},{10,... | collective-permute-start | bytes 393224 | tf_op jit(solution)/shard_map/ppermute | solution.py:25
  12.9 21.5 %collective-permute-start.6 = (bf16[128,1408]{1,0:T(8,128)(2,1)S(1)}, bf16[128,1408]{1,0:T(8,128)(2,1)S(1)}, u32[]{:S(2)}, u32[]{:S(2)}) collective-permute-start(bf16[128,1408]{1,0:T(8,128)(2,1)S(1)} %concatenate.3.refs_4_.refs_5_), channel_id=1, source_target_pairs={{0,4},{4,0},{1,5},{5,1},{2,6},{6,2},{3,7},{7,3},{8,12},{12,8},{9,1... | collective-permute-start | bytes 1081352 | tf_op jit(solution)/shard_map/ppermute | solution.py:25
  16.1 8.9 %collective-permute-start.1 = (bf16[256,256]{1,0:T(8,128)(2,1)}, bf16[256,256]{1,0:T(8,128)(2,1)S(1)}, u32[]{:S(2)}, u32[]{:S(2)}) collective-permute-start(bf16[256,256]{1,0:T(8,128)(2,1)} %bitcast.21), channel_id=1, source_target_pairs={{0,2},{1,3},{2,0},{3,1},{4,6},{5,7},{6,4},{7,5},{8,10},{9,11},{10,... | collective-permute-start | bytes 393224 | tf_op jit(solution)/shard_map/ppermute | solution.py:25
  19.8 15.3 %collective-permute-start.9 = (bf16[128,1408]{1,0:T(8,128)(2,1)S(1)}, bf16[128,1408]{1,0:T(8,128)(2,1)S(1)}, u32[]{:S(2)}, u32[]{:S(2)}) collective-permute-start(bf16[128,1408]{1,0:T(8,128)(2,1)S(1)} %collective-permute-done.5.refs_7_.refs_8_), channel_id=1, source_target_pairs={{0,4},{4,0},{1,5},{5,1},{2,6},{6,2},{3,7},{7,3},{8,12},{12,8},{9,1... | collective-permute-start | bytes 1081352 | tf_op jit(solution)/shard_map/ppermute | solution.py:25
  24.4 10.8 %collective-permute-start.8 = (bf16[128,1408]{1,0:T(8,128)(2,1)S(1)}, bf16[128,1408]{1,0:T(8,128)(2,1)S(1)}, u32[]{:S(2)}, u32[]{:S(2)}) collective-permute-start(bf16[128,1408]{1,0:T(8,128)(2,1)S(1)} %collective-permute-done.4.refs_6_.refs_7_), channel_id=1, source_target_pairs={{0,4},{4,0},{1,5},{5,1},{2,6},{6,2},{3,7},{7,3},{8,12},{12,8},{9,1... | collective-permute-start | bytes 1081352 | tf_op jit(solution)/shard_map/ppermute | solution.py:25
  24.7 10.5 %collective-permute-start.7 = (bf16[128,1408]{1,0:T(8,128)(2,1)S(1)}, bf16[128,1408]{1,0:T(8,128)(2,1)S(1)}, u32[]{:S(2)}, u32[]{:S(2)}) collective-permute-start(bf16[128,1408]{1,0:T(8,128)(2,1)S(1)} %collective-permute-done.3.refs_5_.refs_6_), channel_id=1, source_target_pairs={{0,4},{4,0},{1,5},{5,1},{2,6},{6,2},{3,7},{7,3},{8,12},{12,8},{9,1... | collective-permute-start | bytes 1081352 | tf_op jit(solution)/shard_map/ppermute | solution.py:25
  30.8 21.2 %collective-permute-start.14 = (bf16[256,256]{1,0:T(8,128)(2,1)}, bf16[256,256]{1,0:T(8,128)(2,1)S(1)}, u32[]{:S(2)}, u32[]{:S(2)}) collective-permute-start(bf16[256,256]{1,0:T(8,128)(2,1)} %bitcast.26), channel_id=1, source_target_pairs={{0,3},{1,2},{2,1},{3,0},{4,7},{5,6},{6,5},{7,4},{8,11},{9,10},{10,... | collective-permute-start | bytes 393224 | tf_op jit(solution)/shard_map/ppermute | solution.py:25
  34.4 18.3 %collective-permute-start.13 = (bf16[256,256]{1,0:T(8,128)(2,1)}, bf16[256,256]{1,0:T(8,128)(2,1)S(1)}, u32[]{:S(2)}, u32[]{:S(2)}) collective-permute-start(bf16[256,256]{1,0:T(8,128)(2,1)} %bitcast.27), channel_id=1, source_target_pairs={{0,2},{1,3},{2,0},{3,1},{4,6},{5,7},{6,4},{7,5},{8,10},{9,11},{10,... | collective-permute-start | bytes 393224 | tf_op jit(solution)/shard_map/ppermute | solution.py:25
  41.4 12.7 %collective-permute-start.12 = (bf16[256,256]{1,0:T(8,128)(2,1)S(1)}, bf16[256,256]{1,0:T(8,128)(2,1)S(1)}, u32[]{:S(2)}, u32[]{:S(2)}) collective-permute-start(bf16[256,256]{1,0:T(8,128)(2,1)S(1)} %bitcast.30), channel_id=1, source_target_pairs={{0,1},{1,0},{2,3},{3,2},{4,5},{5,4},{6,7},{7,6},{8,9},{9,8},{10,11... | collective-permute-start | bytes 393224 | tf_op jit(solution)/shard_map/ppermute | solution.py:25
  42.6 11.5 %collective-permute-start.17 = (bf16[512,128]{1,0:T(8,128)(2,1)S(1)}, bf16[512,128]{1,0:T(8,128)(2,1)S(1)}, u32[]{:S(2)}, u32[]{:S(2)}) collective-permute-start(bf16[512,128]{1,0:T(8,128)(2,1)S(1)} %copy-done.23), channel_id=1, source_target_pairs={{0,24},{8,16},{16,8},{24,0},{1,25},{9,17},{17,9},{25,1},{2,26},{10... | collective-permute-start | bytes 393224 | tf_op jit(solution)/shard_map/ppermute | solution.py:25
  45.0 9.7 %collective-permute-start.16 = (bf16[512,128]{1,0:T(8,128)(2,1)S(1)}, bf16[512,128]{1,0:T(8,128)(2,1)S(1)}, u32[]{:S(2)}, u32[]{:S(2)}) collective-permute-start(bf16[512,128]{1,0:T(8,128)(2,1)S(1)} %copy-done.23), channel_id=1, source_target_pairs={{0,16},{8,24},{16,0},{24,8},{1,17},{9,25},{17,1},{25,9},{2,18},{10... | collective-permute-start | bytes 393224 | tf_op jit(solution)/shard_map/ppermute | solution.py:25
  82.1 49.4 %collective-permute-start.40 = (bf16[512,1024]{1,0:T(8,128)(2,1)}, bf16[512,1024]{1,0:T(8,128)(2,1)S(1)}, u32[]{:S(2)}, u32[]{:S(2)}) collective-permute-start(bf16[512,1024]{1,0:T(8,128)(2,1)} %get-tuple-element.130), channel_id=1, source_target_pairs={{0,4},{4,0},{1,5},{5,1},{2,6},{6,2},{3,7},{7,3},{8,12},{12,8},{9,1... | collective-permute-start | bytes 3145736 | tf_op jit(solution)/shard_map/ppermute | solution.py:25
  101.7 18.4 %collective-permute-start.44 = (bf16[512,512]{1,0:T(8,128)(2,1)}, bf16[512,512]{1,0:T(8,128)(2,1)S(1)}, u32[]{:S(2)}, u32[]{:S(2)}) collective-permute-start(bf16[512,512]{1,0:T(8,128)(2,1)} %get-tuple-element.136), channel_id=1, source_target_pairs={{0,4},{4,0},{1,5},{5,1},{2,6},{6,2},{3,7},{7,3},{8,12},{12,8},{9,1... | collective-permute-start | bytes 1572872 | tf_op jit(solution)/shard_map/ppermute | solution.py:25
  104.6 8.4 %collective-permute-start.22 = (bf16[256,256]{1,0:T(8,128)(2,1)}, bf16[256,256]{1,0:T(8,128)(2,1)S(1)}, u32[]{:S(2)}, u32[]{:S(2)}) collective-permute-start(bf16[256,256]{1,0:T(8,128)(2,1)} %get-tuple-element.89), channel_id=1, source_target_pairs={{0,1},{1,0},{2,3},{3,2},{4,5},{5,4},{6,7},{7,6},{8,9},{9,8},{10,11... | collective-permute-start | bytes 393224 | tf_op jit(solution)/shard_map/ppermute | solution.py:25
  104.9 13.0 %collective-permute-start.23 = (bf16[256,256]{1,0:T(8,128)(2,1)}, bf16[256,256]{1,0:T(8,128)(2,1)S(1)}, u32[]{:S(2)}, u32[]{:S(2)}) collective-permute-start(bf16[256,256]{1,0:T(8,128)(2,1)} %get-tuple-element.90), channel_id=1, source_target_pairs={{0,2},{1,3},{2,0},{3,1},{4,6},{5,7},{6,4},{7,5},{8,10},{9,11},{10,... | collective-permute-start | bytes 393224 | tf_op jit(solution)/shard_map/ppermute | solution.py:25
  106.7 12.0 %collective-permute-start.24 = (bf16[256,256]{1,0:T(8,128)(2,1)}, bf16[256,256]{1,0:T(8,128)(2,1)S(1)}, u32[]{:S(2)}, u32[]{:S(2)}) collective-permute-start(bf16[256,256]{1,0:T(8,128)(2,1)} %get-tuple-element.91), channel_id=1, source_target_pairs={{0,3},{1,2},{2,1},{3,0},{4,7},{5,6},{6,5},{7,4},{8,11},{9,10},{10,... | collective-permute-start | bytes 393224 | tf_op jit(solution)/shard_map/ppermute | solution.py:25
  113.0 8.9 %collective-permute-start.34 = (bf16[176,384]{1,0:T(8,128)(2,1)}, bf16[176,384]{1,0:T(8,128)(2,1)S(1)}, u32[]{:S(2)}, u32[]{:S(2)}) collective-permute-start(bf16[176,384]{1,0:T(8,128)(2,1)} %get-tuple-element.124), channel_id=1, source_target_pairs={{0,8},{8,0},{16,24},{24,16},{1,9},{9,1},{17,25},{25,17},{2,10},{10... | collective-permute-start | bytes 405512 | tf_op jit(solution)/shard_map/ppermute | solution.py:25
  118.7 11.6 %collective-permute-start.36 = (bf16[176,384]{1,0:T(8,128)(2,1)}, bf16[176,384]{1,0:T(8,128)(2,1)S(1)}, u32[]{:S(2)}, u32[]{:S(2)}) collective-permute-start(bf16[176,384]{1,0:T(8,128)(2,1)} %get-tuple-element.126), channel_id=1, source_target_pairs={{0,24},{8,16},{16,8},{24,0},{1,25},{9,17},{17,9},{25,1},{2,26},{10... | collective-permute-start | bytes 405512 | tf_op jit(solution)/shard_map/ppermute | solution.py:25
  120.0 17.0 %collective-permute-start.30 = (bf16[272,256]{1,0:T(8,128)(2,1)}, bf16[272,256]{1,0:T(8,128)(2,1)S(1)}, u32[]{:S(2)}, u32[]{:S(2)}) collective-permute-start(bf16[272,256]{1,0:T(8,128)(2,1)} %get-tuple-element.118), channel_id=1, source_target_pairs={{0,1},{1,0},{2,3},{3,2},{4,5},{5,4},{6,7},{7,6},{8,9},{9,8},{10,11... | collective-permute-start | bytes 417800 | tf_op jit(solution)/shard_map/ppermute | solution.py:25
  121.9 16.7 %collective-permute-start.31 = (bf16[272,256]{1,0:T(8,128)(2,1)}, bf16[272,256]{1,0:T(8,128)(2,1)S(1)}, u32[]{:S(2)}, u32[]{:S(2)}) collective-permute-start(bf16[272,256]{1,0:T(8,128)(2,1)} %get-tuple-element.119), channel_id=1, source_target_pairs={{0,2},{1,3},{2,0},{3,1},{4,6},{5,7},{6,4},{7,5},{8,10},{9,11},{10,... | collective-permute-start | bytes 417800 | tf_op jit(solution)/shard_map/ppermute | solution.py:25
  123.6 15.0 %collective-permute-start.32 = (bf16[272,256]{1,0:T(8,128)(2,1)}, bf16[272,256]{1,0:T(8,128)(2,1)S(1)}, u32[]{:S(2)}, u32[]{:S(2)}) collective-permute-start(bf16[272,256]{1,0:T(8,128)(2,1)} %get-tuple-element.120), channel_id=1, source_target_pairs={{0,3},{1,2},{2,1},{3,0},{4,7},{5,6},{6,5},{7,4},{8,11},{9,10},{10,... | collective-permute-start | bytes 417800 | tf_op jit(solution)/shard_map/ppermute | solution.py:25
  130.3 9.5 %collective-permute-start.45 = (bf16[128,512]{1,0:T(8,128)(2,1)}, bf16[128,512]{1,0:T(8,128)(2,1)S(1)}, u32[]{:S(2)}, u32[]{:S(2)}) collective-permute-start(bf16[128,512]{1,0:T(8,128)(2,1)} %get-tuple-element.138), channel_id=1, source_target_pairs={{0,8},{8,0},{16,24},{24,16},{1,9},{9,1},{17,25},{25,17},{2,10},{10... | collective-permute-start | bytes 393224 | tf_op jit(solution)/shard_map/ppermute | solution.py:25
  131.5 9.5 %collective-permute-start.46 = (bf16[128,512]{1,0:T(8,128)(2,1)}, bf16[128,512]{1,0:T(8,128)(2,1)S(1)}, u32[]{:S(2)}, u32[]{:S(2)}) collective-permute-start(bf16[128,512]{1,0:T(8,128)(2,1)} %get-tuple-element.139), channel_id=1, source_target_pairs={{0,16},{8,24},{16,0},{24,8},{1,17},{9,25},{17,1},{25,9},{2,18},{10... | collective-permute-start | bytes 393224 | tf_op jit(solution)/shard_map/ppermute | solution.py:25
  137.1 9.0 %collective-permute-start.47 = (bf16[128,512]{1,0:T(8,128)(2,1)}, bf16[128,512]{1,0:T(8,128)(2,1)S(1)}, u32[]{:S(2)}, u32[]{:S(2)}) collective-permute-start(bf16[128,512]{1,0:T(8,128)(2,1)} %get-tuple-element.140), channel_id=1, source_target_pairs={{0,24},{8,16},{16,8},{24,0},{1,25},{9,17},{17,9},{25,1},{2,26},{10... | collective-permute-start | bytes 393224 | tf_op jit(solution)/shard_map/ppermute | solution.py:25
  138.6 9.6 %collective-permute-start.39 = (bf16[144,384]{1,0:T(8,128)(2,1)}, bf16[144,384]{1,0:T(8,128)(2,1)S(1)}, u32[]{:S(2)}, u32[]{:S(2)}) collective-permute-start(bf16[144,384]{1,0:T(8,128)(2,1)} %get-tuple-element.127.refs_0_), channel_id=1, source_target_pairs={{0,3},{1,2},{2,1},{3,0},{4,7},{5,6},{6,5},{7,4},{8,11},{9,10},{10,... | collective-permute-start | bytes 331784 | tf_op jit(solution)/shard_map/ppermute | solution.py:25
  138.6 17.5 %collective-permute-start.41 = (bf16[128,1024]{1,0:T(8,128)(2,1)}, bf16[128,1024]{1,0:T(8,128)(2,1)S(1)}, u32[]{:S(2)}, u32[]{:S(2)}) collective-permute-start(bf16[128,1024]{1,0:T(8,128)(2,1)} %get-tuple-element.132), channel_id=1, source_target_pairs={{0,8},{8,0},{16,24},{24,16},{1,9},{9,1},{17,25},{25,17},{2,10},{10... | collective-permute-start | bytes 786440 | tf_op jit(solution)/shard_map/ppermute | solution.py:25
  139.8 16.3 %collective-permute-start.42 = (bf16[128,1024]{1,0:T(8,128)(2,1)}, bf16[128,1024]{1,0:T(8,128)(2,1)S(1)}, u32[]{:S(2)}, u32[]{:S(2)}) collective-permute-start(bf16[128,1024]{1,0:T(8,128)(2,1)} %get-tuple-element.133), channel_id=1, source_target_pairs={{0,16},{8,24},{16,0},{24,8},{1,17},{9,25},{17,1},{25,9},{2,18},{10... | collective-permute-start | bytes 786440 | tf_op jit(solution)/shard_map/ppermute | solution.py:25
  141.1 15.1 %collective-permute-start.43 = (bf16[128,1024]{1,0:T(8,128)(2,1)}, bf16[128,1024]{1,0:T(8,128)(2,1)S(1)}, u32[]{:S(2)}, u32[]{:S(2)}) collective-permute-start(bf16[128,1024]{1,0:T(8,128)(2,1)} %get-tuple-element.134), channel_id=1, source_target_pairs={{0,24},{8,16},{16,8},{24,0},{1,25},{9,17},{17,9},{25,1},{2,26},{10... | collective-permute-start | bytes 786440 | tf_op jit(solution)/shard_map/ppermute | solution.py:25
  146.1 6.9 %collective-permute-start.38 = (bf16[144,384]{1,0:T(8,128)(2,1)S(1)}, bf16[144,384]{1,0:T(8,128)(2,1)S(1)}, u32[]{:S(2)}, u32[]{:S(2)}) collective-permute-start(bf16[144,384]{1,0:T(8,128)(2,1)S(1)} %copy-done.39), channel_id=1, source_target_pairs={{0,2},{1,3},{2,0},{3,1},{4,6},{5,7},{6,4},{7,5},{8,10},{9,11},{10,... | collective-permute-start | bytes 331784 | tf_op jit(solution)/shard_map/ppermute | solution.py:25
  (67 other events, 567.0 us)
where the time goes:
time: 159 us; the launch traced here: 158 us
  starting transfers between devices  60.8 us (38%)
  Pallas kernels  50 us (31%)
  waiting for transfers between devices  32.6 us (21%)
  local copies, waits for them, and re-layouts  12.2 us (8%)
  other arithmetic  1.67 us (1%)
    ppermute x44, starting transfers between devices, sent(): return lax.ppermute(block, axis, xor_route(lax.axis_size(axis), k))  55.5 us
    pallas_call x14, Pallas kernels, call(): pl.pallas_call(kernel, out_shape=[jax.ShapeDtypeStruct(shape, kind) for s...  50 us
    ppermute x44, waiting for transfers between devices, sent(): return lax.ppermute(block, axis, xor_route(lax.axis_size(axis), k))  28.6 us
    unnamed x107, local copies, waits for them, and re-layouts  9.69 us
    ppermute x4, starting transfers between devices, passed_along(): return lax.ppermute(block, axis, route)  5.33 us
    ppermute x4, waiting for transfers between devices, passed_along(): return lax.ppermute(block, axis, route)  3.95 us
  transfers between devices with their start and end apart: 48, of which 14 were waited for; matrix products, arithmetic and copies ran while one was open for 2% of the time, Pallas kernels for 23%

commit v1 on v0

--- a/solution.py
+++ b/solution.py
@@ -11,7 +11,6 @@
 epsilon = 1e-05
 f32 = jnp.float32
 bf16 = jnp.bfloat16
-exact = lax.Precision.HIGHEST
 LANES = 128
 HALO = 16
 EDGE = 8
@@ -39,10 +38,6 @@
     while len(parts) > 1:
         parts = [a + b for a, b in zip(parts[0::2], parts[1::2])]
     return parts[0]
-
-
-def f32_sum(parts):
-    return tree_sum([part.astype(f32) for part in parts])
 
 
 def passed_along(block, axis, distance):
@@ -105,28 +100,29 @@
     return jnp.broadcast_to(row, (LANES, row.shape[1])).T
 
 
-def per_head(values, pair_at, width):
-    first = values[:, 2 * pair_at : 2 * pair_at + 1]
-    second = values[:, 2 * pair_at + 1 : 2 * pair_at + 2]
-    lane = iota((values.shape[0], 2 * width), 1)
-    return jnp.where(lane < width, first, second)
+def terms(values, count):
+    parts = []
+    for _ in range(count):
+        parts.append(values.astype(bf16))
+        values = values - parts[-1].astype(f32)
+    return parts
 
 
 def spread(values, heads, width):
-    return jnp.concatenate([per_head(values, q, width) for q in range(heads // 2)], axis=1)
+    same = iota((LANES, heads * width), 1) // width == iota((LANES, heads * width), 0)
+    same = same.astype(bf16)
+    return sum(nn(part, same) for part in terms(values, 2))
 
 
 def gathered_heads(values, heads, width):
-    lane = iota((values.shape[0], LANES), 1)
-    wide = iota((values.shape[0], 2 * width), 1)
-    total = jnp.zeros((values.shape[0], LANES), f32)
-    for q in range(heads // 2):
-        both = values[:, 2 * width * q : 2 * width * (q + 1)]
-        first = jnp.sum(jnp.where(wide < width, both, 0.0), axis=1, keepdims=True)
-        second = jnp.sum(jnp.where(wide < width, 0.0, both), axis=1, keepdims=True)
-        total = jnp.where(lane == 2 * q, first, total)
-        total = jnp.where(lane == 2 * q + 1, second, total)
-    return total
+    same = iota((heads * width, LANES), 0) // width == iota((heads * width, LANES), 1)
+    same = same.astype(bf16)
+    return sum(nn(part, same) for part in terms(values, 2))
+
+
+def running(mask, values):
+    mask = mask.astype(bf16)
+    return sum(nn(mask, part) for part in terms(values, 3))
 
 
 def unit(pair, p, where):
@@ -148,9 +144,24 @@
         at += size
 
 
-def norm_kernel(pair, gain_lane, n_blocks, n_pieces, where, *refs):
-    blocks, pieces = refs[:n_blocks], refs[n_blocks : n_blocks + n_pieces]
-    normed, x_perm, inv_ref, gain_ref, edge_ref, hold = refs[n_blocks + n_pieces :]
+def pack_kernel(w_zx, w_bc, w_dt, gain, params, out, params_out):
+    shard, inner = w_zx.shape[0], w_zx.shape[2]
+    heads, wide_bc = w_dt.shape[0], w_bc.shape[1]
+    both = w_zx[...].astype(f32)
+    for j in range(2):
+        out[:, j * inner : (j + 1) * inner] = both[:, j, :].astype(bf16)
+    out[:, 2 * inner : 2 * inner + wide_bc] = w_bc[...]
+    row = iota((LANES - heads, shard), 0)
+    rest = jnp.where(row == 0, gain[...].astype(f32), 0.0)
+    tile = jnp.concatenate([w_dt[...].astype(f32), rest], axis=0).T
+    out[:, 2 * inner + wide_bc :] = tile.astype(bf16)
+    params_out[...] = jnp.zeros(params_out.shape, f32)
+    params_out[0:3, 0:heads] = params[...]
+
+
+def norm_kernel(pair, n_blocks, where, *refs):
+    blocks = refs[:n_blocks]
+    x_perm, inv_ref, edge_ref, hold = refs[n_blocks:]
     rows, part = blocks[0].shape
     swap = n_blocks * part // LANES // 2 if pair else 0
     total = jnp.zeros((rows, 1), f32)
@@ -160,38 +171,39 @@
         total += jnp.sum(value * value, axis=1, keepdims=True)
     inv = lax.rsqrt(total / (n_blocks * part) + epsilon)
     inv_ref[...] = jnp.broadcast_to(inv, inv_ref.shape)
-    eye = iota((LANES, LANES), 0) == iota((LANES, LANES), 1)
-    per_piece = pieces[0].shape[0] // LANES
     for p in range(n_blocks * part // LANES):
-        piece = pieces[p // per_piece]
-        at = p % per_piece * LANES
-        tile = piece.shape[1] - LANES
-        gain = piece[at : at + LANES, tile : tile + LANES][:, gain_lane : gain_lane + 1]
-        gain = jnp.sum(jnp.where(eye, gain.astype(f32), 0.0), axis=0, keepdims=True)
         block, lane = unit(pair, p, where)
-        value = hold[block, :, pl.ds(lane, LANES)]
-        cut = slice(p * LANES, (p + 1) * LANES)
-        value16 = (value * inv * gain).astype(bf16)
-        normed[:, cut] = value16
+        value = hold[block, :, pl.ds(lane, LANES)].astype(bf16)
+        x_perm[:, p * LANES : (p + 1) * LANES] = value
         there = p ^ swap
-        edge_ref[:, there * LANES : (there + 1) * LANES] = value16[rows - HALO :, :]
-        x_perm[:, cut] = value.astype(bf16)
-        gain_ref[:, cut] = gain
+        edge_ref[:, there * LANES : (there + 1) * LANES] = value[rows - HALO :, :]
 
 
 def forward_kernel(heads, n_pieces, *refs):
-    normed, edge, conv_x, conv_bc, params = refs[:5]
-    pieces = refs[5 : 5 + n_pieces]
+    x_perm, inv, edge, conv_x, conv_bc, params = refs[:6]
+    pieces = refs[6 : 6 + n_pieces]
     (z_ref, xe_ref, be_ref, ux_ref, ubc_ref, dt_ref, cum_ref, y_ref, state_ref, w_in) = refs[
-        5 + n_pieces : 15 + n_pieces
+        6 + n_pieces : 16 + n_pieces
     ]
-    rows_in, xe, be = refs[15 + n_pieces :]
+    normed, gain_ref, rows_in, xe, be = refs[16 + n_pieces :]
     rows, inner = ux_ref.shape
     width = inner // heads
     state_n = ubc_ref.shape[1] // 2
     taps = conv_x.shape[0] - 1
     assembled(w_in, pieces, 0)
-    rows_in[0:HALO, :] = edge[...]
+    tile = 2 * inner + 2 * state_n
+    eye = iota((LANES, LANES), 0) == iota((LANES, LANES), 1)
+    for p in range(w_in.shape[0] // LANES):
+        cut = slice(p * LANES, (p + 1) * LANES)
+        gain = w_in[cut, tile : tile + LANES][:, heads : heads + 1].astype(f32)
+        gain_ref[:, cut] = jnp.sum(jnp.where(eye, gain, 0.0), axis=0, keepdims=True)
+    gains = gain_ref[...]
+    normed[...] = (x_perm[...].astype(f32) * inv[:, 0:1] * gains).astype(bf16)
+    before = edge[...].astype(f32)
+    before_inv = lax.rsqrt(
+        jnp.sum(before * before, axis=1, keepdims=True) / before.shape[1] + epsilon
+    )
+    rows_in[0:HALO, :] = (before * before_inv * gains).astype(bf16)
     rows_in[HALO : HALO + rows, :] = normed[...]
     z_ref[...] = nn(normed[...], w_in[:, 0:inner]).astype(bf16)
     x_raw = nn(rows_in[...], w_in[:, inner : 2 * inner]).astype(bf16)
@@ -223,18 +235,13 @@
     lane = iota((rows, LANES), 1)
     step = jnp.where(lane < heads, softplus(dt + params[0:1, :]), 0.0)
     lower = iota((rows, rows), 0) >= iota((rows, rows), 1)
-    cum = lax.dot_general(
-        lower.astype(f32),
-        -step * jnp.exp(params[1:2, :]),
-        (((1,), (0,)), ((), ())),
-        precision=exact,
-        preferred_element_type=f32,
-    )
+    cum = running(lower, -step * jnp.exp(params[1:2, :]))
     cum_ref[...] = cum
     cum_t = cum.T
     gram = nt(c_mat, b_mat)
     scaled = x_act * spread(step, heads, width)
     scaled16 = scaled.astype(bf16)
+    skip = spread(params[...], heads, width)[2:3, :]
     pair_lane = iota((rows, 2 * width), 1)
     for q in range(heads // 2):
         cut = slice(2 * width * q, 2 * width * (q + 1))
@@ -243,38 +250,44 @@
             decay = jnp.exp(jnp.where(lower, cum[:, h : h + 1] - cum_t[h : h + 1, :], -jnp.inf))
             both.append(nn(decay * gram, scaled16[:, cut]))
         y_ref[:, cut] = (
-            jnp.where(pair_lane < width, both[0], both[1])
-            + x_act[:, cut] * per_head(jnp.broadcast_to(params[2:3, :], (rows, LANES)), q, width)
+            jnp.where(pair_lane < width, both[0], both[1]) + x_act[:, cut] * skip[:, cut]
         )
     to_end = jnp.exp(cum[rows - 1 : rows, :] - cum)
     state_ref[...] = tn(scaled * spread(to_end, heads, width), b_mat)
 
 
-def gate_kernel(pair, heads, n_blocks, n_pieces, where, *refs):
-    state, ubc, cum, y_loc, z, gain = refs[:6]
-    blocks = refs[6 : 6 + n_blocks]
-    pieces = refs[6 + n_blocks : 6 + n_blocks + n_pieces]
-    y_ref, go_ref, raw_ref, stats_ref, cot_ref, w_ref, hold = refs[6 + n_blocks + n_pieces :]
+def cot_kernel(pair, n_blocks, n_pieces, where, *refs):
+    normed = refs[0]
+    blocks = refs[1 : 1 + n_blocks]
+    pieces = refs[1 + n_blocks : 1 + n_blocks + n_pieces]
+    go_ref, w_ref, normed_t, cot_t, hold, cot = refs[1 + n_blocks + n_pieces :]
+    assembled(w_ref, pieces, 1)
+    for k, block in enumerate(blocks):
+        hold[k] = block[...].astype(f32)
+    for p in range(cot.shape[1] // LANES):
+        block, lane = unit(pair, p, where)
+        cut = slice(p * LANES, (p + 1) * LANES)
+        value = hold[block, :, pl.ds(lane, LANES)]
+        cot[:, cut] = value.astype(bf16)
+        cot_t[cut, :] = value.T.astype(bf16)
+        normed_t[cut, :] = normed[:, cut].astype(f32).T.astype(bf16)
+    go_ref[...] = nt(cot[...], w_ref[...])
+
+
+def gate_kernel(heads, state, ubc, cum, y_loc, z, gain, go, y_ref, raw_ref, stats_ref):
     rows, inner = y_ref.shape
     width = inner // heads
     state_n = ubc.shape[1] // 2
-    assembled(w_ref, pieces, 1)
-    for k, block in enumerate(blocks):
-        hold[k] = block[...].astype(f32)
-    for p in range(cot_ref.shape[1] // LANES):
-        block, lane = unit(pair, p, where)
-        cot_ref[:, p * LANES : (p + 1) * LANES] = hold[block, :, pl.ds(lane, LANES)].astype(bf16)
     u_c = ubc[:, state_n:]
     c_mat = u_c * sigmoid(u_c)
     y = y_loc[...] + nt(c_mat, state[...]) * spread(jnp.exp(cum[...]), heads, width)
     y_ref[...] = y
     z_val = z[...].astype(f32)
     gated = y * z_val * sigmoid(z_val)
-    raw_ref[...] = (gated * gain[...]).astype(bf16)
-    grad_o = nt(cot_ref[...], w_ref[...])
-    go_ref[...] = grad_o
+    raw = gated * gain[...]
+    raw_ref[...] = raw.astype(bf16)
     squares = jnp.sum(gated * gated, axis=1, keepdims=True)
-    cross = jnp.sum(grad_o * gain[...] * gated, axis=1, keepdims=True)
+    cross = jnp.sum(go[...] * raw, axis=1, keepdims=True)
     lane = iota((rows, LANES), 1)
     both = jnp.where(lane == 0, squares, jnp.where(lane == 1, cross, 0.0))
     stats_ref[...] = both.T[0:8, :]
@@ -293,7 +306,7 @@
 def gate_back_kernel(heads, full_inner, n_stats, *refs):
     stats = refs[:n_stats]
     go, y, z, gain, ubc, cum = refs[n_stats : n_stats + 6]
-    dy_ref, dz_ref, state_ref, inv_ref, ggain_ref = refs[n_stats + 6 :]
+    dy_ref, dz_ref, state_ref, inv_ref, ggain_ref, gated_ref = refs[n_stats + 6 :]
     rows, inner = y.shape
     width = inner // heads
     state_n = ubc.shape[1] // 2
@@ -308,7 +321,9 @@
     y_val = y[...]
     gated = y_val * silu
     grad_o = go[...]
-    ggain_ref[...] = jnp.sum(grad_o * gated * inv, axis=0, keepdims=True)
+    unit_gated = gated * inv
+    gated_ref[...] = (unit_gated * gain[...]).astype(bf16)
+    ggain_ref[...] = jnp.sum(grad_o * unit_gated, axis=0, keepdims=True)
     grad_gin = inv * grad_o * gain[...] - gated * coef
     dy = grad_gin * silu
     dy_ref[...] = dy
@@ -319,7 +334,7 @@
 
 
 def inner_back_kernel(
-    heads, dy_ref, dz, cum_ref, dt, params, ux, ubc, state, raw, cot, inv, normed,
+    heads, dy_ref, dz, cum_ref, dt, params, ux, ubc, state, gated, cot_t, normed_t,
     dxs_ref, dbc_ref, dcum_ref, own_ref, other_ref,
 ):
     rows, inner = dy_ref.shape
@@ -363,11 +378,10 @@
     dcum_ref[...] = dcum - dcum_t.T + gathered_heads(dy * cross, heads, width)
     dbc_ref[:, 0:state_n] = tn(grad_gram, c_mat)
     dbc_ref[:, state_n:] = nn(dy * exp_cum, state[...]) + nn(grad_gram, b_mat)
-    weighted = (cot[...].astype(f32) * inv[:, 0:1]).astype(bf16)
     half = own_ref.shape[0]
     for ref, cut in ((own_ref, slice(0, half)), (other_ref, slice(half, 2 * half))):
-        ref[:, 0:inner] = tn(normed[:, cut], dz[...]).astype(bf16)
-        ref[:, inner:] = tn(weighted[:, cut], raw[...]).astype(bf16)
+        ref[:, 0:inner] = nn(normed_t[cut, :], dz[...]).astype(bf16)
+        ref[:, inner:] = nn(cot_t[cut, :], gated[...]).astype(bf16)
 
 
 def ssd_back_kernel(
@@ -402,24 +416,19 @@
     held = jnp.sum(jnp.where(head_of, held, 0.0), axis=0, keepdims=True)
     last = jnp.sum(end_term, axis=0, keepdims=True) + jnp.exp(cum[rows - 1 : rows, :]) * held
     upper = iota((rows, rows), 0) <= iota((rows, rows), 1)
-    grad_log = last + lax.dot_general(
-        upper.astype(f32),
-        dcum_ref[...] - end_term,
-        (((1,), (0,)), ((), ())),
-        precision=exact,
-        preferred_element_type=f32,
-    )
+    grad_log = last + running(upper, dcum_ref[...] - end_term)
     grad_step = gathered_heads(grad_scaled * x_act, heads, width) + grad_log * rate
     grad_raw = jnp.where(lane < heads, grad_step * sigmoid(shifted), 0.0)
     raw_ref[...] = grad_raw.astype(bf16)
     row = iota((8, LANES), 0)
     bias_grad = jnp.sum(grad_raw, axis=0, keepdims=True)
     rate_grad = jnp.sum(grad_log * step, axis=0, keepdims=True) * rate
-    skip_grad = jnp.sum(gathered_heads(dy * x_act, heads, width), axis=0, keepdims=True)
+    skip_rows = jnp.broadcast_to(jnp.sum(dy * x_act, axis=0, keepdims=True), (8, inner))
+    skip_grad = gathered_heads(skip_rows, heads, width)[0:1, :]
     ghead_ref[...] = jnp.where(
         row == 0, bias_grad, jnp.where(row == 1, rate_grad, jnp.where(row == 2, skip_grad, 0.0))
     )
-    skip = spread(jnp.broadcast_to(params[2:3, :], (rows, LANES)), heads, width)
+    skip = spread(params[...], heads, width)[2:3, :]
     gux = (grad_scaled * step_wide + dy * skip) * (sig_x * (1.0 + u_x * (1.0 - sig_x)))
     gux_ref[...] = gux
     slope = sig_bc * (1.0 + u_bc * (1.0 - sig_bc))
@@ -430,11 +439,11 @@
 
 
 def last_kernel(pair, gain_lane, n_blocks, where, *refs):
-    edge, gux, gubc, xe, be, dz, raw, normed, x_perm, inv, gain, conv_x, conv_bc, w_in = refs[:14]
+    edge, gux, gubc, xe, be, dz, raw, normed_t, x_perm, inv, gain, conv_x, conv_bc, w_in = refs[:14]
     ggain, ghead = refs[14:16]
     blocks = refs[16 : 16 + n_blocks]
     gx_own, gx_other, gb_own, gb_other = refs[16 + n_blocks : 20 + n_blocks]
-    hold, gx_ext, gb_ext, x_ext, b_ext, small = refs[20 + n_blocks :]
+    hold, gx_ext, gb_ext, x_ext, b_ext, small, grads = refs[20 + n_blocks :]
     rows, inner = gux.shape
     wide_bc = gubc.shape[1]
     taps = conv_x.shape[0] - 1
@@ -465,12 +474,11 @@
     for j in range(2):
         small[3 * n + j : 3 * n + j + 1, 0:wide_bc] = ggain[:, j * wide_bc : (j + 1) * wide_bc]
     small[3 * n + 2 : 3 * n + 5, 0:LANES] = ghead[0:3, :]
-    dbcd = jnp.concatenate([dbc, raw[...]], axis=1)
-    part = (
-        nt(dz[...], w_in[:, 0:inner])
-        + nt(dx, w_in[:, inner : 2 * inner])
-        + nt(dbcd, w_in[:, 2 * inner :])
-    )
+    grads[:, 0:inner] = dz[...]
+    grads[:, inner : 2 * inner] = dx
+    grads[:, 2 * inner : 2 * inner + wide_bc] = dbc
+    grads[:, 2 * inner + wide_bc :] = raw[...]
+    part = nt(grads[...], w_in[...])
     for p in range(part.shape[1] // LANES):
         block, lane = unit(pair, p, where)
         hold[block, :, pl.ds(lane, LANES)] = part[:, p * LANES : (p + 1) * LANES].astype(bf16)
@@ -487,13 +495,15 @@
     high = small[...].astype(bf16)
     low = (small[...] - high.astype(f32)).astype(bf16)
     count = small.shape[0]
-    for cut, gx_ref, gb_ref in (
-        (slice(0, half), gx_own, gb_own),
-        (slice(half, 2 * half), gx_other, gb_other),
-    ):
-        gx_ref[...] = tn(normed[:, cut], dx).astype(bf16)
-        g_bcd = tn(normed[:, cut], dbcd)
-        g_gain = tn(along[:, cut], jnp.ones((rows, LANES), bf16))
+    gain_sum = jnp.sum(along, axis=0, keepdims=True)
+    for first, gx_ref, gb_ref in ((0, gx_own, gb_own), (half, gx_other, gb_other)):
+        cut = slice(first, first + half)
+        g_both = nn(normed_t[cut, :], grads[:, inner:])
+        gx_ref[...] = g_both[:, 0:inner].astype(bf16)
+        g_bcd = g_both[:, inner:]
+        g_gain = jnp.concatenate(
+            [column_of(gain_sum[:, j : j + LANES]) for j in range(first, first + half, LANES)], axis=0
+        )
         gb_ref[0:half, 0:wide_bc] = g_bcd[:, 0:wide_bc].astype(bf16)
         gb_ref[0:half, wide_bc:] = jnp.where(at, g_gain, g_bcd[:, wide_bc:]).astype(bf16)
         gb_ref[half : half + count, :] = high
@@ -521,10 +531,10 @@
     gdt_ref, cx_ref, ghead_ref, ggain_ref, shared_ref = refs[n_blocks:]
     total = tree_sum([b[...].astype(f32) for b in refs[:n_blocks]])
     wide_bc = cx_ref.shape[1] // 2
-    n, size = taps + 1, gdt_ref.shape[0]
+    n, size = taps + 1, gdt_ref.shape[1]
     half = (total.shape[0] - size) // 2
     small = total[size : size + half] + total[size + half :]
-    gdt_ref[...] = total[0:size, wide_bc : wide_bc + heads]
+    gdt_ref[...] = total[0:size, wide_bc:].T[0:heads, :]
     for j in range(2):
         cut = slice(j * wide_bc, (j + 1) * wide_bc)
         cx_ref[:, cut] = small[j * n : (j + 1) * n, 0:wide_bc]
@@ -546,10 +556,17 @@
     ngain_ref[...] = row_of(total[0:size, wide_bc:][:, gain_lane : gain_lane + 1])
 
 
-def input_kernel(pair, full_d, n_blocks, where, *refs):
-    blocks = refs[:n_blocks]
-    x_local, cot, inv, gain, out_ref, out = refs[n_blocks:]
+def input_kernel(pair, full_d, n_blocks, n_grads, where, *refs):
+    blocks, outs = refs[:n_blocks], refs[n_blocks : 2 * n_blocks]
+    early, late = (refs[(2 * n_blocks + j * n_grads) :][:n_grads] for j in range(2))
+    rest = refs[2 * n_blocks + 2 * n_grads :]
+    x_local, cot, inv, gain, inv_gate = rest[:5]
+    gains = rest[-1]
+    output_ref, grad_ref = rest[5:7]
     rows, _ = x_local.shape
+    total = tree_sum([b[...].astype(f32) for b in outs])
+    x_val = x_local[...].astype(f32)
+    output_ref[...] = (x_val + total * inv_gate[:, 0:1]).astype(bf16)
     total = tree_sum([b[...].astype(f32) for b in blocks])
     dots = column_of((total[rows : rows + 1, :] + total[rows + 1 : rows + 2, :]) / full_d)[:, 0:1]
     scale = inv[:, 0:1]
@@ -558,14 +575,19 @@
 
         @pl.when(block == 0)
         def _():
-            cut = pl.ds(lane, LANES)
-            xhat = x_local[:, cut].astype(f32) * scale
-            out[:, cut] = gain[:, p * LANES : (p + 1) * LANES] + 0.0 * xhat
-
-    gains = out[...]
-    xhat = x_local[...].astype(f32) * scale
-    grad = cot[...].astype(f32) + scale * (total[0:rows, :] * gains - xhat * dots)
-    out_ref[...] = grad.astype(bf16)
+            gains[:, pl.ds(lane, LANES)] = jnp.broadcast_to(
+                gain[:, p * LANES : (p + 1) * LANES], (8, LANES)
+            )
+
+    grad = scale * (total[0:rows, :] * gains[0:1, :] - x_val * (scale * dots))
+    grad_ref[...] = (cot[...].astype(f32) + grad).astype(bf16)
+    if n_grads > 0:
+        gzx_ref, gout_ref = rest[7:9]
+        inner = gzx_ref.shape[2]
+        total = tree_sum([b[...].astype(f32) for b in early])
+        gzx_ref[:, 0, :] = total[:, 0:inner]
+        gzx_ref[:, 1, :] = tree_sum([b[...].astype(f32) for b in late])
+        gout_ref[...] = total[:, inner:].T
 
 
 VMEM = pl.BlockSpec(memory_space=pltpu.VMEM)
@@ -608,11 +630,15 @@
 
     def reduced(own, other, extra=0):
         recv = sent(other, "seq", 1)
-        blocks = call(
-            functools.partial(fold_kernel, dp_n),
-            [((shard + extra, own.shape[1]), bf16)] * dp_n,
-            [own, recv],
-        )
+        if extra == 0:
+            both = (own.astype(f32) + recv.astype(f32)).astype(bf16)
+            blocks = [both[k * shard : (k + 1) * shard] for k in range(dp_n)]
+        else:
+            blocks = call(
+                functools.partial(fold_kernel, dp_n),
+                [((shard + extra, own.shape[1]), bf16)] * dp_n,
+                [own, recv],
+            )
         return scattered(blocks, "dp")
 
     def reduced_apart(own, other):
@@ -621,32 +647,34 @@
 
     x_local = hidden_in[0, 0]
     cot_local = cotangent[0, 0]
-    pad = jnp.zeros((shard, LANES - heads - 1), bf16)
-    packed = [w_zx.reshape(shard, 2 * inner), w_bc, w_dt, norm_gain[:, None], pad]
-    pieces = gathered(jnp.concatenate(packed, axis=1), 0)
+    wide_bcd = wide_bc + LANES
+    if pair:
+        packed, params = call(
+            pack_kernel,
+            [((shard, 2 * inner + wide_bcd), bf16), ((8, LANES), f32)],
+            [w_zx, w_bc, w_dt.T, norm_gain[None], head_params],
+        )
+    else:
+        pad = jnp.zeros((shard, LANES - heads - 1), bf16)
+        packed = [w_zx.reshape(shard, 2 * inner), w_bc, w_dt, norm_gain[:, None], pad]
+        packed = jnp.concatenate(packed, axis=1)
+        params = jnp.pad(head_params, ((0, 5), (0, LANES - heads)))
+    pieces = gathered(packed, 0)
     x_blocks = exchanged(x_local, "head")
     out_pieces = gathered(w_out, 1)
     cot_blocks = exchanged(cot_local, "head")
-    params = jnp.pad(head_params, ((0, 5), (0, LANES - heads)))
     gain_row = gate_gain[None]
     n_in, n_out = len(pieces), len(out_pieces)
-    wide_bcd = wide_bc + LANES
-
-    normed, x_perm, inv_in, norm_row, edge = call(
-        functools.partial(norm_kernel, pair, heads, head_n, n_in),
-        [
-            ((rows, full_d), bf16),
-            ((rows, full_d), bf16),
-            ((rows, LANES), f32),
-            ((1, full_d), f32),
-            ((HALO, full_d), bf16),
-        ],
-        [where, *x_blocks, *pieces],
+
+    x_perm, inv_in, edge = call(
+        functools.partial(norm_kernel, pair, head_n),
+        [((rows, full_d), bf16), ((rows, LANES), f32), ((HALO, full_d), bf16)],
+        [where, *x_blocks],
         [((head_n, rows, part_d), f32)],
         1,
     )
     edge = passed_along(edge, "seq", 1)
-    z, x_ext, bc_ext, u_x, u_bc, dt, cum, y_loc, own_state, w_in = call(
+    z, x_ext, bc_ext, u_x, u_bc, dt, cum, y_loc, own_state, w_in, normed, norm_row = call(
         functools.partial(forward_kernel, heads, n_in),
         [
             ((rows, inner), bf16),
@@ -659,8 +687,10 @@
             ((rows, inner), f32),
             ((inner, state_n), f32),
             ((full_d, 2 * inner + wide_bcd), bf16),
+            ((rows, full_d), bf16),
+            ((1, full_d), f32),
         ],
-        [normed, edge, conv_x, conv_bc, params, *pieces],
+        [x_perm, inv_in, edge, conv_x, conv_bc, params, *pieces],
         [
             ((HALO + rows, full_d), bf16),
             ((HALO + rows, inner), f32),
@@ -669,19 +699,22 @@
     )
     total_decay = jnp.repeat(jnp.exp(cum[rows - 1, :heads]), inner // heads)[:, None]
     state_in = entering(total_decay, own_state, "seq", False)
-    y, grad_o, gated_raw, stats, cot_perm, w_out_full = call(
-        functools.partial(gate_kernel, pair, heads, head_n, n_out),
+    grad_o, w_out_full, normed_t, cot_t = call(
+        functools.partial(cot_kernel, pair, head_n, n_out),
         [
             ((rows, inner), f32),
-            ((rows, inner), f32),
-            ((rows, inner), bf16),
-            ((8, rows), f32),
-            ((rows, full_d), bf16),
             ((inner, full_d), bf16),
+            ((full_d, rows), bf16),
+            ((full_d, rows), bf16),
         ],
-        [where, state_in, u_bc, cum, y_loc, z, gain_row, *cot_blocks, *out_pieces],
-        [((head_n, rows, part_d), f32)],
+        [where, normed, *cot_blocks, *out_pieces],
+        [((head_n, rows, part_d), f32), ((rows, full_d), bf16)],
         1,
+    )
+    y, gated_raw, stats = call(
+        functools.partial(gate_kernel, heads),
+        [((rows, inner), f32), ((rows, inner), bf16), ((8, rows), f32)],
+        [state_in, u_bc, cum, y_loc, z, gain_row, grad_o],
     )
     stats = exchanged(stats, "head")
     out_blocks = call(
@@ -691,9 +724,9 @@
         [((head_n, rows, part_d), bf16)],
         1,
     )
-    out_sum = f32_sum(scattered(out_blocks, "head"))
-
-    dy, dz, from_cross, inv_gate, g_ggain = call(
+    out_parts = scattered(out_blocks, "head")
+
+    dy, dz, from_cross, inv_gate, g_ggain, gated = call(
         functools.partial(gate_back_kernel, heads, full_inner, head_n),
         [
             ((rows, inner), f32),
@@ -701,10 +734,10 @@
             ((inner, state_n), f32),
             ((rows, LANES), f32),
             ((1, inner), f32),
+            ((rows, inner), bf16),
         ],
         [*stats, grad_o, y, z, gain_row, u_bc, cum],
     )
-    output = (x_local.astype(f32) + out_sum * inv_gate[:, :1]).astype(bf16)
     grad_next = entering(total_decay, from_cross, "seq", True)
     dxs, dbc, dcum, early_own, early_other = call(
         functools.partial(inner_back_kernel, heads),
@@ -715,7 +748,7 @@
             ((full_d // 2, 2 * inner), bf16),
             ((full_d // 2, 2 * inner), bf16),
         ],
-        [dy, dz, cum, dt, params, u_x, u_bc, state_in, gated_raw, cot_perm, inv_gate, normed],
+        [dy, dz, cum, dt, params, u_x, u_bc, state_in, gated, cot_t, normed_t],
     )
     gux, gubc, edge_out, raw16, g_head = call(
         functools.partial(ssd_back_kernel, heads),
@@ -737,7 +770,7 @@
         + [((full_d // 2, inner), bf16)] * 2
         + [((full_d // 2 + 2 * count, wide_bcd), bf16)] * 2,
         [
-            where, edge_next, gux, gubc, x_ext, bc_ext, dz, raw16, normed, x_perm, inv_in, norm_row,
+            where, edge_next, gux, gubc, x_ext, bc_ext, dz, raw16, normed_t, x_perm, inv_in, norm_row,
             conv_x, conv_bc, w_in, g_ggain, g_head,
         ],
         [
@@ -747,18 +780,19 @@
             ((HALO + rows, inner), f32),
             ((HALO + rows, wide_bc), f32),
             ((count, wide_bcd), f32),
+            ((rows, 2 * inner + wide_bcd), bf16),
         ],
         1,
     )
     blocks, (gx_own, gx_other, gb_own, gb_other) = results[:head_n], results[head_n:]
     if pair:
-        early = f32_sum(reduced(early_own, early_other))
+        early = reduced(early_own, early_other)
         g_bcd = reduced(gb_own, gb_other, 2 * count)
-        g_x = f32_sum(reduced(gx_own, gx_other))
+        g_x = reduced(gx_own, gx_other)
         g_dt, g_cx, g_head, g_ggain, shared = call(
             functools.partial(small_kernel, taps, heads, dp_n),
             [
-                ((shard, heads), f32),
+                ((heads, shard), f32),
                 ((n, inner), f32),
                 ((3, heads), f32),
                 ((1, inner), f32),
@@ -766,6 +800,7 @@
             ],
             g_bcd,
         )
+        g_dt = g_dt.T
     else:
         early = reduced_apart(early_own, early_other)
         g_bcd = reduced_apart(gb_own, gb_other)
@@ -780,11 +815,15 @@
         g_head = small[3 * n + 2 : 3 * n + 5, :heads]
         shared = jnp.concatenate([g_bcd, small[2 * n : 3 * n]], axis=0)
     parts = scattered(blocks, "head")
-    (grad_input,) = call(
-        functools.partial(input_kernel, pair, full_d, head_n),
-        [((rows, part_d), bf16)],
-        [where, *parts, x_local, cot_local, inv_in, norm_row],
-        [((rows, part_d), f32)],
+    grads = [((shard, 2, inner), f32), ((inner, shard), f32)] if pair else []
+    output, grad_input, *grads = call(
+        functools.partial(input_kernel, pair, full_d, head_n, dp_n if pair else 0),
+        [((rows, part_d), bf16), ((rows, part_d), bf16), *grads],
+        [
+            where, *parts, *out_parts, *(early if pair else []), *(g_x if pair else []),
+            x_local, cot_local, inv_in, norm_row, inv_gate,
+        ],
+        [((8, part_d), f32)],
         1,
     )
     shared = exchanged(shared, "head")
@@ -795,11 +834,13 @@
             shared,
         )
         g_ngain = g_ngain.reshape(shard)
+        g_zx, g_out = grads
     else:
         shared = tree_sum(shared)
         g_bc, g_cbc = shared[:shard, :wide_bc], shared[shard:, :wide_bc]
         g_ngain = shared[:shard, wide_bc + heads]
-    g_zx = jnp.stack([early[:, :inner], g_x], axis=1)
+        g_zx = jnp.stack([early[:, :inner], g_x], axis=1)
+        g_out = early[:, inner:].T
     return (
         output[None, None],
         grad_input[None, None],
@@ -807,7 +848,7 @@
         g_zx,
         g_bc,
         g_dt,
-        early[:, inner:].T,
+        g_out,
         g_cx,
         g_cbc,
         g_head,

time: 159 us -> 151 us (0.950)
  local copies, waits for them, and re-layouts: 12.2 us -> 6.14 us
    unnamed x107 -> x96, local copies, waits for them, and re-layouts: 9.69 us -> 4.66 us
    ppermute x4, waiting for transfers between devices: 3.95 us -> 1.87 us  [passed_along(): return lax.ppermute(block, axis, route)]
    ppermute x44, waiting for transfers between devices: 28.6 us -> 30.4 us  [sent(): return lax.ppermute(block, axis, xor_route(lax.axis_size(axis), k))]
  transfers between devices with their start and end apart: 48 -> 48, of which waited for: 14 -> 23; matrix products, arithmetic and copies ran while one was open for 2% -> 2% of each run, Pallas kernels for 23% -> 21%
where the time goes in v1:
time: 151 us
  starting transfers between devices  61.1 us (40%)
  Pallas kernels  48.6 us (32%)
  waiting for transfers between devices  32.3 us (21%)
  local copies, waits for them, and re-layouts  6.14 us (4%)
    ppermute x44, starting transfers between devices, sent(): return lax.ppermute(block, axis, xor_route(lax.axis_size(axis), k))  55.8 us
    pallas_call x14, Pallas kernels, call(): pl.pallas_call(kernel, out_shape=[jax.ShapeDtypeStruct(shape, kind) for s...  48.6 us
    ppermute x44, waiting for transfers between devices, sent(): return lax.ppermute(block, axis, xor_route(lax.axis_size(axis), k))  30.4 us
    ppermute x4, starting transfers between devices, passed_along(): return lax.ppermute(block, axis, route)  5.33 us
    unnamed x96, local copies, waits for them, and re-layouts  4.66 us
  transfers between devices with their start and end apart: 48, of which 23 were waited for; matrix products, arithmetic and copies ran while one was open for 2% of the time, Pallas kernels for 21%

profile of v1, /device:TPU:0, one launch (start us, length us, event | category | flops | bytes accessed | tf_op | source)
XLA Modules:
  0.0 150.5 jit_solution(4846198838453802474)
XLA Ops:
  0.6 2.7 %shard_map.195 = (bf16[128,1408]{1,0:T(8,128)(2,1)}, f32[8,128]{1,0:T(8,128)}) custom-call(bf16[128,2,512]{2,1,0:T(2,128)(2,1)} %w_zx.1, bf16[128,256]{1,0:T(8,128)(2,1)} %w_bc.1, bf16[8,128]{1,0:T(8,128)(2,1)} %bitcast.24, bf16[1,128]{1,0:T(2,128)(2,1)} %bitcast.25, f32[3,8]{1,0:T(4,128)} %params.1), custom_call_target="tpu_custom_call" | custom-call | tf_op jit(solution)/shard_map/pallas_call | solution.py:598
  3.3 3.9 %collective-permute-start.6 = (bf16[128,1408]{1,0:T(8,128)(2,1)}, bf16[128,1408]{1,0:T(8,128)(2,1)S(1)}, u32[]{:S(2)}, u32[]{:S(2)}) collective-permute-start(bf16[128,1408]{1,0:T(8,128)(2,1)} %get-tuple-element.83.refs_6_), channel_id=1, source_target_pairs={{0,24},{8,16},{16,8},{24,0},{1,25},{9,17},{17,9},{25,1},{2,26},{10... | collective-permute-start | bytes 1081352 | tf_op jit(solution)/shard_map/ppermute | solution.py:24
  7.9 4.0 %collective-permute-start.2 = (bf16[256,256]{1,0:T(8,128)(2,1)}, bf16[256,256]{1,0:T(8,128)(2,1)S(1)}, u32[]{:S(2)}, u32[]{:S(2)}) collective-permute-start(bf16[256,256]{1,0:T(8,128)(2,1)} %bitcast.12), channel_id=1, source_target_pairs={{0,3},{1,2},{2,1},{3,0},{4,7},{5,6},{6,5},{7,4},{8,11},{9,10},{10,... | collective-permute-start | bytes 393224 | tf_op jit(solution)/shard_map/ppermute | solution.py:24
  11.9 4.4 %collective-permute-done.2.refs_3_ = bf16[256,256]{1,0:T(8,128)(2,1)S(1)} collective-permute-done((bf16[256,256]{1,0:T(8,128)(2,1)}, bf16[256,256]{1,0:T(8,128)(2,1)S(1)}, u32[]{:S(2)}, u32[]{:S(2)}) %collective-permute-start.2) | collective-permute-done | bytes 131104 | tf_op jit(solution)/shard_map/ppermute | solution.py:24
  16.2 4.8 %collective-permute-start = (bf16[256,256]{1,0:T(8,128)(2,1)}, bf16[256,256]{1,0:T(8,128)(2,1)S(1)}, u32[]{:S(2)}, u32[]{:S(2)}) collective-permute-start(bf16[256,256]{1,0:T(8,128)(2,1)} %bitcast.14), channel_id=1, source_target_pairs={{0,1},{1,0},{2,3},{3,2},{4,5},{5,4},{6,7},{7,6},{8,9},{9,8},{10,11... | collective-permute-start | bytes 393224 | tf_op jit(solution)/shard_map/ppermute | solution.py:24
  25.1 2.8 %collective-permute-start.14 = (bf16[256,256]{1,0:T(8,128)(2,1)}, bf16[256,256]{1,0:T(8,128)(2,1)S(1)}, u32[]{:S(2)}, u32[]{:S(2)}) collective-permute-start(bf16[256,256]{1,0:T(8,128)(2,1)} %bitcast.17), channel_id=1, source_target_pairs={{0,3},{1,2},{2,1},{3,0},{4,7},{5,6},{6,5},{7,4},{8,11},{9,10},{10,... | collective-permute-start | bytes 393224 | tf_op jit(solution)/shard_map/ppermute | solution.py:24
  28.6 2.2 %shard_map.194 = (bf16[256,1024]{1,0:T(8,128)(2,1)}, f32[256,128]{1,0:T(8,128)}, bf16[16,1024]{1,0:T(8,128)(2,1)}) custom-call(s32[2]{0:T(128)} %pad_add_fusion.where, bf16[256,256]{1,0:T(8,128)(2,1)} %bitcast.15, bf16[256,256]{1,0:T(8,128)(2,1)} %copy-done.29, bf16[256,256]{1,0:T(8,128)(2,1)} %copy-done.28, bf16[256,256]{1,0:T(8,128)(2,1)} %copy-done.27), custom_call_target="tpu_custom_call" | custom-call | tf_op jit(solution)/shard_map/pallas_call | solution.py:598
  34.5 3.5 %collective-permute-start.13 = (bf16[256,256]{1,0:T(8,128)(2,1)}, bf16[256,256]{1,0:T(8,128)(2,1)S(1)}, u32[]{:S(2)}, u32[]{:S(2)}) collective-permute-start(bf16[256,256]{1,0:T(8,128)(2,1)} %bitcast.18), channel_id=1, source_target_pairs={{0,2},{1,3},{2,0},{3,1},{4,6},{5,7},{6,4},{7,5},{8,10},{9,11},{10,... | collective-permute-start | bytes 393224 | tf_op jit(solution)/shard_map/ppermute | solution.py:24
  38.4 1.7 %collective-permute-start.17 = (bf16[512,128]{1,0:T(8,128)(2,1)}, bf16[512,128]{1,0:T(8,128)(2,1)S(1)}, u32[]{:S(2)}, u32[]{:S(2)}) collective-permute-start(bf16[512,128]{1,0:T(8,128)(2,1)} %refs_5_.1), channel_id=1, source_target_pairs={{0,24},{8,16},{16,8},{24,0},{1,25},{9,17},{17,9},{25,1},{2,26},{10... | collective-permute-start | bytes 393224 | tf_op jit(solution)/shard_map/ppermute | solution.py:24
  42.1 6.0 %shard_map.196 = (bf16[256,512]{1,0:T(8,128)(2,1)}, bf16[272,512]{1,0:T(8,128)(2,1)}, bf16[272,256]{1,0:T(8,128)(2,1)}, f32[256,512]{1,0:T(8,128)}, f32[256,256]...) custom-call(bf16[256,1024]{1,0:T(8,128)(2,1)} %get-tuple-element.79., ...), custom_call_target="tpu_custom_call" | custom-call | tf_op jit(solution)/shard_map/pallas_call | solution.py:598
  52.3 3.7 %shard_map.197 = (f32[256,512]{1,0:T(8,128)}, bf16[512,1024]{1,0:T(8,128)(2,1)}, bf16[1024,256]{1,0:T(8,128)(2,1)}, bf16[1024,256]{1,0:T(8,128)(2,1)}) custom-call(s32[2]{0:T(128)} %pad_add_fusion.where, bf16[256,1024]{1,0:T(8,128)(2,1)} %get-tuple-element.89.refs_0_, bf16[256,256]{1,0:T(8,128)(2,1)} %bitcast.20, bf16[256,256]{1,0:T(8,128)(2,1)} %copy-done.23, ...), custom_call_target="tpu_custom_call" | custom-call | tf_op jit(solution)/shard_map/pallas_call | solution.py:598
  56.7 2.9 %shard_map.198 = (f32[256,512]{1,0:T(8,128)}, bf16[256,512]{1,0:T(8,128)(2,1)}, f32[8,256]{1,0:T(8,128)}) custom-call(f32[512,128]{1,0:T(8,128)} %copy-done, f32[256,256]{1,0:T(8,128)} %get-tuple-element.85.ubc.refs_8_, f32[256,128]{1,0:T(8,128)} %get-tuple-element.86.cum.refs_9_.cum_ref, f32[256,512]{1,0:T(8,128)} %get-tuple-element.87.y_loc, ...), custom_call_target="tpu_custom_call" | custom-call | tf_op jit(solution)/shard_map/pallas_call | solution.py:598
  60.8 1.8 %collective-permute-start.23 = (f32[8,256]{1,0:T(8,128)}, f32[8,256]{1,0:T(8,128)S(1)}, u32[]{:S(2)}, u32[]{:S(2)}) collective-permute-start(f32[8,256]{1,0:T(8,128)} %get-tuple-element.91.refs_0_), channel_id=1, source_target_pairs={{0,2},{1,3},{2,0},{3,1},{4,6},{5,7},{6,4},{7,5},{8,10},{9,11},{10,... | collective-permute-start | bytes 24584 | tf_op jit(solution)/shard_map/ppermute | solution.py:24
  67.1 3.2 %shard_map.199 = (f32[256,512]{1,0:T(8,128)}, bf16[256,512]{1,0:T(8,128)(2,1)}, f32[512,128]{1,0:T(8,128)}, f32[256,128]{1,0:T(8,128)}, f32[1,512]{1,0:T(1,128)}, /*index=5*/bf16[256,512]{1,0:T(8,128)(2,1)}) custom-call(f32[8,256]{1,0:T(8,128)} %get-tuple-element.91.refs_0_, f32[8,256]{1,0:T(8,128)} %copy-done.47, f32[8,256]{1,0:T(8,128)} %copy-done.46, ...), custom_call_target="tpu_custom_call" | custom-call | tf_op jit(solution)/shard_map/pallas_call | solution.py:598
  70.3 1.5 collective-permute-start.25
  71.8 5.6 %shard_map.200 = (f32[256,512]{1,0:T(8,128)}, f32[256,256]{1,0:T(8,128)}, f32[256,128]{1,0:T(8,128)}, bf16[512,1024]{1,0:T(8,128)(2,1)}, bf16[512,1024]{1,0:T(8,128)(2,1)}) custom-call(f32[256,512]{1,0:T(8,128)} %get-tuple-element.94.dy_ref, bf16[256,512]{1,0:T(8,128)(2,1)} %get-tuple-element.95.dz.refs_5_, ...), custom_call_target="tpu_custom_call" | custom-call | tf_op jit(solution)/shard_map/pallas_call | solution.py:598
  78.1 4.3 %shard_map.201 = (f32[256,512]{1,0:T(8,128)}, f32[256,256]{1,0:T(8,128)}, f32[8,768]{1,0:T(8,128)}, bf16[256,128]{1,0:T(8,128)(2,1)}, f32[8,128]{1,0:T(8,128)}) custom-call(f32[512,128]{1,0:T(8,128)} %copy-done.10, f32[256,512]{1,0:T(8,128)} %get-tuple-element.101.dxs, f32[256,256]{1,0:T(8,128)} %get-tuple-element.102.dbc, ...), custom_call_target="tpu_custom_call" | custom-call | tf_op jit(solution)/shard_map/pallas_call | solution.py:598
  86.3 6.5 %shard_map.202 = (bf16[272,256]{1,0:T(8,128)(2,1)}, bf16[272,256]{1,0:T(8,128)(2,1)}, bf16[272,256]{1,0:T(8,128)(2,1)}, bf16[272,256]{1,0:T(8,128)(2,1)}, bf16[5...) custom-call(s32[2]{0:T(128)} %pad_add_fusion.where, ...), custom_call_target="tpu_custom_call" | custom-call | tf_op jit(solution)/shard_map/pallas_call | solution.py:598
  93.3 2.6 %shard_map.203 = (bf16[256,256]{1,0:T(8,128)(2,1)}, bf16[256,256]{1,0:T(8,128)(2,1)}, bf16[256,256]{1,0:T(8,128)(2,1)}, bf16[256,256]{1,0:T(8,128)(2,1)}) custom-call(s32[2]{0:T(128)} %pad_add_fusion.where, bf16[256,512]{1,0:T(8,128)(2,1)} %get-tuple-element.118.raw, bf16[512,1024]{1,0:T(8,128)(2,1)} %get-tuple-element.119.weights), custom_call_target="tpu_custom_call" | custom-call | tf_op jit(solution)/shard_map/pallas_call | solution.py:598
  97.2 2.0 %shard_map.205 = (bf16[176,384]{1,0:T(8,128)(2,1)}, bf16[176,384]{1,0:T(8,128)(2,1)}, bf16[176,384]{1,0:T(8,128)(2,1)}, bf16[176,384]{1,0:T(8,128)(2,1)}) custom-call(bf16[560,384]{1,0:T(8,128)(2,1)} %get-tuple-element.131.own, bf16[560,384]{1,0:T(8,128)(2,1)} %collective-permute-done.41.other), custom_call_target="tpu_custom_call" | custom-call | tf_op jit(solution)/shard_map/pallas_call | solution.py:598
  103.5 1.9 %collective-permute-done.42.refs_1_ = bf16[176,384]{1,0:T(8,128)(2,1)S(1)} collective-permute-done((bf16[176,384]{1,0:T(8,128)(2,1)}, bf16[176,384]{1,0:T(8,128)(2,1)S(1)}, u32[]{:S(2)}, u32[]{:S(2)}) %collective-permute-start.42) | collective-permute-done | bytes 135200 | tf_op jit(solution)/shard_map/ppermute | solution.py:24
  106.3 2.4 %collective-permute-done.43.refs_2_ = bf16[176,384]{1,0:T(8,128)(2,1)S(1)} collective-permute-done((bf16[176,384]{1,0:T(8,128)(2,1)}, bf16[176,384]{1,0:T(8,128)(2,1)S(1)}, u32[]{:S(2)}, u32[]{:S(2)}) %collective-permute-start.43) | collective-permute-done | bytes 135200 | tf_op jit(solution)/shard_map/ppermute | solution.py:24
  110.5 1.8 %shard_map.206 = (f32[8,128]{1,0:T(8,128)}, f32[5,512]{1,0:T(8,128)}, f32[3,8]{1,0:T(4,128)}, f32[1,512]{1,0:T(1,128)}, bf16[144,384]{1,0:T(8,128)(2,1)}) custom-call(bf16[176,384]{1,0:T(8,128)(2,1)} %get-tuple-element.133.refs_0_, bf16[176,384]{1,0:T(8,128)(2,1)} %copy-done.17, bf16[176,384]{1,0:T(8,128)(2,1)} %copy-done.18, bf16[176,384]{1,0:T(8,128)(2,1)} %copy-done.19), custom_call_target="tpu_custom_call" | custom-call | tf_op jit(solution)/shard_map/pallas_call | solution.py:598
  112.3 2.7 %collective-permute-start.28 = (bf16[272,256]{1,0:T(8,128)(2,1)}, bf16[272,256]{1,0:T(8,128)(2,1)S(1)}, u32[]{:S(2)}, u32[]{:S(2)}) collective-permute-start(bf16[272,256]{1,0:T(8,128)(2,1)} %get-tuple-element.116), channel_id=1, source_target_pairs={{0,2},{1,3},{2,0},{3,1},{4,6},{5,7},{6,4},{7,5},{8,10},{9,11},{10,... | collective-permute-start | bytes 417800 | tf_op jit(solution)/shard_map/ppermute | solution.py:24
  116.6 1.6 %collective-permute-done.31.refs_6_ = bf16[256,256]{1,0:T(8,128)(2,1)S(1)} collective-permute-done((bf16[256,256]{1,0:T(8,128)(2,1)}, bf16[256,256]{1,0:T(8,128)(2,1)S(1)}, u32[]{:S(2)}, u32[]{:S(2)}) %collective-permute-start.31) | collective-permute-done | bytes 131104 | tf_op jit(solution)/shard_map/ppermute | solution.py:24
  118.2 2.2 %collective-permute-start.40 = (bf16[128,512]{1,0:T(8,128)(2,1)S(1)}, bf16[128,512]{1,0:T(8,128)(2,1)S(1)}, u32[]{:S(2)}, u32[]{:S(2)}) collective-permute-start(bf16[128,512]{1,0:T(8,128)(2,1)S(1)} %get-tuple-element.151), channel_id=1, source_target_pairs={{0,24},{8,16},{16,8},{24,0},{1,25},{9,17},{17,9},{25,1},{2,26},{10... | collective-permute-start | bytes 393224 | tf_op jit(solution)/shard_map/ppermute | solution.py:24
  120.4 2.1 %collective-permute-start.47 = (bf16[144,384]{1,0:T(8,128)(2,1)S(1)}, bf16[144,384]{1,0:T(8,128)(2,1)S(1)}, u32[]{:S(2)}, u32[]{:S(2)}) collective-permute-start(bf16[144,384]{1,0:T(8,128)(2,1)S(1)} %copy-done.39), channel_id=1, source_target_pairs={{0,3},{1,2},{2,1},{3,0},{4,7},{5,6},{6,5},{7,4},{8,11},{9,10},{10,... | collective-permute-start | bytes 331784 | tf_op jit(solution)/shard_map/ppermute | solution.py:24
  124.6 5.8 %collective-permute-done.28.refs_2_ = bf16[272,256]{1,0:T(8,128)(2,1)S(1)} collective-permute-done((bf16[272,256]{1,0:T(8,128)(2,1)}, bf16[272,256]{1,0:T(8,128)(2,1)S(1)}, u32[]{:S(2)}, u32[]{:S(2)}) %collective-permute-start.28) | collective-permute-done | bytes 139296 | tf_op jit(solution)/shard_map/ppermute | solution.py:24
  132.7 3.1 %collective-permute-start.46 = (bf16[144,384]{1,0:T(8,128)(2,1)S(1)}, bf16[144,384]{1,0:T(8,128)(2,1)S(1)}, u32[]{:S(2)}, u32[]{:S(2)}) collective-permute-start(bf16[144,384]{1,0:T(8,128)(2,1)S(1)} %copy-done.39), channel_id=1, source_target_pairs={{0,2},{1,3},{2,0},{3,1},{4,6},{5,7},{6,4},{7,5},{8,10},{9,11},{10,... | collective-permute-start | bytes 331784 | tf_op jit(solution)/shard_map/ppermute | solution.py:24
  136.3 4.0 %collective-permute-done.46.refs_2_ = bf16[144,384]{1,0:T(8,128)(2,1)S(1)} collective-permute-done((bf16[144,384]{1,0:T(8,128)(2,1)S(1)}, bf16[144,384]{1,0:T(8,128)(2,1)S(1)}, u32[]{:S(2)}, u32[]{:S(2)}) %collective-permute-start.46) | collective-permute-done | bytes 110624 | tf_op jit(solution)/shard_map/ppermute | solution.py:24
  142.3 1.8 %shard_map.207 = (f32[128,256]{1,0:T(8,128)}, f32[5,256]{1,0:T(8,128)}, f32[1,128]{1,0:T(1,128)}) custom-call(bf16[144,384]{1,0:T(8,128)(2,1)} %get-tuple-element.137.refs_0_, bf16[144,384]{1,0:T(8,128)(2,1)} %copy-done.42, bf16[144,384]{1,0:T(8,128)(2,1)} %copy-done.41, bf16[144,384]{1,0:T(8,128)(2,1)} %copy-done.40), custom_call_target="tpu_custom_call" | custom-call | tf_op jit(solution)/shard_map/pallas_call | solution.py:598
  146.9 3.5 %shard_map.204 = (bf16[256,256]{1,0:T(8,128)(2,1)}, bf16[256,256]{1,0:T(8,128)(2,1)}, f32[128,2,512]{2,1,0:T(2,128)}, f32[512,128]{1,0:T(8,128)}) custom-call(s32[2]{0:T(128)} %pad_add_fusion.where, bf16[272,256]{1,0:T(8,128)(2,1)} %get-tuple-element.114.refs_0_, bf16[272,256]{1,0:T(8,128)(2,1)} %copy-done.14, bf16[272,256]{1,0:T(8,128)(2,1)} %copy-done.15, ...), custom_call_target="tpu_custom_call" | custom-call | tf_op jit(solution)/shard_map/pallas_call | solution.py:598
  (179 shorter events, 46.6 us)
Async XLA Ops:
  3.3 19.1 %collective-permute-start.6 = (bf16[128,1408]{1,0:T(8,128)(2,1)}, bf16[128,1408]{1,0:T(8,128)(2,1)S(1)}, u32[]{:S(2)}, u32[]{:S(2)}) collective-permute-start(bf16[128,1408]{1,0:T(8,128)(2,1)} %get-tuple-element.83.refs_6_), channel_id=1, source_target_pairs={{0,24},{8,16},{16,8},{24,0},{1,25},{9,17},{17,9},{25,1},{2,26},{10... | collective-permute-start | bytes 1081352 | tf_op jit(solution)/shard_map/ppermute | solution.py:24
  7.2 16.3 %collective-permute-start.5 = (bf16[128,1408]{1,0:T(8,128)(2,1)}, bf16[128,1408]{1,0:T(8,128)(2,1)S(1)}, u32[]{:S(2)}, u32[]{:S(2)}) collective-permute-start(bf16[128,1408]{1,0:T(8,128)(2,1)} %get-tuple-element.83.refs_6_), channel_id=1, source_target_pairs={{0,16},{8,24},{16,0},{24,8},{1,17},{9,25},{17,1},{25,9},{2,18},{10... | collective-permute-start | bytes 1081352 | tf_op jit(solution)/shard_map/ppermute | solution.py:24
  7.7 16.1 %collective-permute-start.4 = (bf16[128,1408]{1,0:T(8,128)(2,1)}, bf16[128,1408]{1,0:T(8,128)(2,1)S(1)}, u32[]{:S(2)}, u32[]{:S(2)}) collective-permute-start(bf16[128,1408]{1,0:T(8,128)(2,1)} %get-tuple-element.83.refs_6_), channel_id=1, source_target_pairs={{0,8},{8,0},{16,24},{24,16},{1,9},{9,1},{17,25},{25,17},{2,10},{10... | collective-permute-start | bytes 1081352 | tf_op jit(solution)/shard_map/ppermute | solution.py:24
  7.9 8.4 %collective-permute-start.2 = (bf16[256,256]{1,0:T(8,128)(2,1)}, bf16[256,256]{1,0:T(8,128)(2,1)S(1)}, u32[]{:S(2)}, u32[]{:S(2)}) collective-permute-start(bf16[256,256]{1,0:T(8,128)(2,1)} %bitcast.12), channel_id=1, source_target_pairs={{0,3},{1,2},{2,1},{3,0},{4,7},{5,6},{6,5},{7,4},{8,11},{9,10},{10,... | collective-permute-start | bytes 393224 | tf_op jit(solution)/shard_map/ppermute | solution.py:24
  11.9 10.5 %collective-permute-start.1 = (bf16[256,256]{1,0:T(8,128)(2,1)}, bf16[256,256]{1,0:T(8,128)(2,1)S(1)}, u32[]{:S(2)}, u32[]{:S(2)}) collective-permute-start(bf16[256,256]{1,0:T(8,128)(2,1)} %bitcast.13), channel_id=1, source_target_pairs={{0,2},{1,3},{2,0},{3,1},{4,6},{5,7},{6,4},{7,5},{8,10},{9,11},{10,... | collective-permute-start | bytes 393224 | tf_op jit(solution)/shard_map/ppermute | solution.py:24
  16.2 8.8 %collective-permute-start = (bf16[256,256]{1,0:T(8,128)(2,1)}, bf16[256,256]{1,0:T(8,128)(2,1)S(1)}, u32[]{:S(2)}, u32[]{:S(2)}) collective-permute-start(bf16[256,256]{1,0:T(8,128)(2,1)} %bitcast.14), channel_id=1, source_target_pairs={{0,1},{1,0},{2,3},{3,2},{4,5},{5,4},{6,7},{7,6},{8,9},{9,8},{10,11... | collective-permute-start | bytes 393224 | tf_op jit(solution)/shard_map/ppermute | solution.py:24
  22.4 15.6 %collective-permute-start.7 = (bf16[128,1408]{1,0:T(8,128)(2,1)}, bf16[128,1408]{1,0:T(8,128)(2,1)S(1)}, u32[]{:S(2)}, u32[]{:S(2)}) collective-permute-start(bf16[128,1408]{1,0:T(8,128)(2,1)} %get-tuple-element.83.refs_6_), channel_id=1, source_target_pairs={{0,4},{4,0},{1,5},{5,1},{2,6},{6,2},{3,7},{7,3},{8,12},{12,8},{9,1... | collective-permute-start | bytes 1081352 | tf_op jit(solution)/shard_map/ppermute | solution.py:24
  22.4 16.0 %collective-permute-start.10 = (bf16[128,1408]{1,0:T(8,128)(2,1)S(1)}, bf16[128,1408]{1,0:T(8,128)(2,1)S(1)}, u32[]{:S(2)}, u32[]{:S(2)}) collective-permute-start(bf16[128,1408]{1,0:T(8,128)(2,1)S(1)} %collective-permute-done.6.refs_9_), channel_id=1, source_target_pairs={{0,4},{4,0},{1,5},{5,1},{2,6},{6,2},{3,7},{7,3},{8,12},{12,8},{9,1... | collective-permute-start | bytes 1081352 | tf_op jit(solution)/shard_map/ppermute | solution.py:24
  23.6 16.6 %collective-permute-start.9 = (bf16[128,1408]{1,0:T(8,128)(2,1)S(1)}, bf16[128,1408]{1,0:T(8,128)(2,1)S(1)}, u32[]{:S(2)}, u32[]{:S(2)}) collective-permute-start(bf16[128,1408]{1,0:T(8,128)(2,1)S(1)} %collective-permute-done.5.refs_8_), channel_id=1, source_target_pairs={{0,4},{4,0},{1,5},{5,1},{2,6},{6,2},{3,7},{7,3},{8,12},{12,8},{9,1... | collective-permute-start | bytes 1081352 | tf_op jit(solution)/shard_map/ppermute | solution.py:24
  23.9 17.5 %collective-permute-start.8 = (bf16[128,1408]{1,0:T(8,128)(2,1)S(1)}, bf16[128,1408]{1,0:T(8,128)(2,1)S(1)}, u32[]{:S(2)}, u32[]{:S(2)}) collective-permute-start(bf16[128,1408]{1,0:T(8,128)(2,1)S(1)} %collective-permute-done.4.refs_7_), channel_id=1, source_target_pairs={{0,4},{4,0},{1,5},{5,1},{2,6},{6,2},{3,7},{7,3},{8,12},{12,8},{9,1... | collective-permute-start | bytes 1081352 | tf_op jit(solution)/shard_map/ppermute | solution.py:24
  34.5 13.7 %collective-permute-start.13 = (bf16[256,256]{1,0:T(8,128)(2,1)}, bf16[256,256]{1,0:T(8,128)(2,1)S(1)}, u32[]{:S(2)}, u32[]{:S(2)}) collective-permute-start(bf16[256,256]{1,0:T(8,128)(2,1)} %bitcast.18), channel_id=1, source_target_pairs={{0,2},{1,3},{2,0},{3,1},{4,6},{5,7},{6,4},{7,5},{8,10},{9,11},{10,... | collective-permute-start | bytes 393224 | tf_op jit(solution)/shard_map/ppermute | solution.py:24
  38.0 11.5 %collective-permute-start.12 = (bf16[256,256]{1,0:T(8,128)(2,1)}, bf16[256,256]{1,0:T(8,128)(2,1)S(1)}, u32[]{:S(2)}, u32[]{:S(2)}) collective-permute-start(bf16[256,256]{1,0:T(8,128)(2,1)} %bitcast.19), channel_id=1, source_target_pairs={{0,1},{1,0},{2,3},{3,2},{4,5},{5,4},{6,7},{7,6},{8,9},{9,8},{10,11... | collective-permute-start | bytes 393224 | tf_op jit(solution)/shard_map/ppermute | solution.py:24
  38.4 11.2 %collective-permute-start.17 = (bf16[512,128]{1,0:T(8,128)(2,1)}, bf16[512,128]{1,0:T(8,128)(2,1)S(1)}, u32[]{:S(2)}, u32[]{:S(2)}) collective-permute-start(bf16[512,128]{1,0:T(8,128)(2,1)} %refs_5_.1), channel_id=1, source_target_pairs={{0,24},{8,16},{16,8},{24,0},{1,25},{9,17},{17,9},{25,1},{2,26},{10... | collective-permute-start | bytes 393224 | tf_op jit(solution)/shard_map/ppermute | solution.py:24
  40.2 9.9 %collective-permute-start.16 = (bf16[512,128]{1,0:T(8,128)(2,1)}, bf16[512,128]{1,0:T(8,128)(2,1)S(1)}, u32[]{:S(2)}, u32[]{:S(2)}) collective-permute-start(bf16[512,128]{1,0:T(8,128)(2,1)} %refs_5_.1), channel_id=1, source_target_pairs={{0,16},{8,24},{16,0},{24,8},{1,17},{9,25},{17,1},{25,9},{2,18},{10... | collective-permute-start | bytes 393224 | tf_op jit(solution)/shard_map/ppermute | solution.py:24
  41.4 8.8 %collective-permute-start.15 = (bf16[512,128]{1,0:T(8,128)(2,1)}, bf16[512,128]{1,0:T(8,128)(2,1)S(1)}, u32[]{:S(2)}, u32[]{:S(2)}) collective-permute-start(bf16[512,128]{1,0:T(8,128)(2,1)} %refs_5_.1), channel_id=1, source_target_pairs={{0,8},{8,0},{16,24},{24,16},{1,9},{9,1},{17,25},{25,17},{2,10},{10... | collective-permute-start | bytes 393224 | tf_op jit(solution)/shard_map/ppermute | solution.py:24
  48.2 7.8 %collective-permute-start.11 = (f32[512,128]{1,0:T(8,128)}, f32[512,128]{1,0:T(8,128)S(1)}, u32[]{:S(2)}, u32[]{:S(2)}) collective-permute-start(f32[512,128]{1,0:T(8,128)} %get-tuple-element.84), channel_id=1, source_target_pairs={{0,4},{1,5},{2,6},{3,7},{8,12},{9,13},{10,14},{11,15},{16,20},{17,... | collective-permute-start | bytes 786440 | tf_op jit(solution)/shard_map/ppermute | solution.py:46
  83.6 28.7 %collective-permute-start.33 = (bf16[512,1024]{1,0:T(8,128)(2,1)}, bf16[512,1024]{1,0:T(8,128)(2,1)S(1)}, u32[]{:S(2)}, u32[]{:S(2)}) collective-permute-start(bf16[512,1024]{1,0:T(8,128)(2,1)} %get-tuple-element.125), channel_id=1, source_target_pairs={{0,4},{4,0},{1,5},{5,1},{2,6},{6,2},{3,7},{7,3},{8,12},{12,8},{9,1... | collective-permute-start | bytes 3145736 | tf_op jit(solution)/shard_map/ppermute | solution.py:24
  92.7 8.6 %collective-permute-start.37 = (bf16[512,512]{1,0:T(8,128)(2,1)}, bf16[512,512]{1,0:T(8,128)(2,1)S(1)}, u32[]{:S(2)}, u32[]{:S(2)}) collective-permute-start(bf16[512,512]{1,0:T(8,128)(2,1)} %get-tuple-element.127), channel_id=1, source_target_pairs={{0,4},{4,0},{1,5},{5,1},{2,6},{6,2},{3,7},{7,3},{8,12},{12,8},{9,1... | collective-permute-start | bytes 1572872 | tf_op jit(solution)/shard_map/ppermute | solution.py:24
  95.9 19.5 %collective-permute-start.30 = (bf16[256,256]{1,0:T(8,128)(2,1)}, bf16[256,256]{1,0:T(8,128)(2,1)}, u32[]{:S(2)}, u32[]{:S(2)}) collective-permute-start(bf16[256,256]{1,0:T(8,128)(2,1)} %get-tuple-element.121), channel_id=1, source_target_pairs={{0,1},{1,0},{2,3},{3,2},{4,5},{5,4},{6,7},{7,6},{8,9},{9,8},{10,11... | collective-permute-start | bytes 393224 | tf_op jit(solution)/shard_map/ppermute | solution.py:24
  100.5 8.2 %collective-permute-start.43 = (bf16[176,384]{1,0:T(8,128)(2,1)}, bf16[176,384]{1,0:T(8,128)(2,1)S(1)}, u32[]{:S(2)}, u32[]{:S(2)}) collective-permute-start(bf16[176,384]{1,0:T(8,128)(2,1)} %get-tuple-element.135), channel_id=1, source_target_pairs={{0,16},{8,24},{16,0},{24,8},{1,17},{9,25},{17,1},{25,9},{2,18},{10... | collective-permute-start | bytes 405512 | tf_op jit(solution)/shard_map/ppermute | solution.py:24
  101.3 8.5 %collective-permute-start.44 = (bf16[176,384]{1,0:T(8,128)(2,1)}, bf16[176,384]{1,0:T(8,128)(2,1)S(1)}, u32[]{:S(2)}, u32[]{:S(2)}) collective-permute-start(bf16[176,384]{1,0:T(8,128)(2,1)} %get-tuple-element.136), channel_id=1, source_target_pairs={{0,24},{8,16},{16,8},{24,0},{1,25},{9,17},{17,9},{25,1},{2,26},{10... | collective-permute-start | bytes 405512 | tf_op jit(solution)/shard_map/ppermute | solution.py:24
  105.4 12.8 %collective-permute-start.31 = (bf16[256,256]{1,0:T(8,128)(2,1)}, bf16[256,256]{1,0:T(8,128)(2,1)S(1)}, u32[]{:S(2)}, u32[]{:S(2)}) collective-permute-start(bf16[256,256]{1,0:T(8,128)(2,1)} %get-tuple-element.122), channel_id=1, source_target_pairs={{0,2},{1,3},{2,0},{3,1},{4,6},{5,7},{6,4},{7,5},{8,10},{9,11},{10,... | collective-permute-start | bytes 393224 | tf_op jit(solution)/shard_map/ppermute | solution.py:24
  108.7 11.7 %collective-permute-start.32 = (bf16[256,256]{1,0:T(8,128)(2,1)}, bf16[256,256]{1,0:T(8,128)(2,1)S(1)}, u32[]{:S(2)}, u32[]{:S(2)}) collective-permute-start(bf16[256,256]{1,0:T(8,128)(2,1)} %get-tuple-element.123), channel_id=1, source_target_pairs={{0,3},{1,2},{2,1},{3,0},{4,7},{5,6},{6,5},{7,4},{8,11},{9,10},{10,... | collective-permute-start | bytes 393224 | tf_op jit(solution)/shard_map/ppermute | solution.py:24
  109.8 13.4 %collective-permute-start.27 = (bf16[272,256]{1,0:T(8,128)(2,1)}, bf16[272,256]{1,0:T(8,128)(2,1)S(1)}, u32[]{:S(2)}, u32[]{:S(2)}) collective-permute-start(bf16[272,256]{1,0:T(8,128)(2,1)} %get-tuple-element.115), channel_id=1, source_target_pairs={{0,1},{1,0},{2,3},{3,2},{4,5},{5,4},{6,7},{7,6},{8,9},{9,8},{10,11... | collective-permute-start | bytes 417800 | tf_op jit(solution)/shard_map/ppermute | solution.py:24
  112.3 18.0 %collective-permute-start.28 = (bf16[272,256]{1,0:T(8,128)(2,1)}, bf16[272,256]{1,0:T(8,128)(2,1)S(1)}, u32[]{:S(2)}, u32[]{:S(2)}) collective-permute-start(bf16[272,256]{1,0:T(8,128)(2,1)} %get-tuple-element.116), channel_id=1, source_target_pairs={{0,2},{1,3},{2,0},{3,1},{4,6},{5,7},{6,4},{7,5},{8,10},{9,11},{10,... | collective-permute-start | bytes 417800 | tf_op jit(solution)/shard_map/ppermute | solution.py:24
  115.4 16.3 %collective-permute-start.29 = (bf16[272,256]{1,0:T(8,128)(2,1)}, bf16[272,256]{1,0:T(8,128)(2,1)S(1)}, u32[]{:S(2)}, u32[]{:S(2)}) collective-permute-start(bf16[272,256]{1,0:T(8,128)(2,1)} %get-tuple-element.117), channel_id=1, source_target_pairs={{0,3},{1,2},{2,1},{3,0},{4,7},{5,6},{6,5},{7,4},{8,11},{9,10},{10,... | collective-permute-start | bytes 417800 | tf_op jit(solution)/shard_map/ppermute | solution.py:24
  118.2 14.5 %collective-permute-start.40 = (bf16[128,512]{1,0:T(8,128)(2,1)S(1)}, bf16[128,512]{1,0:T(8,128)(2,1)S(1)}, u32[]{:S(2)}, u32[]{:S(2)}) collective-permute-start(bf16[128,512]{1,0:T(8,128)(2,1)S(1)} %get-tuple-element.151), channel_id=1, source_target_pairs={{0,24},{8,16},{16,8},{24,0},{1,25},{9,17},{17,9},{25,1},{2,26},{10... | collective-permute-start | bytes 393224 | tf_op jit(solution)/shard_map/ppermute | solution.py:24
  120.4 15.4 %collective-permute-start.47 = (bf16[144,384]{1,0:T(8,128)(2,1)S(1)}, bf16[144,384]{1,0:T(8,128)(2,1)S(1)}, u32[]{:S(2)}, u32[]{:S(2)}) collective-permute-start(bf16[144,384]{1,0:T(8,128)(2,1)S(1)} %copy-done.39), channel_id=1, source_target_pairs={{0,3},{1,2},{2,1},{3,0},{4,7},{5,6},{6,5},{7,4},{8,11},{9,10},{10,... | collective-permute-start | bytes 331784 | tf_op jit(solution)/shard_map/ppermute | solution.py:24
  123.3 22.7 %collective-permute-start.36 = (bf16[128,1024]{1,0:T(8,128)(2,1)S(1)}, bf16[128,1024]{1,0:T(8,128)(2,1)S(1)}, u32[]{:S(2)}, u32[]{:S(2)}) collective-permute-start(bf16[128,1024]{1,0:T(8,128)(2,1)S(1)} %get-tuple-element.147), channel_id=1, source_target_pairs={{0,24},{8,16},{16,8},{24,0},{1,25},{9,17},{17,9},{25,1},{2,26},{10... | collective-permute-start | bytes 786440 | tf_op jit(solution)/shard_map/ppermute | solution.py:24
  130.3 15.6 %collective-permute-start.35 = (bf16[128,1024]{1,0:T(8,128)(2,1)S(1)}, bf16[128,1024]{1,0:T(8,128)(2,1)S(1)}, u32[]{:S(2)}, u32[]{:S(2)}) collective-permute-start(bf16[128,1024]{1,0:T(8,128)(2,1)S(1)} %get-tuple-element.148), channel_id=1, source_target_pairs={{0,16},{8,24},{16,0},{24,8},{1,17},{9,25},{17,1},{25,9},{2,18},{10... | collective-permute-start | bytes 786440 | tf_op jit(solution)/shard_map/ppermute | solution.py:24
  131.7 14.3 %collective-permute-start.34 = (bf16[128,1024]{1,0:T(8,128)(2,1)S(1)}, bf16[128,1024]{1,0:T(8,128)(2,1)S(1)}, u32[]{:S(2)}, u32[]{:S(2)}) collective-permute-start(bf16[128,1024]{1,0:T(8,128)(2,1)S(1)} %get-tuple-element.149), channel_id=1, source_target_pairs={{0,8},{8,0},{16,24},{24,16},{1,9},{9,1},{17,25},{25,17},{2,10},{10... | collective-permute-start | bytes 786440 | tf_op jit(solution)/shard_map/ppermute | solution.py:24
  132.7 7.5 %collective-permute-start.46 = (bf16[144,384]{1,0:T(8,128)(2,1)S(1)}, bf16[144,384]{1,0:T(8,128)(2,1)S(1)}, u32[]{:S(2)}, u32[]{:S(2)}) collective-permute-start(bf16[144,384]{1,0:T(8,128)(2,1)S(1)} %copy-done.39), channel_id=1, source_target_pairs={{0,2},{1,3},{2,0},{3,1},{4,6},{5,7},{6,4},{7,5},{8,10},{9,11},{10,... | collective-permute-start | bytes 331784 | tf_op jit(solution)/shard_map/ppermute | solution.py:24
  (64 other events, 422.4 us)

commit v2 on v1

--- a/solution.py
+++ b/solution.py
@@ -128,9 +128,9 @@
 def unit(pair, p, where):
     if pair:
         t, k = divmod(p, 4)
-        return k ^ where[0], pl.multiple_of((t ^ where[1]) * LANES, LANES)
+        return k ^ (where[0] >> 1), pl.multiple_of((t ^ (where[0] & 1)) * LANES, LANES)
     j, u = divmod(p, 2)
-    return j ^ where[0], u * LANES
+    return j ^ (where[0] >> 1), u * LANES
 
 
 def assembled(scratch, pieces, axis):
@@ -144,67 +144,52 @@
         at += size
 
 
-def pack_kernel(w_zx, w_bc, w_dt, gain, params, out, params_out):
-    shard, inner = w_zx.shape[0], w_zx.shape[2]
-    heads, wide_bc = w_dt.shape[0], w_bc.shape[1]
-    both = w_zx[...].astype(f32)
-    for j in range(2):
-        out[:, j * inner : (j + 1) * inner] = both[:, j, :].astype(bf16)
-    out[:, 2 * inner : 2 * inner + wide_bc] = w_bc[...]
+def pack_kernel(w_bc, w_dt, gain, params, out, params_out):
+    shard, wide_bc = w_bc.shape
+    heads = w_dt.shape[0]
+    out[:, 0:wide_bc] = w_bc[...]
     row = iota((LANES - heads, shard), 0)
     rest = jnp.where(row == 0, gain[...].astype(f32), 0.0)
     tile = jnp.concatenate([w_dt[...].astype(f32), rest], axis=0).T
-    out[:, 2 * inner + wide_bc :] = tile.astype(bf16)
+    out[:, wide_bc:] = tile.astype(bf16)
     params_out[...] = jnp.zeros(params_out.shape, f32)
     params_out[0:3, 0:heads] = params[...]
 
 
-def norm_kernel(pair, n_blocks, where, *refs):
-    blocks = refs[:n_blocks]
-    x_perm, inv_ref, edge_ref, hold = refs[n_blocks:]
-    rows, part = blocks[0].shape
-    swap = n_blocks * part // LANES // 2 if pair else 0
-    total = jnp.zeros((rows, 1), f32)
+def forward_kernel(pair, heads, n_blocks, n_pieces, where, *refs):
+    conv_x, conv_bc, params = refs[:3]
+    blocks = refs[3 : 3 + n_blocks]
+    zx_pieces = refs[3 + n_blocks : 3 + n_blocks + n_pieces]
+    bcd_pieces = refs[3 + n_blocks + n_pieces : 3 + n_blocks + 2 * n_pieces]
+    (
+        z_ref, xe_ref, be_ref, ux_ref, ubc_ref, dt_ref, cum_ref, y_ref, state_ref, w_in, x_perm,
+        inv_ref, normed, gain_ref, rows_in, xe, be, hold,
+    ) = refs[3 + n_blocks + 2 * n_pieces :]
+    rows, inner = ux_ref.shape
+    width = inner // heads
+    state_n = ubc_ref.shape[1] // 2
+    taps = conv_x.shape[0] - 1
+    assembled(w_in.at[:, 0 : 2 * inner], zx_pieces, 0)
+    assembled(w_in.at[:, 2 * inner :], bcd_pieces, 0)
+    total = jnp.zeros((HALO + rows, 1), f32)
     for k, block in enumerate(blocks):
         value = block[...].astype(f32)
         hold[k] = value
         total += jnp.sum(value * value, axis=1, keepdims=True)
-    inv = lax.rsqrt(total / (n_blocks * part) + epsilon)
-    inv_ref[...] = jnp.broadcast_to(inv, inv_ref.shape)
-    for p in range(n_blocks * part // LANES):
-        block, lane = unit(pair, p, where)
-        value = hold[block, :, pl.ds(lane, LANES)].astype(bf16)
-        x_perm[:, p * LANES : (p + 1) * LANES] = value
-        there = p ^ swap
-        edge_ref[:, there * LANES : (there + 1) * LANES] = value[rows - HALO :, :]
-
-
-def forward_kernel(heads, n_pieces, *refs):
-    x_perm, inv, edge, conv_x, conv_bc, params = refs[:6]
-    pieces = refs[6 : 6 + n_pieces]
-    (z_ref, xe_ref, be_ref, ux_ref, ubc_ref, dt_ref, cum_ref, y_ref, state_ref, w_in) = refs[
-        6 + n_pieces : 16 + n_pieces
-    ]
-    normed, gain_ref, rows_in, xe, be = refs[16 + n_pieces :]
-    rows, inner = ux_ref.shape
-    width = inner // heads
-    state_n = ubc_ref.shape[1] // 2
-    taps = conv_x.shape[0] - 1
-    assembled(w_in, pieces, 0)
+    inv = lax.rsqrt(total / x_perm.shape[1] + epsilon)
+    inv_ref[...] = jnp.broadcast_to(inv[HALO:], inv_ref.shape)
     tile = 2 * inner + 2 * state_n
     eye = iota((LANES, LANES), 0) == iota((LANES, LANES), 1)
     for p in range(w_in.shape[0] // LANES):
         cut = slice(p * LANES, (p + 1) * LANES)
         gain = w_in[cut, tile : tile + LANES][:, heads : heads + 1].astype(f32)
-        gain_ref[:, cut] = jnp.sum(jnp.where(eye, gain, 0.0), axis=0, keepdims=True)
-    gains = gain_ref[...]
-    normed[...] = (x_perm[...].astype(f32) * inv[:, 0:1] * gains).astype(bf16)
-    before = edge[...].astype(f32)
-    before_inv = lax.rsqrt(
-        jnp.sum(before * before, axis=1, keepdims=True) / before.shape[1] + epsilon
-    )
-    rows_in[0:HALO, :] = (before * before_inv * gains).astype(bf16)
-    rows_in[HALO : HALO + rows, :] = normed[...]
+        gain = jnp.sum(jnp.where(eye, gain, 0.0), axis=0, keepdims=True)
+        gain_ref[:, cut] = gain
+        block, lane = unit(pair, p, where)
+        value = hold[block, :, pl.ds(lane, LANES)]
+        x_perm[:, cut] = value[HALO:].astype(bf16)
+        rows_in[:, cut] = (value * inv * gain).astype(bf16)
+    normed[...] = rows_in[HALO : HALO + rows, :]
     z_ref[...] = nn(normed[...], w_in[:, 0:inner]).astype(bf16)
     x_raw = nn(rows_in[...], w_in[:, inner : 2 * inner]).astype(bf16)
     xe_ref[...] = x_raw
@@ -256,12 +241,17 @@
     state_ref[...] = tn(scaled * spread(to_end, heads, width), b_mat)
 
 
-def cot_kernel(pair, n_blocks, n_pieces, where, *refs):
-    normed = refs[0]
-    blocks = refs[1 : 1 + n_blocks]
-    pieces = refs[1 + n_blocks : 1 + n_blocks + n_pieces]
-    go_ref, w_ref, normed_t, cot_t, hold, cot = refs[1 + n_blocks + n_pieces :]
-    assembled(w_ref, pieces, 1)
+def gate_kernel(pair, heads, n_blocks, n_pieces, where, *refs):
+    normed, state, ubc, cum, y_loc, z, gain = refs[:7]
+    blocks = refs[7 : 7 + n_blocks]
+    pieces = refs[7 + n_blocks : 7 + n_blocks + n_pieces]
+    rest = refs[7 + n_blocks + n_pieces :]
+    y_ref, go_ref, stats_ref, normed_t, cot_t = rest[:5]
+    outs, (hold, cot, weights, out_hold) = rest[5 : 5 + n_blocks], rest[5 + n_blocks :]
+    rows, inner = y_ref.shape
+    width = inner // heads
+    state_n = ubc.shape[1] // 2
+    assembled(weights, pieces, 1)
     for k, block in enumerate(blocks):
         hold[k] = block[...].astype(f32)
     for p in range(cot.shape[1] // LANES):
@@ -271,13 +261,8 @@
         cot[:, cut] = value.astype(bf16)
         cot_t[cut, :] = value.T.astype(bf16)
         normed_t[cut, :] = normed[:, cut].astype(f32).T.astype(bf16)
-    go_ref[...] = nt(cot[...], w_ref[...])
-
-
-def gate_kernel(heads, state, ubc, cum, y_loc, z, gain, go, y_ref, raw_ref, stats_ref):
-    rows, inner = y_ref.shape
-    width = inner // heads
-    state_n = ubc.shape[1] // 2
+    grad_o = nt(cot[...], weights[...])
+    go_ref[...] = grad_o
     u_c = ubc[:, state_n:]
     c_mat = u_c * sigmoid(u_c)
     y = y_loc[...] + nt(c_mat, state[...]) * spread(jnp.exp(cum[...]), heads, width)
@@ -285,22 +270,17 @@
     z_val = z[...].astype(f32)
     gated = y * z_val * sigmoid(z_val)
     raw = gated * gain[...]
-    raw_ref[...] = raw.astype(bf16)
     squares = jnp.sum(gated * gated, axis=1, keepdims=True)
-    cross = jnp.sum(go[...] * raw, axis=1, keepdims=True)
+    cross = jnp.sum(grad_o * raw, axis=1, keepdims=True)
     lane = iota((rows, LANES), 1)
     both = jnp.where(lane == 0, squares, jnp.where(lane == 1, cross, 0.0))
     stats_ref[...] = both.T[0:8, :]
-
-
-def out_kernel(pair, where, raw, weights, *refs):
-    hold = refs[-1]
-    part = nn(raw[...], weights[...]).astype(bf16)
+    part = nn(raw, weights[...]).astype(bf16)
     for p in range(weights.shape[1] // LANES):
         block, lane = unit(pair, p, where)
-        hold[block, :, pl.ds(lane, LANES)] = part[:, p * LANES : (p + 1) * LANES]
-    for k, ref in enumerate(refs[:-1]):
-        ref[...] = hold[k]
+        out_hold[block, :, pl.ds(lane, LANES)] = part[:, p * LANES : (p + 1) * LANES]
+    for k, ref in enumerate(outs):
+        ref[...] = out_hold[k]
 
 
 def gate_back_kernel(heads, full_inner, n_stats, *refs):
@@ -510,21 +490,19 @@
         gb_ref[half + count :, :] = low
 
 
-def fold_kernel(n_blocks, own, other, *blocks):
-    size = (own.shape[0] - blocks[0].shape[0]) // (n_blocks - 1)
-    extra = blocks[0].shape[0] - size
-    for k, ref in enumerate(blocks):
+def fold_kernel(n_blocks, own, other, x_own, x_other, *refs):
+    blocks, x_blocks = refs[:n_blocks], refs[n_blocks:]
+    size = x_blocks[0].shape[0]
+    first, half = n_blocks * size, (blocks[0].shape[0] - size) // 2
+    total = [ref[first:, :].astype(f32) for ref in (own, other)]
+    total = (total[0][:half] + total[0][half:]) + (total[1][:half] + total[1][half:])
+    high, low = terms(total, 2)
+    for k in range(n_blocks):
         cut = slice(k * size, (k + 1) * size)
-        ref[0:size, :] = (own[cut, :].astype(f32) + other[cut, :].astype(f32)).astype(bf16)
-    if extra > 0:
-        first, half = n_blocks * size, extra // 2
-        total = [ref[first:, :].astype(f32) for ref in (own, other)]
-        total = (total[0][:half] + total[0][half:]) + (total[1][:half] + total[1][half:])
-        high = total.astype(bf16)
-        low = (total - high.astype(f32)).astype(bf16)
-        for ref in blocks:
-            ref[size : size + half, :] = high
-            ref[size + half :, :] = low
+        blocks[k][0:size, :] = (own[cut, :].astype(f32) + other[cut, :].astype(f32)).astype(bf16)
+        blocks[k][size : size + half, :] = high
+        blocks[k][size + half :, :] = low
+        x_blocks[k][...] = (x_own[cut, :].astype(f32) + x_other[cut, :].astype(f32)).astype(bf16)
 
 
 def small_kernel(taps, heads, n_blocks, *refs):
@@ -540,20 +518,24 @@
         cx_ref[:, cut] = small[j * n : (j + 1) * n, 0:wide_bc]
         ggain_ref[:, cut] = small[3 * n + j : 3 * n + j + 1, 0:wide_bc]
     ghead_ref[...] = small[3 * n + 2 : 3 * n + 5, 0:heads]
-    shared_ref[0:size, :] = total[0:size].astype(bf16)
-    high = small[2 * n : 2 * n + 8].astype(bf16)
+    shared_ref[0:size, :] = total[0:size, 0:wide_bc].astype(bf16)
+    tail = jnp.concatenate([small[2 * n : 2 * n + 7, 0:wide_bc], jnp.zeros((1, wide_bc), f32)], axis=0)
+    gain = row_of(total[0:size, wide_bc:][:, heads : heads + 1])
+    gain = jnp.concatenate([gain, jnp.zeros((1, wide_bc - size), f32)], axis=1)
+    tail = jnp.where(iota((8, wide_bc), 0) == 7, gain, tail)
+    high, low = terms(tail, 2)
     shared_ref[size : size + 8, :] = high
-    shared_ref[size + 8 :, :] = (small[2 * n : 2 * n + 8] - high.astype(f32)).astype(bf16)
-
-
-def shared_kernel(gain_lane, n_blocks, *refs):
+    shared_ref[size + 8 :, :] = low
+
+
+def shared_kernel(n_blocks, *refs):
     gbc_ref, cbc_ref, ngain_ref = refs[n_blocks:]
     total = tree_sum([b[...].astype(f32) for b in refs[:n_blocks]])
-    size, wide_bc = gbc_ref.shape
-    gbc_ref[...] = total[0:size, 0:wide_bc]
-    rows = total[size : size + 8, 0:wide_bc] + total[size + 8 :, 0:wide_bc]
+    size = gbc_ref.shape[0]
+    gbc_ref[...] = total[0:size]
+    rows = total[size : size + 8] + total[size + 8 :]
     cbc_ref[...] = rows[0 : cbc_ref.shape[0]]
-    ngain_ref[...] = row_of(total[0:size, wide_bc:][:, gain_lane : gain_lane + 1])
+    ngain_ref[...] = rows[7:8, 0 : ngain_ref.shape[1]]
 
 
 def input_kernel(pair, full_d, n_blocks, n_grads, where, *refs):
@@ -620,7 +602,7 @@
     pair = seq_n == 2 and dp_n == head_n == 4 and shard == LANES and part_d == 2 * LANES
     state_n = wide_bc // 2
 
-    where = jnp.stack([head_i ^ dp_i, seq_i] if pair else [head_i, seq_i]).astype(jnp.int32)
+    where = ((head_i ^ dp_i) * 2 + seq_i if pair else head_i * 2).astype(jnp.int32).reshape(1)
 
     def gathered(part, axis):
         if not pair:
@@ -628,17 +610,10 @@
         own = exchanged(part, "dp")
         return own + [sent(p, "seq", 1) for p in own]
 
-    def reduced(own, other, extra=0):
+    def reduced(own, other):
         recv = sent(other, "seq", 1)
-        if extra == 0:
-            both = (own.astype(f32) + recv.astype(f32)).astype(bf16)
-            blocks = [both[k * shard : (k + 1) * shard] for k in range(dp_n)]
-        else:
-            blocks = call(
-                functools.partial(fold_kernel, dp_n),
-                [((shard + extra, own.shape[1]), bf16)] * dp_n,
-                [own, recv],
-            )
+        both = (own.astype(f32) + recv.astype(f32)).astype(bf16)
+        blocks = [both[k * shard : (k + 1) * shard] for k in range(dp_n)]
         return scattered(blocks, "dp")
 
     def reduced_apart(own, other):
@@ -648,34 +623,29 @@
     x_local = hidden_in[0, 0]
     cot_local = cotangent[0, 0]
     wide_bcd = wide_bc + LANES
+    x_halo = passed_along(x_local, "seq", 1)[rows - HALO :]
+    zx_pieces = gathered(w_zx.reshape(shard, 2 * inner), 0)
+    x_blocks = exchanged(jnp.concatenate([x_halo, x_local], axis=0), "head")
     if pair:
         packed, params = call(
             pack_kernel,
-            [((shard, 2 * inner + wide_bcd), bf16), ((8, LANES), f32)],
-            [w_zx, w_bc, w_dt.T, norm_gain[None], head_params],
+            [((shard, wide_bcd), bf16), ((8, LANES), f32)],
+            [w_bc, w_dt.T, norm_gain[None], head_params],
         )
     else:
         pad = jnp.zeros((shard, LANES - heads - 1), bf16)
-        packed = [w_zx.reshape(shard, 2 * inner), w_bc, w_dt, norm_gain[:, None], pad]
-        packed = jnp.concatenate(packed, axis=1)
+        packed = jnp.concatenate([w_bc, w_dt, norm_gain[:, None], pad], axis=1)
         params = jnp.pad(head_params, ((0, 5), (0, LANES - heads)))
-    pieces = gathered(packed, 0)
-    x_blocks = exchanged(x_local, "head")
+    bcd_pieces = gathered(packed, 0)
     out_pieces = gathered(w_out, 1)
     cot_blocks = exchanged(cot_local, "head")
     gain_row = gate_gain[None]
-    n_in, n_out = len(pieces), len(out_pieces)
-
-    x_perm, inv_in, edge = call(
-        functools.partial(norm_kernel, pair, head_n),
-        [((rows, full_d), bf16), ((rows, LANES), f32), ((HALO, full_d), bf16)],
-        [where, *x_blocks],
-        [((head_n, rows, part_d), f32)],
-        1,
-    )
-    edge = passed_along(edge, "seq", 1)
-    z, x_ext, bc_ext, u_x, u_bc, dt, cum, y_loc, own_state, w_in, normed, norm_row = call(
-        functools.partial(forward_kernel, heads, n_in),
+    n_in, n_out = len(zx_pieces), len(out_pieces)
+
+    (
+        z, x_ext, bc_ext, u_x, u_bc, dt, cum, y_loc, own_state, w_in, x_perm, inv_in, normed, norm_row,
+    ) = call(
+        functools.partial(forward_kernel, pair, heads, head_n, n_in),
         [
             ((rows, inner), bf16),
             ((HALO + rows, inner), bf16),
@@ -688,42 +658,41 @@
             ((inner, state_n), f32),
             ((full_d, 2 * inner + wide_bcd), bf16),
             ((rows, full_d), bf16),
+            ((rows, LANES), f32),
+            ((rows, full_d), bf16),
             ((1, full_d), f32),
         ],
-        [x_perm, inv_in, edge, conv_x, conv_bc, params, *pieces],
+        [where, conv_x, conv_bc, params, *x_blocks, *zx_pieces, *bcd_pieces],
         [
             ((HALO + rows, full_d), bf16),
             ((HALO + rows, inner), f32),
             ((HALO + rows, wide_bc), f32),
+            ((head_n, HALO + rows, part_d), f32),
         ],
+        1,
     )
     total_decay = jnp.repeat(jnp.exp(cum[rows - 1, :heads]), inner // heads)[:, None]
     state_in = entering(total_decay, own_state, "seq", False)
-    grad_o, w_out_full, normed_t, cot_t = call(
-        functools.partial(cot_kernel, pair, head_n, n_out),
+    y, grad_o, stats, normed_t, cot_t, *out_blocks = call(
+        functools.partial(gate_kernel, pair, heads, head_n, n_out),
         [
             ((rows, inner), f32),
-            ((inner, full_d), bf16),
+            ((rows, inner), f32),
+            ((8, rows), f32),
             ((full_d, rows), bf16),
             ((full_d, rows), bf16),
+        ]
+        + [((rows, part_d), bf16)] * head_n,
+        [where, normed, state_in, u_bc, cum, y_loc, z, gain_row, *cot_blocks, *out_pieces],
+        [
+            ((head_n, rows, part_d), f32),
+            ((rows, full_d), bf16),
+            ((inner, full_d), bf16),
+            ((head_n, rows, part_d), bf16),
         ],
-        [where, normed, *cot_blocks, *out_pieces],
-        [((head_n, rows, part_d), f32), ((rows, full_d), bf16)],
         1,
     )
-    y, gated_raw, stats = call(
-        functools.partial(gate_kernel, heads),
-        [((rows, inner), f32), ((rows, inner), bf16), ((8, rows), f32)],
-        [state_in, u_bc, cum, y_loc, z, gain_row, grad_o],
-    )
     stats = exchanged(stats, "head")
-    out_blocks = call(
-        functools.partial(out_kernel, pair),
-        [((rows, part_d), bf16)] * head_n,
-        [where, gated_raw, w_out_full],
-        [((head_n, rows, part_d), bf16)],
-        1,
-    )
     out_parts = scattered(out_blocks, "head")
 
     dy, dz, from_cross, inv_gate, g_ggain, gated = call(
@@ -787,8 +756,15 @@
     blocks, (gx_own, gx_other, gb_own, gb_other) = results[:head_n], results[head_n:]
     if pair:
         early = reduced(early_own, early_other)
-        g_bcd = reduced(gb_own, gb_other, 2 * count)
-        g_x = reduced(gx_own, gx_other)
+        gb_recv = sent(gb_other, "seq", 1)
+        gx_recv = sent(gx_other, "seq", 1)
+        folded = call(
+            functools.partial(fold_kernel, dp_n),
+            [((shard + 2 * count, wide_bcd), bf16)] * dp_n + [((shard, inner), bf16)] * dp_n,
+            [gb_own, gb_recv, gx_own, gx_recv],
+        )
+        g_bcd = scattered(folded[:dp_n], "dp")
+        g_x = scattered(folded[dp_n:], "dp")
         g_dt, g_cx, g_head, g_ggain, shared = call(
             functools.partial(small_kernel, taps, heads, dp_n),
             [
@@ -796,7 +772,7 @@
                 ((n, inner), f32),
                 ((3, heads), f32),
                 ((1, inner), f32),
-                ((shard + 16, wide_bcd), bf16),
+                ((shard + 16, wide_bc), bf16),
             ],
             g_bcd,
         )
@@ -829,7 +805,7 @@
     shared = exchanged(shared, "head")
     if pair:
         g_bc, g_cbc, g_ngain = call(
-            functools.partial(shared_kernel, heads, head_n),
+            functools.partial(shared_kernel, head_n),
             [((shard, wide_bc), f32), ((n, wide_bc), f32), ((1, shard), f32)],
             shared,
         )

time: 151 us -> 152 us (level)
  waiting for transfers between devices: 32.3 us -> 44.5 us
  Pallas kernels: 48.6 us -> 41.2 us
  starting transfers between devices: 61.1 us -> 57.2 us
    ppermute x44 -> x51, waiting for transfers between devices: 30.4 us -> 40.5 us  [sent(): return lax.ppermute(block, axis, xor_route(lax.axis_size(axis), k))]
    pallas_call x14 -> x11, Pallas kernels: 48.6 us -> 41.2 us  [call(): pl.pallas_call(kernel, out_shape=[jax.ShapeDtypeStruct(shape, kind) for s...]
    ppermute x44 -> x51, starting transfers between devices: 55.8 us -> 51.9 us  [sent(): return lax.ppermute(block, axis, xor_route(lax.axis_size(axis), k))]
    ppermute x4, waiting for transfers between devices: 1.87 us -> 3.95 us  [passed_along(): return lax.ppermute(block, axis, route)]
    unnamed x96 -> x127, local copies, waits for them, and re-layouts: 4.66 us -> 5.56 us
  transfers between devices with their start and end apart: 48 -> 55, of which waited for: 23 -> 23; matrix products, arithmetic and copies ran while one was open for 2% -> 2% of each run, Pallas kernels for 21% -> 15%
where the time goes in v2:
time: 152 us
  starting transfers between devices  57.2 us (38%)
  waiting for transfers between devices  44.5 us (29%)
  Pallas kernels  41.2 us (27%)
  local copies, waits for them, and re-layouts  6.39 us (4%)
    ppermute x51, starting transfers between devices, sent(): return lax.ppermute(block, axis, xor_route(lax.axis_size(axis), k))  51.9 us
    pallas_call x11, Pallas kernels, call(): pl.pallas_call(kernel, out_shape=[jax.ShapeDtypeStruct(shape, kind) for s...  41.2 us
    ppermute x51, waiting for transfers between devices, sent(): return lax.ppermute(block, axis, xor_route(lax.axis_size(axis), k))  40.5 us
    unnamed x127, local copies, waits for them, and re-layouts  5.56 us
    ppermute x4, starting transfers between devices, passed_along(): return lax.ppermute(block, axis, route)  5.33 us
    ppermute x4, waiting for transfers between devices, passed_along(): return lax.ppermute(block, axis, route)  3.95 us
  transfers between devices with their start and end apart: 55, of which 23 were waited for; matrix products, arithmetic and copies ran while one was open for 2% of the time, Pallas kernels for 15%

profile of v2, /device:TPU:0, one launch (start us, length us, event | category | flops | bytes accessed | tf_op | source)
XLA Modules:
  0.0 151.9 jit_solution(14296679996060365498)
XLA Ops:
  2.2 3.9 %collective-permute-start.13 = (bf16[128,384]{1,0:T(8,128)(2,1)}, bf16[128,384]{1,0:T(8,128)(2,1)S(1)}, u32[]{:S(2)}, u32[]{:S(2)}) collective-permute-start(bf16[128,384]{1,0:T(8,128)(2,1)} %get-tuple-element.81.refs_15_), channel_id=1, source_target_pairs={{0,24},{8,16},{16,8},{24,0},{1,25},{9,17},{17,9},{25,1},{2,26},{10... | collective-permute-start | bytes 294920 | tf_op jit(solution)/shard_map/ppermute | solution.py:24
  9.2 2.0 %collective-permute-done.12.refs_17_ = bf16[128,384]{1,0:T(8,128)(2,1)S(1)} collective-permute-done((bf16[128,384]{1,0:T(8,128)(2,1)}, bf16[128,384]{1,0:T(8,128)(2,1)S(1)}, u32[]{:S(2)}, u32[]{:S(2)}) %collective-permute-start.12) | collective-permute-done | bytes 98336 | tf_op jit(solution)/shard_map/ppermute | solution.py:24
  18.3 3.6 %collective-permute-start.3 = (bf16[272,256]{1,0:T(8,128)(2,1)S(1)}, bf16[272,256]{1,0:T(8,128)(2,1)S(1)}, u32[]{:S(2)}, u32[]{:S(2)}) collective-permute-start(bf16[272,256]{1,0:T(8,128)(2,1)S(1)} %pad_maximum_fusion.refs_3_), channel_id=1, source_target_pairs={{0,3},{1,2},{2,1},{3,0},{4,7},{5,6},{6,5},{7,4},{8,11},{9,10},{10,... | collective-permute-start | bytes 417800 | tf_op jit(solution)/shard_map/ppermute | solution.py:24
  22.0 1.6 %collective-permute-done.6.refs_10_ = bf16[128,1024]{1,0:T(8,128)(2,1)S(1)} collective-permute-done((bf16[128,1024]{1,0:T(8,128)(2,1)S(1)}, bf16[128,1024]{1,0:T(8,128)(2,1)S(1)}, u32[]{:S(2)}, u32[]{:S(2)}) %collective-permute-start.6) | collective-permute-done | bytes 262176 | tf_op jit(solution)/shard_map/ppermute | solution.py:24
  25.2 2.6 %collective-permute-done.5.refs_9_ = bf16[128,1024]{1,0:T(8,128)(2,1)S(1)} collective-permute-done((bf16[128,1024]{1,0:T(8,128)(2,1)S(1)}, bf16[128,1024]{1,0:T(8,128)(2,1)S(1)}, u32[]{:S(2)}, u32[]{:S(2)}) %collective-permute-start.5) | collective-permute-done | bytes 262176 | tf_op jit(solution)/shard_map/ppermute | solution.py:24
  28.6 5.6 %collective-permute-done.2.refs_5_ = bf16[272,256]{1,0:T(8,128)(2,1)S(1)} collective-permute-done((bf16[272,256]{1,0:T(8,128)(2,1)S(1)}, bf16[272,256]{1,0:T(8,128)(2,1)S(1)}, u32[]{:S(2)}, u32[]{:S(2)}) %collective-permute-start.2) | collective-permute-done | bytes 139296 | tf_op jit(solution)/shard_map/ppermute | solution.py:24
  34.1 2.5 %collective-permute-start.21 = (bf16[256,256]{1,0:T(8,128)(2,1)}, bf16[256,256]{1,0:T(8,128)(2,1)S(1)}, u32[]{:S(2)}, u32[]{:S(2)}) collective-permute-start(bf16[256,256]{1,0:T(8,128)(2,1)} %bitcast.18), channel_id=1, source_target_pairs={{0,3},{1,2},{2,1},{3,0},{4,7},{5,6},{6,5},{7,4},{8,11},{9,10},{10,... | collective-permute-start | bytes 393224 | tf_op jit(solution)/shard_map/ppermute | solution.py:24
  36.8 1.9 %collective-permute-start.19 = (bf16[256,256]{1,0:T(8,128)(2,1)}, bf16[256,256]{1,0:T(8,128)(2,1)S(1)}, u32[]{:S(2)}, u32[]{:S(2)}) collective-permute-start(bf16[256,256]{1,0:T(8,128)(2,1)} %bitcast.20), channel_id=1, source_target_pairs={{0,1},{1,0},{2,3},{3,2},{4,5},{5,4},{6,7},{7,6},{8,9},{9,8},{10,11... | collective-permute-start | bytes 393224 | tf_op jit(solution)/shard_map/ppermute | solution.py:24
  41.5 6.2 %shard_map.195 = (bf16[256,512]{1,0:T(8,128)(2,1)}, bf16[272,512]{1,0:T(8,128)(2,1)}, bf16[272,256]{1,0:T(8,128)(2,1)}, f32[256,512]{1,0:T(8,128)}, f32[256,256]...) custom-call(s32[1]{0:T(128)} %bitcast.where, ...), custom_call_target="tpu_custom_call" | custom-call | tf_op jit(solution)/shard_map/pallas_call | solution.py:580
  50.7 2.1 %collective-permute-done.22.refs_12_ = bf16[512,128]{1,0:T(8,128)(2,1)S(1)} collective-permute-done((bf16[512,128]{1,0:T(8,128)(2,1)S(1)}, bf16[512,128]{1,0:T(8,128)(2,1)S(1)}, u32[]{:S(2)}, u32[]{:S(2)}) %collective-permute-start.22) | collective-permute-done | bytes 131104 | tf_op jit(solution)/shard_map/ppermute | solution.py:24
  54.9 4.3 %shard_map.196 = (f32[256,512]{1,0:T(8,128)}, f32[256,512]{1,0:T(8,128)}, f32[8,256]{1,0:T(8,128)}, bf16[1024,256]{1,0:T(8,128)(2,1)}, bf16[1024,256]{1,0:T(8,12...) custom-call(s32[1]{0:T(128)} %bitcast.where, ...), custom_call_target="tpu_custom_call" | custom-call | tf_op jit(solution)/shard_map/pallas_call | solution.py:580
  59.2 2.5 %collective-permute-start.31 = (f32[8,256]{1,0:T(8,128)}, f32[8,256]{1,0:T(8,128)S(1)}, u32[]{:S(2)}, u32[]{:S(2)}) collective-permute-start(f32[8,256]{1,0:T(8,128)} %get-tuple-element.88.refs_0_), channel_id=1, source_target_pairs={{0,3},{1,2},{2,1},{3,0},{4,7},{5,6},{6,5},{7,4},{8,11},{9,10},{10,... | collective-permute-start | bytes 24584 | tf_op jit(solution)/shard_map/ppermute | solution.py:24
  61.7 1.9 %collective-permute-start.29 = (f32[8,256]{1,0:T(8,128)}, f32[8,256]{1,0:T(8,128)S(1)}, u32[]{:S(2)}, u32[]{:S(2)}) collective-permute-start(f32[8,256]{1,0:T(8,128)} %get-tuple-element.88.refs_0_), channel_id=1, source_target_pairs={{0,1},{1,0},{2,3},{3,2},{4,5},{5,4},{6,7},{7,6},{8,9},{9,8},{10,11... | collective-permute-start | bytes 24584 | tf_op jit(solution)/shard_map/ppermute | solution.py:24
  67.1 3.2 %shard_map.197 = (f32[256,512]{1,0:T(8,128)}, bf16[256,512]{1,0:T(8,128)(2,1)}, f32[512,128]{1,0:T(8,128)}, f32[256,128]{1,0:T(8,128)}, f32[1,512]{1,0:T(1,128)}, /*index=5*/bf16[256,512]{1,0:T(8,128)(2,1)}) custom-call(f32[8,256]{1,0:T(8,128)} %get-tuple-element.88.refs_0_, f32[8,256]{1,0:T(8,128)} %copy-done.57, f32[8,256]{1,0:T(8,128)} %copy-done.56, ...), custom_call_target="tpu_custom_call" | custom-call | tf_op jit(solution)/shard_map/pallas_call | solution.py:580
  70.3 5.6 %shard_map.198 = (f32[256,512]{1,0:T(8,128)}, f32[256,256]{1,0:T(8,128)}, f32[256,128]{1,0:T(8,128)}, bf16[512,1024]{1,0:T(8,128)(2,1)}, bf16[512,1024]{1,0:T(8,128)(2,1)}) custom-call(f32[256,512]{1,0:T(8,128)} %get-tuple-element.92.dy_ref, bf16[256,512]{1,0:T(8,128)(2,1)} %get-tuple-element.93.dz.refs_5_, ...), custom_call_target="tpu_custom_call" | custom-call | tf_op jit(solution)/shard_map/pallas_call | solution.py:580
  77.4 1.9 %collective-permute-done.32.next_ref = f32[512,128]{1,0:T(8,128)S(1)} collective-permute-done((f32[512,128]{1,0:T(8,128)S(1)}, f32[512,128]{1,0:T(8,128)S(1)}, u32[]{:S(2)}, u32[]{:S(2)}) %collective-permute-start.32) | collective-permute-done | bytes 262176 | tf_op jit(solution)/shard_map/ppermute | solution.py:46
  80.0 4.3 %shard_map.199 = (f32[256,512]{1,0:T(8,128)}, f32[256,256]{1,0:T(8,128)}, f32[8,768]{1,0:T(8,128)}, bf16[256,128]{1,0:T(8,128)(2,1)}, f32[8,128]{1,0:T(8,128)}) custom-call(f32[512,128]{1,0:T(8,128)} %copy-done.13, f32[256,512]{1,0:T(8,128)} %get-tuple-element.99.dxs, f32[256,256]{1,0:T(8,128)} %get-tuple-element.100.dbc, ...), custom_call_target="tpu_custom_call" | custom-call | tf_op jit(solution)/shard_map/pallas_call | solution.py:580
  85.6 2.0 %collective-permute-done.33.refs_0_ = f32[8,768]{1,0:T(8,128)S(1)} collective-permute-done((f32[8,768]{1,0:T(8,128)}, f32[8,768]{1,0:T(8,128)S(1)}, u32[]{:S(2)}, u32[]{:S(2)}) %collective-permute-start.33) | collective-permute-done | bytes 24608 | tf_op jit(solution)/shard_map/ppermute | solution.py:46
  88.2 6.5 %shard_map.200 = (bf16[272,256]{1,0:T(8,128)(2,1)}, bf16[272,256]{1,0:T(8,128)(2,1)}, bf16[272,256]{1,0:T(8,128)(2,1)}, bf16[272,256]{1,0:T(8,128)(2,1)}, bf16[5...) custom-call(s32[1]{0:T(128)} %bitcast.where, ...), custom_call_target="tpu_custom_call" | custom-call | tf_op jit(solution)/shard_map/pallas_call | solution.py:580
  95.3 2.2 %collective-permute-done.44.other = bf16[560,384]{1,0:T(8,128)(2,1)S(1)} collective-permute-done((bf16[560,384]{1,0:T(8,128)(2,1)}, bf16[560,384]{1,0:T(8,128)(2,1)S(1)}, u32[]{:S(2)}, u32[]{:S(2)}) %collective-permute-start.44) | collective-permute-done | bytes 430112 | tf_op jit(solution)/shard_map/ppermute | solution.py:24
  98.4 2.5 %shard_map.201 = (bf16[176,384]{1,0:T(8,128)(2,1)}, bf16[176,384]{1,0:T(8,128)(2,1)}, bf16[176,384]{1,0:T(8,128)(2,1)}, bf16[176,384]{1,0:T(8,128)(2,1)}, bf16[1...) custom-call(bf16[560,384]{1,0:T(8,128)(2,1)} %get-tuple-element.124.own, ...), custom_call_target="tpu_custom_call" | custom-call | tf_op jit(solution)/shard_map/pallas_call | solution.py:580
  105.4 2.2 %collective-permute-done.49.refs_1_ = bf16[176,384]{1,0:T(8,128)(2,1)S(1)} collective-permute-done((bf16[176,384]{1,0:T(8,128)(2,1)}, bf16[176,384]{1,0:T(8,128)(2,1)S(1)}, u32[]{:S(2)}, u32[]{:S(2)}) %collective-permute-start.49) | collective-permute-done | bytes 135200 | tf_op jit(solution)/shard_map/ppermute | solution.py:24
  107.6 2.0 %collective-permute-start.38 = (bf16[256,256]{1,0:T(8,128)(2,1)}, bf16[256,256]{1,0:T(8,128)(2,1)S(1)}, u32[]{:S(2)}, u32[]{:S(2)}) collective-permute-start(bf16[256,256]{1,0:T(8,128)(2,1)} %get-tuple-element.120), channel_id=1, source_target_pairs={{0,2},{1,3},{2,0},{3,1},{4,6},{5,7},{6,4},{7,5},{8,10},{9,11},{10,... | collective-permute-start | bytes 393224 | tf_op jit(solution)/shard_map/ppermute | solution.py:24
  112.9 1.9 %shard_map.203 = (f32[8,128]{1,0:T(8,128)}, f32[5,512]{1,0:T(8,128)}, f32[3,8]{1,0:T(4,128)}, f32[1,512]{1,0:T(1,128)}, bf16[144,256]{1,0:T(8,128)(2,1)}) custom-call(bf16[176,384]{1,0:T(8,128)(2,1)} %get-tuple-element.135.refs_0_, bf16[176,384]{1,0:T(8,128)(2,1)} %copy-done.23, bf16[176,384]{1,0:T(8,128)(2,1)} %copy-done.24, bf16[176,384]{1,0:T(8,128)(2,1)} %copy-done.25), custom_call_target="tpu_custom_call" | custom-call | tf_op jit(solution)/shard_map/pallas_call | solution.py:580
  114.8 1.9 %collective-permute-start.35 = (bf16[272,256]{1,0:T(8,128)(2,1)S(1)}, bf16[272,256]{1,0:T(8,128)(2,1)S(1)}, u32[]{:S(2)}, u32[]{:S(2)}) collective-permute-start(bf16[272,256]{1,0:T(8,128)(2,1)S(1)} %copy-done.60), channel_id=1, source_target_pairs={{0,2},{1,3},{2,0},{3,1},{4,6},{5,7},{6,4},{7,5},{8,10},{9,11},{10,... | collective-permute-start | bytes 417800 | tf_op jit(solution)/shard_map/ppermute | solution.py:24
  118.7 2.5 %collective-permute-done.38.refs_6_ = bf16[256,256]{1,0:T(8,128)(2,1)S(1)} collective-permute-done((bf16[256,256]{1,0:T(8,128)(2,1)}, bf16[256,256]{1,0:T(8,128)(2,1)S(1)}, u32[]{:S(2)}, u32[]{:S(2)}) %collective-permute-start.38) | collective-permute-done | bytes 131104 | tf_op jit(solution)/shard_map/ppermute | solution.py:24
  122.0 2.5 %collective-permute-start.54 = (bf16[144,256]{1,0:T(8,128)(2,1)S(1)}, bf16[144,256]{1,0:T(8,128)(2,1)S(1)}, u32[]{:S(2)}, u32[]{:S(2)}) collective-permute-start(bf16[144,256]{1,0:T(8,128)(2,1)S(1)} %copy-done.50), channel_id=1, source_target_pairs={{0,3},{1,2},{2,1},{3,0},{4,7},{5,6},{6,5},{7,4},{8,11},{9,10},{10,... | collective-permute-start | bytes 221192 | tf_op jit(solution)/shard_map/ppermute | solution.py:24
  126.5 6.4 %collective-permute-done.35.refs_2_ = bf16[272,256]{1,0:T(8,128)(2,1)S(1)} collective-permute-done((bf16[272,256]{1,0:T(8,128)(2,1)S(1)}, bf16[272,256]{1,0:T(8,128)(2,1)S(1)}, u32[]{:S(2)}, u32[]{:S(2)}) %collective-permute-start.35) | collective-permute-done | bytes 139296 | tf_op jit(solution)/shard_map/ppermute | solution.py:24
  137.6 3.0 %collective-permute-done.53.refs_2_ = bf16[144,256]{1,0:T(8,128)(2,1)S(1)} collective-permute-done((bf16[144,256]{1,0:T(8,128)(2,1)S(1)}, bf16[144,256]{1,0:T(8,128)(2,1)S(1)}, u32[]{:S(2)}, u32[]{:S(2)}) %collective-permute-start.53) | collective-permute-done | bytes 73760 | tf_op jit(solution)/shard_map/ppermute | solution.py:24
  142.7 1.7 %shard_map.204 = (f32[128,256]{1,0:T(8,128)}, f32[5,256]{1,0:T(8,128)}, f32[1,128]{1,0:T(1,128)}) custom-call(bf16[144,256]{1,0:T(8,128)(2,1)} %get-tuple-element.139.refs_0_, bf16[144,256]{1,0:T(8,128)(2,1)} %copy-done.53, bf16[144,256]{1,0:T(8,128)(2,1)} %copy-done.52, bf16[144,256]{1,0:T(8,128)(2,1)} %copy-done.51), custom_call_target="tpu_custom_call" | custom-call | tf_op jit(solution)/shard_map/pallas_call | solution.py:580
  145.8 1.7 %collective-permute-done.48.refs_15_ = bf16[128,512]{1,0:T(8,128)(2,1)S(1)} collective-permute-done((bf16[128,512]{1,0:T(8,128)(2,1)}, bf16[128,512]{1,0:T(8,128)(2,1)S(1)}, u32[]{:S(2)}, u32[]{:S(2)}) %collective-permute-start.48) | collective-permute-done | bytes 131104 | tf_op jit(solution)/shard_map/ppermute | solution.py:24
  148.4 3.5 %shard_map.202 = (bf16[256,256]{1,0:T(8,128)(2,1)}, bf16[256,256]{1,0:T(8,128)(2,1)}, f32[128,2,512]{2,1,0:T(2,128)}, f32[512,128]{1,0:T(8,128)}) custom-call(s32[1]{0:T(128)} %bitcast.where, bf16[272,256]{1,0:T(8,128)(2,1)} %get-tuple-element.114.refs_0_, bf16[272,256]{1,0:T(8,128)(2,1)} %copy-done.20, bf16[272,256]{1,0:T(8,128)(2,1)} %copy-done.21, ...), custom_call_target="tpu_custom_call" | custom-call | tf_op jit(solution)/shard_map/pallas_call | solution.py:580
  (220 shorter events, 52.4 us)
Async XLA Ops:
  2.2 7.0 %collective-permute-start.13 = (bf16[128,384]{1,0:T(8,128)(2,1)}, bf16[128,384]{1,0:T(8,128)(2,1)S(1)}, u32[]{:S(2)}, u32[]{:S(2)}) collective-permute-start(bf16[128,384]{1,0:T(8,128)(2,1)} %get-tuple-element.81.refs_15_), channel_id=1, source_target_pairs={{0,24},{8,16},{16,8},{24,0},{1,25},{9,17},{17,9},{25,1},{2,26},{10... | collective-permute-start | bytes 294920 | tf_op jit(solution)/shard_map/ppermute | solution.py:24
  6.7 8.3 %collective-permute-start = (bf16[256,256]{1,0:T(8,128)(2,1)}, bf16[256,256]{1,0:T(8,128)(2,1)S(1)}, u32[]{:S(2)}, u32[]{:S(2)}) collective-permute-start(bf16[256,256]{1,0:T(8,128)(2,1)} %bitcast.23), channel_id=1, source_target_pairs={{0,4},{1,5},{2,6},{3,7},{8,12},{9,13},{10,14},{11,15},{16,20},{17,... | collective-permute-start | bytes 393224 | tf_op jit(solution)/shard_map/ppermute | solution.py:46
  9.2 6.8 %collective-permute-start.17 = (bf16[128,384]{1,0:T(8,128)(2,1)S(1)}, bf16[128,384]{1,0:T(8,128)(2,1)S(1)}, u32[]{:S(2)}, u32[]{:S(2)}) collective-permute-start(bf16[128,384]{1,0:T(8,128)(2,1)S(1)} %collective-permute-done.13.refs_18_), channel_id=1, source_target_pairs={{0,4},{4,0},{1,5},{5,1},{2,6},{6,2},{3,7},{7,3},{8,12},{12,8},{9,1... | collective-permute-start | bytes 294920 | tf_op jit(solution)/shard_map/ppermute | solution.py:24
  12.4 9.6 %collective-permute-start.7 = (bf16[128,1024]{1,0:T(8,128)(2,1)S(1)}, bf16[128,1024]{1,0:T(8,128)(2,1)S(1)}, u32[]{:S(2)}, u32[]{:S(2)}) collective-permute-start(bf16[128,1024]{1,0:T(8,128)(2,1)S(1)} %bitcast.13), channel_id=1, source_target_pairs={{0,4},{4,0},{1,5},{5,1},{2,6},{6,2},{3,7},{7,3},{8,12},{12,8},{9,1... | collective-permute-start | bytes 786440 | tf_op jit(solution)/shard_map/ppermute | solution.py:24
  13.5 10.1 %collective-permute-start.6 = (bf16[128,1024]{1,0:T(8,128)(2,1)S(1)}, bf16[128,1024]{1,0:T(8,128)(2,1)S(1)}, u32[]{:S(2)}, u32[]{:S(2)}) collective-permute-start(bf16[128,1024]{1,0:T(8,128)(2,1)S(1)} %bitcast.14), channel_id=1, source_target_pairs={{0,24},{8,16},{16,8},{24,0},{1,25},{9,17},{17,9},{25,1},{2,26},{10... | collective-permute-start | bytes 786440 | tf_op jit(solution)/shard_map/ppermute | solution.py:24
  15.0 12.8 %collective-permute-start.5 = (bf16[128,1024]{1,0:T(8,128)(2,1)S(1)}, bf16[128,1024]{1,0:T(8,128)(2,1)S(1)}, u32[]{:S(2)}, u32[]{:S(2)}) collective-permute-start(bf16[128,1024]{1,0:T(8,128)(2,1)S(1)} %bitcast.15), channel_id=1, source_target_pairs={{0,16},{8,24},{16,0},{24,8},{1,17},{9,25},{17,1},{25,9},{2,18},{10... | collective-permute-start | bytes 786440 | tf_op jit(solution)/shard_map/ppermute | solution.py:24
  16.1 12.0 %collective-permute-start.4 = (bf16[128,1024]{1,0:T(8,128)(2,1)S(1)}, bf16[128,1024]{1,0:T(8,128)(2,1)S(1)}, u32[]{:S(2)}, u32[]{:S(2)}) collective-permute-start(bf16[128,1024]{1,0:T(8,128)(2,1)S(1)} %bitcast.16), channel_id=1, source_target_pairs={{0,8},{8,0},{16,24},{24,16},{1,9},{9,1},{17,25},{25,17},{2,10},{10... | collective-permute-start | bytes 786440 | tf_op jit(solution)/shard_map/ppermute | solution.py:24
  18.3 9.9 %collective-permute-start.3 = (bf16[272,256]{1,0:T(8,128)(2,1)S(1)}, bf16[272,256]{1,0:T(8,128)(2,1)S(1)}, u32[]{:S(2)}, u32[]{:S(2)}) collective-permute-start(bf16[272,256]{1,0:T(8,128)(2,1)S(1)} %pad_maximum_fusion.refs_3_), channel_id=1, source_target_pairs={{0,3},{1,2},{2,1},{3,0},{4,7},{5,6},{6,5},{7,4},{8,11},{9,10},{10,... | collective-permute-start | bytes 417800 | tf_op jit(solution)/shard_map/ppermute | solution.py:24
  22.0 12.2 %collective-permute-start.2 = (bf16[272,256]{1,0:T(8,128)(2,1)S(1)}, bf16[272,256]{1,0:T(8,128)(2,1)S(1)}, u32[]{:S(2)}, u32[]{:S(2)}) collective-permute-start(bf16[272,256]{1,0:T(8,128)(2,1)S(1)} %pad_maximum_fusion.refs_3_), channel_id=1, source_target_pairs={{0,2},{1,3},{2,0},{3,1},{4,6},{5,7},{6,4},{7,5},{8,10},{9,11},{10,... | collective-permute-start | bytes 417800 | tf_op jit(solution)/shard_map/ppermute | solution.py:24
  23.6 13.1 %collective-permute-start.1 = (bf16[272,256]{1,0:T(8,128)(2,1)S(1)}, bf16[272,256]{1,0:T(8,128)(2,1)S(1)}, u32[]{:S(2)}, u32[]{:S(2)}) collective-permute-start(bf16[272,256]{1,0:T(8,128)(2,1)S(1)} %pad_maximum_fusion.refs_3_), channel_id=1, source_target_pairs={{0,1},{1,0},{2,3},{3,2},{4,5},{5,4},{6,7},{7,6},{8,9},{9,8},{10,11... | collective-permute-start | bytes 417800 | tf_op jit(solution)/shard_map/ppermute | solution.py:24
  27.8 9.0 %collective-permute-start.10 = (bf16[128,1024]{1,0:T(8,128)(2,1)S(1)}, bf16[128,1024]{1,0:T(8,128)(2,1)S(1)}, u32[]{:S(2)}, u32[]{:S(2)}) collective-permute-start(bf16[128,1024]{1,0:T(8,128)(2,1)S(1)} %collective-permute-done.6.refs_10_), channel_id=1, source_target_pairs={{0,4},{4,0},{1,5},{5,1},{2,6},{6,2},{3,7},{7,3},{8,12},{12,8},{9,1... | collective-permute-start | bytes 786440 | tf_op jit(solution)/shard_map/ppermute | solution.py:24
  28.0 10.7 %collective-permute-start.9 = (bf16[128,1024]{1,0:T(8,128)(2,1)S(1)}, bf16[128,1024]{1,0:T(8,128)(2,1)S(1)}, u32[]{:S(2)}, u32[]{:S(2)}) collective-permute-start(bf16[128,1024]{1,0:T(8,128)(2,1)S(1)} %collective-permute-done.5.refs_9_), channel_id=1, source_target_pairs={{0,4},{4,0},{1,5},{5,1},{2,6},{6,2},{3,7},{7,3},{8,12},{12,8},{9,1... | collective-permute-start | bytes 786440 | tf_op jit(solution)/shard_map/ppermute | solution.py:24
  28.3 12.0 %collective-permute-start.8 = (bf16[128,1024]{1,0:T(8,128)(2,1)S(1)}, bf16[128,1024]{1,0:T(8,128)(2,1)S(1)}, u32[]{:S(2)}, u32[]{:S(2)}) collective-permute-start(bf16[128,1024]{1,0:T(8,128)(2,1)S(1)} %collective-permute-done.4.refs_8_), channel_id=1, source_target_pairs={{0,4},{4,0},{1,5},{5,1},{2,6},{6,2},{3,7},{7,3},{8,12},{12,8},{9,1... | collective-permute-start | bytes 786440 | tf_op jit(solution)/shard_map/ppermute | solution.py:24
  34.1 13.6 %collective-permute-start.21 = (bf16[256,256]{1,0:T(8,128)(2,1)}, bf16[256,256]{1,0:T(8,128)(2,1)S(1)}, u32[]{:S(2)}, u32[]{:S(2)}) collective-permute-start(bf16[256,256]{1,0:T(8,128)(2,1)} %bitcast.18), channel_id=1, source_target_pairs={{0,3},{1,2},{2,1},{3,0},{4,7},{5,6},{6,5},{7,4},{8,11},{9,10},{10,... | collective-permute-start | bytes 393224 | tf_op jit(solution)/shard_map/ppermute | solution.py:24
  36.7 12.1 %collective-permute-start.20 = (bf16[256,256]{1,0:T(8,128)(2,1)}, bf16[256,256]{1,0:T(8,128)(2,1)S(1)}, u32[]{:S(2)}, u32[]{:S(2)}) collective-permute-start(bf16[256,256]{1,0:T(8,128)(2,1)} %bitcast.19), channel_id=1, source_target_pairs={{0,2},{1,3},{2,0},{3,1},{4,6},{5,7},{6,4},{7,5},{8,10},{9,11},{10,... | collective-permute-start | bytes 393224 | tf_op jit(solution)/shard_map/ppermute | solution.py:24
  36.8 13.3 %collective-permute-start.19 = (bf16[256,256]{1,0:T(8,128)(2,1)}, bf16[256,256]{1,0:T(8,128)(2,1)S(1)}, u32[]{:S(2)}, u32[]{:S(2)}) collective-permute-start(bf16[256,256]{1,0:T(8,128)(2,1)} %bitcast.20), channel_id=1, source_target_pairs={{0,1},{1,0},{2,3},{3,2},{4,5},{5,4},{6,7},{7,6},{8,9},{9,8},{10,11... | collective-permute-start | bytes 393224 | tf_op jit(solution)/shard_map/ppermute | solution.py:24
  38.7 11.4 %collective-permute-start.24 = (bf16[512,128]{1,0:T(8,128)(2,1)}, bf16[512,128]{1,0:T(8,128)(2,1)S(1)}, u32[]{:S(2)}, u32[]{:S(2)}) collective-permute-start(bf16[512,128]{1,0:T(8,128)(2,1)} %refs_11_.2), channel_id=1, source_target_pairs={{0,24},{8,16},{16,8},{24,0},{1,25},{9,17},{17,9},{25,1},{2,26},{10... | collective-permute-start | bytes 393224 | tf_op jit(solution)/shard_map/ppermute | solution.py:24
  40.3 10.4 %collective-permute-start.23 = (bf16[512,128]{1,0:T(8,128)(2,1)}, bf16[512,128]{1,0:T(8,128)(2,1)S(1)}, u32[]{:S(2)}, u32[]{:S(2)}) collective-permute-start(bf16[512,128]{1,0:T(8,128)(2,1)} %refs_11_.2), channel_id=1, source_target_pairs={{0,16},{8,24},{16,0},{24,8},{1,17},{9,25},{17,1},{25,9},{2,18},{10... | collective-permute-start | bytes 393224 | tf_op jit(solution)/shard_map/ppermute | solution.py:24
  75.9 38.9 %collective-permute-start.40 = (bf16[512,1024]{1,0:T(8,128)(2,1)}, bf16[512,1024]{1,0:T(8,128)(2,1)S(1)}, u32[]{:S(2)}, u32[]{:S(2)}) collective-permute-start(bf16[512,1024]{1,0:T(8,128)(2,1)} %get-tuple-element.123), channel_id=1, source_target_pairs={{0,4},{4,0},{1,5},{5,1},{2,6},{6,2},{3,7},{7,3},{8,12},{12,8},{9,1... | collective-permute-start | bytes 3145736 | tf_op jit(solution)/shard_map/ppermute | solution.py:24
  101.8 8.5 %collective-permute-start.50 = (bf16[176,384]{1,0:T(8,128)(2,1)}, bf16[176,384]{1,0:T(8,128)(2,1)S(1)}, u32[]{:S(2)}, u32[]{:S(2)}) collective-permute-start(bf16[176,384]{1,0:T(8,128)(2,1)} %get-tuple-element.137), channel_id=1, source_target_pairs={{0,16},{8,24},{16,0},{24,8},{1,17},{9,25},{17,1},{25,9},{2,18},{10... | collective-permute-start | bytes 405512 | tf_op jit(solution)/shard_map/ppermute | solution.py:24
  103.3 8.5 %collective-permute-start.51 = (bf16[176,384]{1,0:T(8,128)(2,1)}, bf16[176,384]{1,0:T(8,128)(2,1)S(1)}, u32[]{:S(2)}, u32[]{:S(2)}) collective-permute-start(bf16[176,384]{1,0:T(8,128)(2,1)} %get-tuple-element.138), channel_id=1, source_target_pairs={{0,24},{8,16},{16,8},{24,0},{1,25},{9,17},{17,9},{25,1},{2,26},{10... | collective-permute-start | bytes 405512 | tf_op jit(solution)/shard_map/ppermute | solution.py:24
  104.4 12.7 %collective-permute-start.37 = (bf16[256,256]{1,0:T(8,128)(2,1)}, bf16[256,256]{1,0:T(8,128)(2,1)S(1)}, u32[]{:S(2)}, u32[]{:S(2)}) collective-permute-start(bf16[256,256]{1,0:T(8,128)(2,1)} %get-tuple-element.119), channel_id=1, source_target_pairs={{0,1},{1,0},{2,3},{3,2},{4,5},{5,4},{6,7},{7,6},{8,9},{9,8},{10,11... | collective-permute-start | bytes 393224 | tf_op jit(solution)/shard_map/ppermute | solution.py:24
  107.6 13.6 %collective-permute-start.38 = (bf16[256,256]{1,0:T(8,128)(2,1)}, bf16[256,256]{1,0:T(8,128)(2,1)S(1)}, u32[]{:S(2)}, u32[]{:S(2)}) collective-permute-start(bf16[256,256]{1,0:T(8,128)(2,1)} %get-tuple-element.120), channel_id=1, source_target_pairs={{0,2},{1,3},{2,0},{3,1},{4,6},{5,7},{6,4},{7,5},{8,10},{9,11},{10,... | collective-permute-start | bytes 393224 | tf_op jit(solution)/shard_map/ppermute | solution.py:24
  110.3 11.7 %collective-permute-start.39 = (bf16[256,256]{1,0:T(8,128)(2,1)S(1)}, bf16[256,256]{1,0:T(8,128)(2,1)S(1)}, u32[]{:S(2)}, u32[]{:S(2)}) collective-permute-start(bf16[256,256]{1,0:T(8,128)(2,1)S(1)} %copy-done.61), channel_id=1, source_target_pairs={{0,3},{1,2},{2,1},{3,0},{4,7},{5,6},{6,5},{7,4},{8,11},{9,10},{10,... | collective-permute-start | bytes 393224 | tf_op jit(solution)/shard_map/ppermute | solution.py:24
  111.8 13.5 %collective-permute-start.34 = (bf16[272,256]{1,0:T(8,128)(2,1)}, bf16[272,256]{1,0:T(8,128)(2,1)S(1)}, u32[]{:S(2)}, u32[]{:S(2)}) collective-permute-start(bf16[272,256]{1,0:T(8,128)(2,1)} %get-tuple-element.115), channel_id=1, source_target_pairs={{0,1},{1,0},{2,3},{3,2},{4,5},{5,4},{6,7},{7,6},{8,9},{9,8},{10,11... | collective-permute-start | bytes 417800 | tf_op jit(solution)/shard_map/ppermute | solution.py:24
  114.8 18.1 %collective-permute-start.35 = (bf16[272,256]{1,0:T(8,128)(2,1)S(1)}, bf16[272,256]{1,0:T(8,128)(2,1)S(1)}, u32[]{:S(2)}, u32[]{:S(2)}) collective-permute-start(bf16[272,256]{1,0:T(8,128)(2,1)S(1)} %copy-done.60), channel_id=1, source_target_pairs={{0,2},{1,3},{2,0},{3,1},{4,6},{5,7},{6,4},{7,5},{8,10},{9,11},{10,... | collective-permute-start | bytes 417800 | tf_op jit(solution)/shard_map/ppermute | solution.py:24
  117.1 16.7 %collective-permute-start.36 = (bf16[272,256]{1,0:T(8,128)(2,1)S(1)}, bf16[272,256]{1,0:T(8,128)(2,1)S(1)}, u32[]{:S(2)}, u32[]{:S(2)}) collective-permute-start(bf16[272,256]{1,0:T(8,128)(2,1)S(1)} %copy-done.59), channel_id=1, source_target_pairs={{0,3},{1,2},{2,1},{3,0},{4,7},{5,6},{6,5},{7,4},{8,11},{9,10},{10,... | collective-permute-start | bytes 417800 | tf_op jit(solution)/shard_map/ppermute | solution.py:24
  121.2 14.1 %collective-permute-start.46 = (bf16[128,512]{1,0:T(8,128)(2,1)S(1)}, bf16[128,512]{1,0:T(8,128)(2,1)S(1)}, u32[]{:S(2)}, u32[]{:S(2)}) collective-permute-start(bf16[128,512]{1,0:T(8,128)(2,1)S(1)} %copy-done.62), channel_id=1, source_target_pairs={{0,8},{8,0},{16,24},{24,16},{1,9},{9,1},{17,25},{25,17},{2,10},{10... | collective-permute-start | bytes 393224 | tf_op jit(solution)/shard_map/ppermute | solution.py:24
  122.0 14.8 %collective-permute-start.54 = (bf16[144,256]{1,0:T(8,128)(2,1)S(1)}, bf16[144,256]{1,0:T(8,128)(2,1)S(1)}, u32[]{:S(2)}, u32[]{:S(2)}) collective-permute-start(bf16[144,256]{1,0:T(8,128)(2,1)S(1)} %copy-done.50), channel_id=1, source_target_pairs={{0,3},{1,2},{2,1},{3,0},{4,7},{5,6},{6,5},{7,4},{8,11},{9,10},{10,... | collective-permute-start | bytes 221192 | tf_op jit(solution)/shard_map/ppermute | solution.py:24
  125.3 22.2 %collective-permute-start.43 = (bf16[128,1024]{1,0:T(8,128)(2,1)S(1)}, bf16[128,1024]{1,0:T(8,128)(2,1)S(1)}, u32[]{:S(2)}, u32[]{:S(2)}) collective-permute-start(bf16[128,1024]{1,0:T(8,128)(2,1)S(1)} %get-tuple-element.149), channel_id=1, source_target_pairs={{0,24},{8,16},{16,8},{24,0},{1,25},{9,17},{17,9},{25,1},{2,26},{10... | collective-permute-start | bytes 786440 | tf_op jit(solution)/shard_map/ppermute | solution.py:24
  132.9 14.6 %collective-permute-start.42 = (bf16[128,1024]{1,0:T(8,128)(2,1)S(1)}, bf16[128,1024]{1,0:T(8,128)(2,1)S(1)}, u32[]{:S(2)}, u32[]{:S(2)}) collective-permute-start(bf16[128,1024]{1,0:T(8,128)(2,1)S(1)} %get-tuple-element.150), channel_id=1, source_target_pairs={{0,16},{8,24},{16,0},{24,8},{1,17},{9,25},{17,1},{25,9},{2,18},{10... | collective-permute-start | bytes 786440 | tf_op jit(solution)/shard_map/ppermute | solution.py:24
  133.8 13.7 %collective-permute-start.41 = (bf16[128,1024]{1,0:T(8,128)(2,1)S(1)}, bf16[128,1024]{1,0:T(8,128)(2,1)S(1)}, u32[]{:S(2)}, u32[]{:S(2)}) collective-permute-start(bf16[128,1024]{1,0:T(8,128)(2,1)S(1)} %get-tuple-element.151), channel_id=1, source_target_pairs={{0,8},{8,0},{16,24},{24,16},{1,9},{9,1},{17,25},{25,17},{2,10},{10... | collective-permute-start | bytes 786440 | tf_op jit(solution)/shard_map/ppermute | solution.py:24
  (86 other events, 728.8 us)

commit v3 on v2

--- a/solution.py
+++ b/solution.py
@@ -423,17 +423,17 @@
     ggain, ghead = refs[14:16]
     blocks = refs[16 : 16 + n_blocks]
     gx_own, gx_other, gb_own, gb_other = refs[16 + n_blocks : 20 + n_blocks]
-    hold, gx_ext, gb_ext, x_ext, b_ext, small, grads = refs[20 + n_blocks :]
+    hold, gx_ext, gb_ext, small, grads = refs[20 + n_blocks :]
     rows, inner = gux.shape
     wide_bc = gubc.shape[1]
     taps = conv_x.shape[0] - 1
     small[...] = jnp.zeros(small.shape, f32)
 
-    def conv_back(grad, ext, raw_ref, raw_ext, weights, next_rows, firsts, width):
+    def conv_back(grad, ext, raw_ref, weights, next_rows, firsts, width):
         value = grad[...]
         ext[0:rows, :] = value
         ext[rows : rows + EDGE, :] = next_rows
-        raw_ext[...] = raw_ref[...].astype(f32)
+        before = raw_ref[HALO:, :].astype(f32)
 
         def kept(k, row):
             for j, first in enumerate(firsts):
@@ -442,15 +442,15 @@
         total = jnp.zeros((rows, width), f32)
         for k in range(taps):
             ahead = taps - 1 - k
-            total = total + weights[k : k + 1, :] * ext[ahead : ahead + rows, :]
-            back = HALO - taps + 1 + k
-            kept(k, jnp.sum(raw_ext[back : back + rows, :] * value, axis=0, keepdims=True))
+            later = ext[ahead : ahead + rows, :] if ahead > 0 else value
+            total = total + weights[k : k + 1, :] * later
+            kept(k, jnp.sum(before * later, axis=0, keepdims=True))
         kept(taps, jnp.sum(value, axis=0, keepdims=True))
         return total.astype(bf16)
 
     n = taps + 1
-    dx = conv_back(gux, gx_ext, xe, x_ext, conv_x, edge[:, 0:inner], (0, n), inner)
-    dbc = conv_back(gubc, gb_ext, be, b_ext, conv_bc, edge[:, inner:], (2 * n,), wide_bc)
+    dx = conv_back(gux, gx_ext, xe, conv_x, edge[:, 0:inner], (0, n), inner)
+    dbc = conv_back(gubc, gb_ext, be, conv_bc, edge[:, inner:], (2 * n,), wide_bc)
     for j in range(2):
         small[3 * n + j : 3 * n + j + 1, 0:wide_bc] = ggain[:, j * wide_bc : (j + 1) * wide_bc]
     small[3 * n + 2 : 3 * n + 5, 0:LANES] = ghead[0:3, :]
@@ -746,8 +746,6 @@
             ((head_n, rows, part_d), bf16),
             ((rows + EDGE, inner), f32),
             ((rows + EDGE, wide_bc), f32),
-            ((HALO + rows, inner), f32),
-            ((HALO + rows, wide_bc), f32),
             ((count, wide_bcd), f32),
             ((rows, 2 * inner + wide_bcd), bf16),
         ],

time: 152 us -> 152 us (level)
  no operation moved by 1% of the time
where the time goes in v3:
time: 152 us
  starting transfers between devices  57.2 us (38%)
  waiting for transfers between devices  44.5 us (29%)
  Pallas kernels  41 us (27%)
  local copies, waits for them, and re-layouts  6.39 us (4%)
    ppermute x51, starting transfers between devices, sent(): return lax.ppermute(block, axis, xor_route(lax.axis_size(axis), k))  51.9 us
    pallas_call x11, Pallas kernels, call(): pl.pallas_call(kernel, out_shape=[jax.ShapeDtypeStruct(shape, kind) for s...  41 us
    ppermute x51, waiting for transfers between devices, sent(): return lax.ppermute(block, axis, xor_route(lax.axis_size(axis), k))  40.5 us
    unnamed x127, local copies, waits for them, and re-layouts  5.56 us
    ppermute x4, starting transfers between devices, passed_along(): return lax.ppermute(block, axis, route)  5.33 us
    ppermute x4, waiting for transfers between devices, passed_along(): return lax.ppermute(block, axis, route)  3.95 us
  transfers between devices with their start and end apart: 55, of which 23 were waited for; matrix products, arithmetic and copies ran while one was open for 2% of the time, Pallas kernels for 15%

profile of v3, /device:TPU:0, one launch (start us, length us, event | category | flops | bytes accessed | tf_op | source)
XLA Modules:
  0.0 151.7 jit_solution(17896679157320276209)
XLA Ops:
  2.2 3.9 %collective-permute-start.13 = (bf16[128,384]{1,0:T(8,128)(2,1)}, bf16[128,384]{1,0:T(8,128)(2,1)S(1)}, u32[]{:S(2)}, u32[]{:S(2)}) collective-permute-start(bf16[128,384]{1,0:T(8,128)(2,1)} %get-tuple-element.81.refs_15_), channel_id=1, source_target_pairs={{0,24},{8,16},{16,8},{24,0},{1,25},{9,17},{17,9},{25,1},{2,26},{10... | collective-permute-start | bytes 294920 | tf_op jit(solution)/shard_map/ppermute | solution.py:24
  9.2 2.0 %collective-permute-done.12.refs_17_ = bf16[128,384]{1,0:T(8,128)(2,1)S(1)} collective-permute-done((bf16[128,384]{1,0:T(8,128)(2,1)}, bf16[128,384]{1,0:T(8,128)(2,1)S(1)}, u32[]{:S(2)}, u32[]{:S(2)}) %collective-permute-start.12) | collective-permute-done | bytes 98336 | tf_op jit(solution)/shard_map/ppermute | solution.py:24
  18.3 3.6 %collective-permute-start.3 = (bf16[272,256]{1,0:T(8,128)(2,1)S(1)}, bf16[272,256]{1,0:T(8,128)(2,1)S(1)}, u32[]{:S(2)}, u32[]{:S(2)}) collective-permute-start(bf16[272,256]{1,0:T(8,128)(2,1)S(1)} %pad_maximum_fusion.refs_3_), channel_id=1, source_target_pairs={{0,3},{1,2},{2,1},{3,0},{4,7},{5,6},{6,5},{7,4},{8,11},{9,10},{10,... | collective-permute-start | bytes 417800 | tf_op jit(solution)/shard_map/ppermute | solution.py:24
  22.0 1.6 %collective-permute-done.6.refs_10_ = bf16[128,1024]{1,0:T(8,128)(2,1)S(1)} collective-permute-done((bf16[128,1024]{1,0:T(8,128)(2,1)S(1)}, bf16[128,1024]{1,0:T(8,128)(2,1)S(1)}, u32[]{:S(2)}, u32[]{:S(2)}) %collective-permute-start.6) | collective-permute-done | bytes 262176 | tf_op jit(solution)/shard_map/ppermute | solution.py:24
  25.2 2.6 %collective-permute-done.5.refs_9_ = bf16[128,1024]{1,0:T(8,128)(2,1)S(1)} collective-permute-done((bf16[128,1024]{1,0:T(8,128)(2,1)S(1)}, bf16[128,1024]{1,0:T(8,128)(2,1)S(1)}, u32[]{:S(2)}, u32[]{:S(2)}) %collective-permute-start.5) | collective-permute-done | bytes 262176 | tf_op jit(solution)/shard_map/ppermute | solution.py:24
  28.6 5.6 %collective-permute-done.2.refs_5_ = bf16[272,256]{1,0:T(8,128)(2,1)S(1)} collective-permute-done((bf16[272,256]{1,0:T(8,128)(2,1)S(1)}, bf16[272,256]{1,0:T(8,128)(2,1)S(1)}, u32[]{:S(2)}, u32[]{:S(2)}) %collective-permute-start.2) | collective-permute-done | bytes 139296 | tf_op jit(solution)/shard_map/ppermute | solution.py:24
  34.1 2.5 %collective-permute-start.21 = (bf16[256,256]{1,0:T(8,128)(2,1)}, bf16[256,256]{1,0:T(8,128)(2,1)S(1)}, u32[]{:S(2)}, u32[]{:S(2)}) collective-permute-start(bf16[256,256]{1,0:T(8,128)(2,1)} %bitcast.18), channel_id=1, source_target_pairs={{0,3},{1,2},{2,1},{3,0},{4,7},{5,6},{6,5},{7,4},{8,11},{9,10},{10,... | collective-permute-start | bytes 393224 | tf_op jit(solution)/shard_map/ppermute | solution.py:24
  36.8 1.9 %collective-permute-start.19 = (bf16[256,256]{1,0:T(8,128)(2,1)}, bf16[256,256]{1,0:T(8,128)(2,1)S(1)}, u32[]{:S(2)}, u32[]{:S(2)}) collective-permute-start(bf16[256,256]{1,0:T(8,128)(2,1)} %bitcast.20), channel_id=1, source_target_pairs={{0,1},{1,0},{2,3},{3,2},{4,5},{5,4},{6,7},{7,6},{8,9},{9,8},{10,11... | collective-permute-start | bytes 393224 | tf_op jit(solution)/shard_map/ppermute | solution.py:24
  41.5 6.2 %shard_map.195 = (bf16[256,512]{1,0:T(8,128)(2,1)}, bf16[272,512]{1,0:T(8,128)(2,1)}, bf16[272,256]{1,0:T(8,128)(2,1)}, f32[256,512]{1,0:T(8,128)}, f32[256,256]...) custom-call(s32[1]{0:T(128)} %bitcast.where, ...), custom_call_target="tpu_custom_call" | custom-call | tf_op jit(solution)/shard_map/pallas_call | solution.py:580
  50.7 2.1 %collective-permute-done.22.refs_12_ = bf16[512,128]{1,0:T(8,128)(2,1)S(1)} collective-permute-done((bf16[512,128]{1,0:T(8,128)(2,1)S(1)}, bf16[512,128]{1,0:T(8,128)(2,1)S(1)}, u32[]{:S(2)}, u32[]{:S(2)}) %collective-permute-start.22) | collective-permute-done | bytes 131104 | tf_op jit(solution)/shard_map/ppermute | solution.py:24
  54.9 4.3 %shard_map.196 = (f32[256,512]{1,0:T(8,128)}, f32[256,512]{1,0:T(8,128)}, f32[8,256]{1,0:T(8,128)}, bf16[1024,256]{1,0:T(8,128)(2,1)}, bf16[1024,256]{1,0:T(8,12...) custom-call(s32[1]{0:T(128)} %bitcast.where, ...), custom_call_target="tpu_custom_call" | custom-call | tf_op jit(solution)/shard_map/pallas_call | solution.py:580
  59.2 2.5 %collective-permute-start.31 = (f32[8,256]{1,0:T(8,128)}, f32[8,256]{1,0:T(8,128)S(1)}, u32[]{:S(2)}, u32[]{:S(2)}) collective-permute-start(f32[8,256]{1,0:T(8,128)} %get-tuple-element.88.refs_0_), channel_id=1, source_target_pairs={{0,3},{1,2},{2,1},{3,0},{4,7},{5,6},{6,5},{7,4},{8,11},{9,10},{10,... | collective-permute-start | bytes 24584 | tf_op jit(solution)/shard_map/ppermute | solution.py:24
  61.7 1.9 %collective-permute-start.29 = (f32[8,256]{1,0:T(8,128)}, f32[8,256]{1,0:T(8,128)S(1)}, u32[]{:S(2)}, u32[]{:S(2)}) collective-permute-start(f32[8,256]{1,0:T(8,128)} %get-tuple-element.88.refs_0_), channel_id=1, source_target_pairs={{0,1},{1,0},{2,3},{3,2},{4,5},{5,4},{6,7},{7,6},{8,9},{9,8},{10,11... | collective-permute-start | bytes 24584 | tf_op jit(solution)/shard_map/ppermute | solution.py:24
  67.1 3.2 %shard_map.197 = (f32[256,512]{1,0:T(8,128)}, bf16[256,512]{1,0:T(8,128)(2,1)}, f32[512,128]{1,0:T(8,128)}, f32[256,128]{1,0:T(8,128)}, f32[1,512]{1,0:T(1,128)}, /*index=5*/bf16[256,512]{1,0:T(8,128)(2,1)}) custom-call(f32[8,256]{1,0:T(8,128)} %get-tuple-element.88.refs_0_, f32[8,256]{1,0:T(8,128)} %copy-done.57, f32[8,256]{1,0:T(8,128)} %copy-done.56, ...), custom_call_target="tpu_custom_call" | custom-call | tf_op jit(solution)/shard_map/pallas_call | solution.py:580
  70.3 5.6 %shard_map.198 = (f32[256,512]{1,0:T(8,128)}, f32[256,256]{1,0:T(8,128)}, f32[256,128]{1,0:T(8,128)}, bf16[512,1024]{1,0:T(8,128)(2,1)}, bf16[512,1024]{1,0:T(8,128)(2,1)}) custom-call(f32[256,512]{1,0:T(8,128)} %get-tuple-element.92.dy_ref, bf16[256,512]{1,0:T(8,128)(2,1)} %get-tuple-element.93.dz.refs_5_, ...), custom_call_target="tpu_custom_call" | custom-call | tf_op jit(solution)/shard_map/pallas_call | solution.py:580
  77.4 1.9 %collective-permute-done.32.next_ref = f32[512,128]{1,0:T(8,128)S(1)} collective-permute-done((f32[512,128]{1,0:T(8,128)S(1)}, f32[512,128]{1,0:T(8,128)S(1)}, u32[]{:S(2)}, u32[]{:S(2)}) %collective-permute-start.32) | collective-permute-done | bytes 262176 | tf_op jit(solution)/shard_map/ppermute | solution.py:46
  80.0 4.3 %shard_map.199 = (f32[256,512]{1,0:T(8,128)}, f32[256,256]{1,0:T(8,128)}, f32[8,768]{1,0:T(8,128)}, bf16[256,128]{1,0:T(8,128)(2,1)}, f32[8,128]{1,0:T(8,128)}) custom-call(f32[512,128]{1,0:T(8,128)} %copy-done.13, f32[256,512]{1,0:T(8,128)} %get-tuple-element.99.dxs, f32[256,256]{1,0:T(8,128)} %get-tuple-element.100.dbc, ...), custom_call_target="tpu_custom_call" | custom-call | tf_op jit(solution)/shard_map/pallas_call | solution.py:580
  85.6 2.0 %collective-permute-done.33.refs_0_ = f32[8,768]{1,0:T(8,128)S(1)} collective-permute-done((f32[8,768]{1,0:T(8,128)}, f32[8,768]{1,0:T(8,128)S(1)}, u32[]{:S(2)}, u32[]{:S(2)}) %collective-permute-start.33) | collective-permute-done | bytes 24608 | tf_op jit(solution)/shard_map/ppermute | solution.py:46
  88.2 6.3 %shard_map.200 = (bf16[272,256]{1,0:T(8,128)(2,1)}, bf16[272,256]{1,0:T(8,128)(2,1)}, bf16[272,256]{1,0:T(8,128)(2,1)}, bf16[272,256]{1,0:T(8,128)(2,1)}, bf16[5...) custom-call(s32[1]{0:T(128)} %bitcast.where, ...), custom_call_target="tpu_custom_call" | custom-call | tf_op jit(solution)/shard_map/pallas_call | solution.py:580
  95.1 2.2 %collective-permute-done.44.other = bf16[560,384]{1,0:T(8,128)(2,1)S(1)} collective-permute-done((bf16[560,384]{1,0:T(8,128)(2,1)}, bf16[560,384]{1,0:T(8,128)(2,1)S(1)}, u32[]{:S(2)}, u32[]{:S(2)}) %collective-permute-start.44) | collective-permute-done | bytes 430112 | tf_op jit(solution)/shard_map/ppermute | solution.py:24
  98.2 2.5 %shard_map.201 = (bf16[176,384]{1,0:T(8,128)(2,1)}, bf16[176,384]{1,0:T(8,128)(2,1)}, bf16[176,384]{1,0:T(8,128)(2,1)}, bf16[176,384]{1,0:T(8,128)(2,1)}, bf16[1...) custom-call(bf16[560,384]{1,0:T(8,128)(2,1)} %get-tuple-element.124.own, ...), custom_call_target="tpu_custom_call" | custom-call | tf_op jit(solution)/shard_map/pallas_call | solution.py:580
  105.2 2.2 %collective-permute-done.49.refs_1_ = bf16[176,384]{1,0:T(8,128)(2,1)S(1)} collective-permute-done((bf16[176,384]{1,0:T(8,128)(2,1)}, bf16[176,384]{1,0:T(8,128)(2,1)S(1)}, u32[]{:S(2)}, u32[]{:S(2)}) %collective-permute-start.49) | collective-permute-done | bytes 135200 | tf_op jit(solution)/shard_map/ppermute | solution.py:24
  107.4 2.0 %collective-permute-start.38 = (bf16[256,256]{1,0:T(8,128)(2,1)}, bf16[256,256]{1,0:T(8,128)(2,1)S(1)}, u32[]{:S(2)}, u32[]{:S(2)}) collective-permute-start(bf16[256,256]{1,0:T(8,128)(2,1)} %get-tuple-element.120), channel_id=1, source_target_pairs={{0,2},{1,3},{2,0},{3,1},{4,6},{5,7},{6,4},{7,5},{8,10},{9,11},{10,... | collective-permute-start | bytes 393224 | tf_op jit(solution)/shard_map/ppermute | solution.py:24
  112.7 1.9 %shard_map.203 = (f32[8,128]{1,0:T(8,128)}, f32[5,512]{1,0:T(8,128)}, f32[3,8]{1,0:T(4,128)}, f32[1,512]{1,0:T(1,128)}, bf16[144,256]{1,0:T(8,128)(2,1)}) custom-call(bf16[176,384]{1,0:T(8,128)(2,1)} %get-tuple-element.135.refs_0_, bf16[176,384]{1,0:T(8,128)(2,1)} %copy-done.23, bf16[176,384]{1,0:T(8,128)(2,1)} %copy-done.24, bf16[176,384]{1,0:T(8,128)(2,1)} %copy-done.25), custom_call_target="tpu_custom_call" | custom-call | tf_op jit(solution)/shard_map/pallas_call | solution.py:580
  114.6 1.9 %collective-permute-start.35 = (bf16[272,256]{1,0:T(8,128)(2,1)S(1)}, bf16[272,256]{1,0:T(8,128)(2,1)S(1)}, u32[]{:S(2)}, u32[]{:S(2)}) collective-permute-start(bf16[272,256]{1,0:T(8,128)(2,1)S(1)} %copy-done.60), channel_id=1, source_target_pairs={{0,2},{1,3},{2,0},{3,1},{4,6},{5,7},{6,4},{7,5},{8,10},{9,11},{10,... | collective-permute-start | bytes 417800 | tf_op jit(solution)/shard_map/ppermute | solution.py:24
  118.5 2.5 %collective-permute-done.38.refs_6_ = bf16[256,256]{1,0:T(8,128)(2,1)S(1)} collective-permute-done((bf16[256,256]{1,0:T(8,128)(2,1)}, bf16[256,256]{1,0:T(8,128)(2,1)S(1)}, u32[]{:S(2)}, u32[]{:S(2)}) %collective-permute-start.38) | collective-permute-done | bytes 131104 | tf_op jit(solution)/shard_map/ppermute | solution.py:24
  121.8 2.5 %collective-permute-start.54 = (bf16[144,256]{1,0:T(8,128)(2,1)S(1)}, bf16[144,256]{1,0:T(8,128)(2,1)S(1)}, u32[]{:S(2)}, u32[]{:S(2)}) collective-permute-start(bf16[144,256]{1,0:T(8,128)(2,1)S(1)} %copy-done.50), channel_id=1, source_target_pairs={{0,3},{1,2},{2,1},{3,0},{4,7},{5,6},{6,5},{7,4},{8,11},{9,10},{10,... | collective-permute-start | bytes 221192 | tf_op jit(solution)/shard_map/ppermute | solution.py:24
  126.3 6.4 %collective-permute-done.35.refs_2_ = bf16[272,256]{1,0:T(8,128)(2,1)S(1)} collective-permute-done((bf16[272,256]{1,0:T(8,128)(2,1)S(1)}, bf16[272,256]{1,0:T(8,128)(2,1)S(1)}, u32[]{:S(2)}, u32[]{:S(2)}) %collective-permute-start.35) | collective-permute-done | bytes 139296 | tf_op jit(solution)/shard_map/ppermute | solution.py:24
  137.4 3.0 %collective-permute-done.53.refs_2_ = bf16[144,256]{1,0:T(8,128)(2,1)S(1)} collective-permute-done((bf16[144,256]{1,0:T(8,128)(2,1)S(1)}, bf16[144,256]{1,0:T(8,128)(2,1)S(1)}, u32[]{:S(2)}, u32[]{:S(2)}) %collective-permute-start.53) | collective-permute-done | bytes 73760 | tf_op jit(solution)/shard_map/ppermute | solution.py:24
  142.5 1.7 %shard_map.204 = (f32[128,256]{1,0:T(8,128)}, f32[5,256]{1,0:T(8,128)}, f32[1,128]{1,0:T(1,128)}) custom-call(bf16[144,256]{1,0:T(8,128)(2,1)} %get-tuple-element.139.refs_0_, bf16[144,256]{1,0:T(8,128)(2,1)} %copy-done.53, bf16[144,256]{1,0:T(8,128)(2,1)} %copy-done.52, bf16[144,256]{1,0:T(8,128)(2,1)} %copy-done.51), custom_call_target="tpu_custom_call" | custom-call | tf_op jit(solution)/shard_map/pallas_call | solution.py:580
  145.6 1.7 %collective-permute-done.48.refs_15_ = bf16[128,512]{1,0:T(8,128)(2,1)S(1)} collective-permute-done((bf16[128,512]{1,0:T(8,128)(2,1)}, bf16[128,512]{1,0:T(8,128)(2,1)S(1)}, u32[]{:S(2)}, u32[]{:S(2)}) %collective-permute-start.48) | collective-permute-done | bytes 131104 | tf_op jit(solution)/shard_map/ppermute | solution.py:24
  148.2 3.5 %shard_map.202 = (bf16[256,256]{1,0:T(8,128)(2,1)}, bf16[256,256]{1,0:T(8,128)(2,1)}, f32[128,2,512]{2,1,0:T(2,128)}, f32[512,128]{1,0:T(8,128)}) custom-call(s32[1]{0:T(128)} %bitcast.where, bf16[272,256]{1,0:T(8,128)(2,1)} %get-tuple-element.114.refs_0_, bf16[272,256]{1,0:T(8,128)(2,1)} %copy-done.20, bf16[272,256]{1,0:T(8,128)(2,1)} %copy-done.21, ...), custom_call_target="tpu_custom_call" | custom-call | tf_op jit(solution)/shard_map/pallas_call | solution.py:580
  (220 shorter events, 52.3 us)
Async XLA Ops:
  2.2 7.0 %collective-permute-start.13 = (bf16[128,384]{1,0:T(8,128)(2,1)}, bf16[128,384]{1,0:T(8,128)(2,1)S(1)}, u32[]{:S(2)}, u32[]{:S(2)}) collective-permute-start(bf16[128,384]{1,0:T(8,128)(2,1)} %get-tuple-element.81.refs_15_), channel_id=1, source_target_pairs={{0,24},{8,16},{16,8},{24,0},{1,25},{9,17},{17,9},{25,1},{2,26},{10... | collective-permute-start | bytes 294920 | tf_op jit(solution)/shard_map/ppermute | solution.py:24
  6.7 8.3 %collective-permute-start = (bf16[256,256]{1,0:T(8,128)(2,1)}, bf16[256,256]{1,0:T(8,128)(2,1)S(1)}, u32[]{:S(2)}, u32[]{:S(2)}) collective-permute-start(bf16[256,256]{1,0:T(8,128)(2,1)} %bitcast.23), channel_id=1, source_target_pairs={{0,4},{1,5},{2,6},{3,7},{8,12},{9,13},{10,14},{11,15},{16,20},{17,... | collective-permute-start | bytes 393224 | tf_op jit(solution)/shard_map/ppermute | solution.py:46
  9.2 6.8 %collective-permute-start.17 = (bf16[128,384]{1,0:T(8,128)(2,1)S(1)}, bf16[128,384]{1,0:T(8,128)(2,1)S(1)}, u32[]{:S(2)}, u32[]{:S(2)}) collective-permute-start(bf16[128,384]{1,0:T(8,128)(2,1)S(1)} %collective-permute-done.13.refs_18_), channel_id=1, source_target_pairs={{0,4},{4,0},{1,5},{5,1},{2,6},{6,2},{3,7},{7,3},{8,12},{12,8},{9,1... | collective-permute-start | bytes 294920 | tf_op jit(solution)/shard_map/ppermute | solution.py:24
  12.4 9.6 %collective-permute-start.7 = (bf16[128,1024]{1,0:T(8,128)(2,1)S(1)}, bf16[128,1024]{1,0:T(8,128)(2,1)S(1)}, u32[]{:S(2)}, u32[]{:S(2)}) collective-permute-start(bf16[128,1024]{1,0:T(8,128)(2,1)S(1)} %bitcast.13), channel_id=1, source_target_pairs={{0,4},{4,0},{1,5},{5,1},{2,6},{6,2},{3,7},{7,3},{8,12},{12,8},{9,1... | collective-permute-start | bytes 786440 | tf_op jit(solution)/shard_map/ppermute | solution.py:24
  13.5 10.1 %collective-permute-start.6 = (bf16[128,1024]{1,0:T(8,128)(2,1)S(1)}, bf16[128,1024]{1,0:T(8,128)(2,1)S(1)}, u32[]{:S(2)}, u32[]{:S(2)}) collective-permute-start(bf16[128,1024]{1,0:T(8,128)(2,1)S(1)} %bitcast.14), channel_id=1, source_target_pairs={{0,24},{8,16},{16,8},{24,0},{1,25},{9,17},{17,9},{25,1},{2,26},{10... | collective-permute-start | bytes 786440 | tf_op jit(solution)/shard_map/ppermute | solution.py:24
  15.0 12.8 %collective-permute-start.5 = (bf16[128,1024]{1,0:T(8,128)(2,1)S(1)}, bf16[128,1024]{1,0:T(8,128)(2,1)S(1)}, u32[]{:S(2)}, u32[]{:S(2)}) collective-permute-start(bf16[128,1024]{1,0:T(8,128)(2,1)S(1)} %bitcast.15), channel_id=1, source_target_pairs={{0,16},{8,24},{16,0},{24,8},{1,17},{9,25},{17,1},{25,9},{2,18},{10... | collective-permute-start | bytes 786440 | tf_op jit(solution)/shard_map/ppermute | solution.py:24
  16.1 12.0 %collective-permute-start.4 = (bf16[128,1024]{1,0:T(8,128)(2,1)S(1)}, bf16[128,1024]{1,0:T(8,128)(2,1)S(1)}, u32[]{:S(2)}, u32[]{:S(2)}) collective-permute-start(bf16[128,1024]{1,0:T(8,128)(2,1)S(1)} %bitcast.16), channel_id=1, source_target_pairs={{0,8},{8,0},{16,24},{24,16},{1,9},{9,1},{17,25},{25,17},{2,10},{10... | collective-permute-start | bytes 786440 | tf_op jit(solution)/shard_map/ppermute | solution.py:24
  18.3 9.9 %collective-permute-start.3 = (bf16[272,256]{1,0:T(8,128)(2,1)S(1)}, bf16[272,256]{1,0:T(8,128)(2,1)S(1)}, u32[]{:S(2)}, u32[]{:S(2)}) collective-permute-start(bf16[272,256]{1,0:T(8,128)(2,1)S(1)} %pad_maximum_fusion.refs_3_), channel_id=1, source_target_pairs={{0,3},{1,2},{2,1},{3,0},{4,7},{5,6},{6,5},{7,4},{8,11},{9,10},{10,... | collective-permute-start | bytes 417800 | tf_op jit(solution)/shard_map/ppermute | solution.py:24
  22.0 12.2 %collective-permute-start.2 = (bf16[272,256]{1,0:T(8,128)(2,1)S(1)}, bf16[272,256]{1,0:T(8,128)(2,1)S(1)}, u32[]{:S(2)}, u32[]{:S(2)}) collective-permute-start(bf16[272,256]{1,0:T(8,128)(2,1)S(1)} %pad_maximum_fusion.refs_3_), channel_id=1, source_target_pairs={{0,2},{1,3},{2,0},{3,1},{4,6},{5,7},{6,4},{7,5},{8,10},{9,11},{10,... | collective-permute-start | bytes 417800 | tf_op jit(solution)/shard_map/ppermute | solution.py:24
  23.6 13.1 %collective-permute-start.1 = (bf16[272,256]{1,0:T(8,128)(2,1)S(1)}, bf16[272,256]{1,0:T(8,128)(2,1)S(1)}, u32[]{:S(2)}, u32[]{:S(2)}) collective-permute-start(bf16[272,256]{1,0:T(8,128)(2,1)S(1)} %pad_maximum_fusion.refs_3_), channel_id=1, source_target_pairs={{0,1},{1,0},{2,3},{3,2},{4,5},{5,4},{6,7},{7,6},{8,9},{9,8},{10,11... | collective-permute-start | bytes 417800 | tf_op jit(solution)/shard_map/ppermute | solution.py:24
  27.8 9.0 %collective-permute-start.10 = (bf16[128,1024]{1,0:T(8,128)(2,1)S(1)}, bf16[128,1024]{1,0:T(8,128)(2,1)S(1)}, u32[]{:S(2)}, u32[]{:S(2)}) collective-permute-start(bf16[128,1024]{1,0:T(8,128)(2,1)S(1)} %collective-permute-done.6.refs_10_), channel_id=1, source_target_pairs={{0,4},{4,0},{1,5},{5,1},{2,6},{6,2},{3,7},{7,3},{8,12},{12,8},{9,1... | collective-permute-start | bytes 786440 | tf_op jit(solution)/shard_map/ppermute | solution.py:24
  28.0 10.7 %collective-permute-start.9 = (bf16[128,1024]{1,0:T(8,128)(2,1)S(1)}, bf16[128,1024]{1,0:T(8,128)(2,1)S(1)}, u32[]{:S(2)}, u32[]{:S(2)}) collective-permute-start(bf16[128,1024]{1,0:T(8,128)(2,1)S(1)} %collective-permute-done.5.refs_9_), channel_id=1, source_target_pairs={{0,4},{4,0},{1,5},{5,1},{2,6},{6,2},{3,7},{7,3},{8,12},{12,8},{9,1... | collective-permute-start | bytes 786440 | tf_op jit(solution)/shard_map/ppermute | solution.py:24
  28.3 12.0 %collective-permute-start.8 = (bf16[128,1024]{1,0:T(8,128)(2,1)S(1)}, bf16[128,1024]{1,0:T(8,128)(2,1)S(1)}, u32[]{:S(2)}, u32[]{:S(2)}) collective-permute-start(bf16[128,1024]{1,0:T(8,128)(2,1)S(1)} %collective-permute-done.4.refs_8_), channel_id=1, source_target_pairs={{0,4},{4,0},{1,5},{5,1},{2,6},{6,2},{3,7},{7,3},{8,12},{12,8},{9,1... | collective-permute-start | bytes 786440 | tf_op jit(solution)/shard_map/ppermute | solution.py:24
  34.1 13.6 %collective-permute-start.21 = (bf16[256,256]{1,0:T(8,128)(2,1)}, bf16[256,256]{1,0:T(8,128)(2,1)S(1)}, u32[]{:S(2)}, u32[]{:S(2)}) collective-permute-start(bf16[256,256]{1,0:T(8,128)(2,1)} %bitcast.18), channel_id=1, source_target_pairs={{0,3},{1,2},{2,1},{3,0},{4,7},{5,6},{6,5},{7,4},{8,11},{9,10},{10,... | collective-permute-start | bytes 393224 | tf_op jit(solution)/shard_map/ppermute | solution.py:24
  36.7 12.1 %collective-permute-start.20 = (bf16[256,256]{1,0:T(8,128)(2,1)}, bf16[256,256]{1,0:T(8,128)(2,1)S(1)}, u32[]{:S(2)}, u32[]{:S(2)}) collective-permute-start(bf16[256,256]{1,0:T(8,128)(2,1)} %bitcast.19), channel_id=1, source_target_pairs={{0,2},{1,3},{2,0},{3,1},{4,6},{5,7},{6,4},{7,5},{8,10},{9,11},{10,... | collective-permute-start | bytes 393224 | tf_op jit(solution)/shard_map/ppermute | solution.py:24
  36.8 13.3 %collective-permute-start.19 = (bf16[256,256]{1,0:T(8,128)(2,1)}, bf16[256,256]{1,0:T(8,128)(2,1)S(1)}, u32[]{:S(2)}, u32[]{:S(2)}) collective-permute-start(bf16[256,256]{1,0:T(8,128)(2,1)} %bitcast.20), channel_id=1, source_target_pairs={{0,1},{1,0},{2,3},{3,2},{4,5},{5,4},{6,7},{7,6},{8,9},{9,8},{10,11... | collective-permute-start | bytes 393224 | tf_op jit(solution)/shard_map/ppermute | solution.py:24
  38.7 11.4 %collective-permute-start.24 = (bf16[512,128]{1,0:T(8,128)(2,1)}, bf16[512,128]{1,0:T(8,128)(2,1)S(1)}, u32[]{:S(2)}, u32[]{:S(2)}) collective-permute-start(bf16[512,128]{1,0:T(8,128)(2,1)} %refs_11_.2), channel_id=1, source_target_pairs={{0,24},{8,16},{16,8},{24,0},{1,25},{9,17},{17,9},{25,1},{2,26},{10... | collective-permute-start | bytes 393224 | tf_op jit(solution)/shard_map/ppermute | solution.py:24
  40.3 10.4 %collective-permute-start.23 = (bf16[512,128]{1,0:T(8,128)(2,1)}, bf16[512,128]{1,0:T(8,128)(2,1)S(1)}, u32[]{:S(2)}, u32[]{:S(2)}) collective-permute-start(bf16[512,128]{1,0:T(8,128)(2,1)} %refs_11_.2), channel_id=1, source_target_pairs={{0,16},{8,24},{16,0},{24,8},{1,17},{9,25},{17,1},{25,9},{2,18},{10... | collective-permute-start | bytes 393224 | tf_op jit(solution)/shard_map/ppermute | solution.py:24
  75.9 38.7 %collective-permute-start.40 = (bf16[512,1024]{1,0:T(8,128)(2,1)}, bf16[512,1024]{1,0:T(8,128)(2,1)S(1)}, u32[]{:S(2)}, u32[]{:S(2)}) collective-permute-start(bf16[512,1024]{1,0:T(8,128)(2,1)} %get-tuple-element.123), channel_id=1, source_target_pairs={{0,4},{4,0},{1,5},{5,1},{2,6},{6,2},{3,7},{7,3},{8,12},{12,8},{9,1... | collective-permute-start | bytes 3145736 | tf_op jit(solution)/shard_map/ppermute | solution.py:24
  101.6 8.5 %collective-permute-start.50 = (bf16[176,384]{1,0:T(8,128)(2,1)}, bf16[176,384]{1,0:T(8,128)(2,1)S(1)}, u32[]{:S(2)}, u32[]{:S(2)}) collective-permute-start(bf16[176,384]{1,0:T(8,128)(2,1)} %get-tuple-element.137), channel_id=1, source_target_pairs={{0,16},{8,24},{16,0},{24,8},{1,17},{9,25},{17,1},{25,9},{2,18},{10... | collective-permute-start | bytes 405512 | tf_op jit(solution)/shard_map/ppermute | solution.py:24
  103.1 8.5 %collective-permute-start.51 = (bf16[176,384]{1,0:T(8,128)(2,1)}, bf16[176,384]{1,0:T(8,128)(2,1)S(1)}, u32[]{:S(2)}, u32[]{:S(2)}) collective-permute-start(bf16[176,384]{1,0:T(8,128)(2,1)} %get-tuple-element.138), channel_id=1, source_target_pairs={{0,24},{8,16},{16,8},{24,0},{1,25},{9,17},{17,9},{25,1},{2,26},{10... | collective-permute-start | bytes 405512 | tf_op jit(solution)/shard_map/ppermute | solution.py:24
  104.2 12.7 %collective-permute-start.37 = (bf16[256,256]{1,0:T(8,128)(2,1)}, bf16[256,256]{1,0:T(8,128)(2,1)S(1)}, u32[]{:S(2)}, u32[]{:S(2)}) collective-permute-start(bf16[256,256]{1,0:T(8,128)(2,1)} %get-tuple-element.119), channel_id=1, source_target_pairs={{0,1},{1,0},{2,3},{3,2},{4,5},{5,4},{6,7},{7,6},{8,9},{9,8},{10,11... | collective-permute-start | bytes 393224 | tf_op jit(solution)/shard_map/ppermute | solution.py:24
  107.4 13.6 %collective-permute-start.38 = (bf16[256,256]{1,0:T(8,128)(2,1)}, bf16[256,256]{1,0:T(8,128)(2,1)S(1)}, u32[]{:S(2)}, u32[]{:S(2)}) collective-permute-start(bf16[256,256]{1,0:T(8,128)(2,1)} %get-tuple-element.120), channel_id=1, source_target_pairs={{0,2},{1,3},{2,0},{3,1},{4,6},{5,7},{6,4},{7,5},{8,10},{9,11},{10,... | collective-permute-start | bytes 393224 | tf_op jit(solution)/shard_map/ppermute | solution.py:24
  110.1 11.7 %collective-permute-start.39 = (bf16[256,256]{1,0:T(8,128)(2,1)S(1)}, bf16[256,256]{1,0:T(8,128)(2,1)S(1)}, u32[]{:S(2)}, u32[]{:S(2)}) collective-permute-start(bf16[256,256]{1,0:T(8,128)(2,1)S(1)} %copy-done.61), channel_id=1, source_target_pairs={{0,3},{1,2},{2,1},{3,0},{4,7},{5,6},{6,5},{7,4},{8,11},{9,10},{10,... | collective-permute-start | bytes 393224 | tf_op jit(solution)/shard_map/ppermute | solution.py:24
  111.6 13.5 %collective-permute-start.34 = (bf16[272,256]{1,0:T(8,128)(2,1)}, bf16[272,256]{1,0:T(8,128)(2,1)S(1)}, u32[]{:S(2)}, u32[]{:S(2)}) collective-permute-start(bf16[272,256]{1,0:T(8,128)(2,1)} %get-tuple-element.115), channel_id=1, source_target_pairs={{0,1},{1,0},{2,3},{3,2},{4,5},{5,4},{6,7},{7,6},{8,9},{9,8},{10,11... | collective-permute-start | bytes 417800 | tf_op jit(solution)/shard_map/ppermute | solution.py:24
  114.6 18.1 %collective-permute-start.35 = (bf16[272,256]{1,0:T(8,128)(2,1)S(1)}, bf16[272,256]{1,0:T(8,128)(2,1)S(1)}, u32[]{:S(2)}, u32[]{:S(2)}) collective-permute-start(bf16[272,256]{1,0:T(8,128)(2,1)S(1)} %copy-done.60), channel_id=1, source_target_pairs={{0,2},{1,3},{2,0},{3,1},{4,6},{5,7},{6,4},{7,5},{8,10},{9,11},{10,... | collective-permute-start | bytes 417800 | tf_op jit(solution)/shard_map/ppermute | solution.py:24
  116.9 16.7 %collective-permute-start.36 = (bf16[272,256]{1,0:T(8,128)(2,1)S(1)}, bf16[272,256]{1,0:T(8,128)(2,1)S(1)}, u32[]{:S(2)}, u32[]{:S(2)}) collective-permute-start(bf16[272,256]{1,0:T(8,128)(2,1)S(1)} %copy-done.59), channel_id=1, source_target_pairs={{0,3},{1,2},{2,1},{3,0},{4,7},{5,6},{6,5},{7,4},{8,11},{9,10},{10,... | collective-permute-start | bytes 417800 | tf_op jit(solution)/shard_map/ppermute | solution.py:24
  121.0 14.1 %collective-permute-start.46 = (bf16[128,512]{1,0:T(8,128)(2,1)S(1)}, bf16[128,512]{1,0:T(8,128)(2,1)S(1)}, u32[]{:S(2)}, u32[]{:S(2)}) collective-permute-start(bf16[128,512]{1,0:T(8,128)(2,1)S(1)} %copy-done.62), channel_id=1, source_target_pairs={{0,8},{8,0},{16,24},{24,16},{1,9},{9,1},{17,25},{25,17},{2,10},{10... | collective-permute-start | bytes 393224 | tf_op jit(solution)/shard_map/ppermute | solution.py:24
  121.8 14.8 %collective-permute-start.54 = (bf16[144,256]{1,0:T(8,128)(2,1)S(1)}, bf16[144,256]{1,0:T(8,128)(2,1)S(1)}, u32[]{:S(2)}, u32[]{:S(2)}) collective-permute-start(bf16[144,256]{1,0:T(8,128)(2,1)S(1)} %copy-done.50), channel_id=1, source_target_pairs={{0,3},{1,2},{2,1},{3,0},{4,7},{5,6},{6,5},{7,4},{8,11},{9,10},{10,... | collective-permute-start | bytes 221192 | tf_op jit(solution)/shard_map/ppermute | solution.py:24
  125.1 22.2 %collective-permute-start.43 = (bf16[128,1024]{1,0:T(8,128)(2,1)S(1)}, bf16[128,1024]{1,0:T(8,128)(2,1)S(1)}, u32[]{:S(2)}, u32[]{:S(2)}) collective-permute-start(bf16[128,1024]{1,0:T(8,128)(2,1)S(1)} %get-tuple-element.149), channel_id=1, source_target_pairs={{0,24},{8,16},{16,8},{24,0},{1,25},{9,17},{17,9},{25,1},{2,26},{10... | collective-permute-start | bytes 786440 | tf_op jit(solution)/shard_map/ppermute | solution.py:24
  132.7 14.6 %collective-permute-start.42 = (bf16[128,1024]{1,0:T(8,128)(2,1)S(1)}, bf16[128,1024]{1,0:T(8,128)(2,1)S(1)}, u32[]{:S(2)}, u32[]{:S(2)}) collective-permute-start(bf16[128,1024]{1,0:T(8,128)(2,1)S(1)} %get-tuple-element.150), channel_id=1, source_target_pairs={{0,16},{8,24},{16,0},{24,8},{1,17},{9,25},{17,1},{25,9},{2,18},{10... | collective-permute-start | bytes 786440 | tf_op jit(solution)/shard_map/ppermute | solution.py:24
  133.6 13.7 %collective-permute-start.41 = (bf16[128,1024]{1,0:T(8,128)(2,1)S(1)}, bf16[128,1024]{1,0:T(8,128)(2,1)S(1)}, u32[]{:S(2)}, u32[]{:S(2)}) collective-permute-start(bf16[128,1024]{1,0:T(8,128)(2,1)S(1)} %get-tuple-element.151), channel_id=1, source_target_pairs={{0,8},{8,0},{16,24},{24,16},{1,9},{9,1},{17,25},{25,17},{2,10},{10... | collective-permute-start | bytes 786440 | tf_op jit(solution)/shard_map/ppermute | solution.py:24
  (86 other events, 728.6 us)
